TPU v7x, 32 devices: a whole 2x2x4 slice. The times are simulated.
32 devices in a mesh: parts: 2 (over x), scene: 4 (over y, core), range: 4 (over z).
Axes of the slice: x: 2, y: 2, z: 4, core: 2. Of those that a mesh axis runs over, the one named last changes fastest.
Arguments:
- secondary: bfloat16 [16, 1056, 2, 1024], P(('parts', 'scene'), None, None, 'range'), parts along dimension 0, may hold values from -6 to 6
- reference_store: bfloat16 [8, 4, 256, 2, 1024], P(('parts', 'scene'), None, None, None, 'range'), parts along dimension 0, may hold values from -6 to 6
- tile_owner: int32 [8], P('parts'), parts along dimension 0, may hold values from 0 to 3
- az_kernel: float32 [64, 8], replicated, may hold values from -2 to 2
- rg_kernel: float32 [64, 8], replicated, may hold values from -2 to 2
- az_offset: int32 [16, 1024], P(('parts', 'scene')), parts along dimension 0, may hold values from -12 to 12
- az_index: int32 [16, 1024], P(('parts', 'scene')), parts along dimension 0, may hold values from 0 to 63
- rg_offset: int32 [16, 1024], P(('parts', 'scene'), 'range'), parts along dimension 0, may hold values from -12 to 12
- rg_index: int32 [16, 1024], P(('parts', 'scene'), 'range'), parts along dimension 0, may hold values from 0 to 63
Outputs:
- reference_pairs: float32 [16, 2, 256, 64], P(('parts', 'scene'), None, None, 'range'), parts along dimension 0
- sequential_pairs: float32 [16, 2, 256, 64], P(('parts', 'scene'), None, None, 'range'), parts along dimension 0
- coherence: float32 [16, 256, 64], P(('parts', 'scene'), None, 'range'), parts along dimension 0
There are 2 independent parts, one for each index of `parts`. A program takes and returns all parts, laid end to end along the dimension named above; an argument that names none is the same for every part. Nothing has to cross between parts.
Inputs may be any that keep to these rules, and one draw needn't show every extreme that they name: `tile_owner`: the scene device holding reference tile s.
All inputs are finite; a program needn't handle non-finite values.
Results may differ from a plain program's by a relative error of at most 0.008.
Values may be sent and summed in bfloat16 or wider, within the bound.
No kernel may reach another device: no remote copies, remote signals or barrier semaphores. Data moves between devices by JAX's collectives and lax.ppermute only.
A program may use at most 128 MiB of HBM per device.

v0:
```python
from functools import partial

import jax
import jax.numpy as jnp
from jax import lax
from jax.experimental import pallas as pl
from jax.experimental.pallas import tpu as pltpu
from jax.sharding import PartitionSpec as P


TILE = 256
LOOK_AZ = 4
LOOK_RG = 16

eps_power = 1e-06

BF = jnp.bfloat16
F32 = jnp.float32
ACROSS = (((1,), (0,)), ((), ()))
OVER_ROWS = (((0,), (0,)), ((), ()))
OVER_LANES = (((1,), (1,)), ((), ()))
VMEM = pl.BlockSpec(memory_space=pltpu.VMEM)
SMEM = pl.BlockSpec(memory_space=pltpu.SMEM)
SMALL = pltpu.CompilerParams(vmem_limit_bytes=12 << 20)


def iota(shape, dim):
    return lax.broadcasted_iota(jnp.int32, shape, dim)


def over(value, size):
    return value >> (size.bit_length() - 1)


def dot(a, b, dims=ACROSS):
    return lax.dot_general(a, b, dims, preferred_element_type=F32)


def lane_row(lane, half_rows):
    blocks = half_rows // LOOK_AZ
    inner = lane & (half_rows - 1)
    return LOOK_AZ * (inner & (blocks - 1)) + over(inner, blocks), over(lane, half_rows) & 1


def look_column(place, columns):
    blocks = columns // LOOK_RG
    return LOOK_RG * (place & (blocks - 1)) + over(place, blocks)


def chosen(shape, dim, wanted):
    return (iota(shape, dim) == wanted).astype(F32).astype(BF)


def taps_and_offsets(kernel_t, index_row, offset_row, spread):
    count = kernel_t.shape[1]
    taps = dot(kernel_t.astype(BF), chosen((count, index_row.shape[1]), 0, index_row))
    offsets = jnp.broadcast_to(offset_row.astype(F32), (8, offset_row.shape[1]))
    return dot(jnp.concatenate([taps, offsets], 0).astype(BF), spread)


def resident(*arrays):
    return [pltpu.with_memory_space_constraint(a, pltpu.VMEM) for a in arrays]


def load_kernel(margin, x_ref, *refs):
    count = (len(refs) - 4) // 2
    small_refs, x_out, outs = refs[:count], refs[count], refs[count + 1 : 2 * count + 1]
    head_ref, tail_ref, sems = refs[2 * count + 1 :]
    depth, rows, parts, columns = x_ref.shape
    pieces = [(k, n) for k in range(depth) for n in range(rows // TILE)]

    def copy_of(position):
        k, n = pieces[position]
        size = TILE if n + 1 < rows // TILE else rows - n * TILE
        part = (k, pl.ds(n * TILE, size))
        return pltpu.make_async_copy(x_ref.at[part], x_out.at[part], sems.at[position]), part, size

    copies = [copy_of(position) for position in range(len(pieces))]
    small = [
        pltpu.make_async_copy(source, target, sems.at[len(pieces) + n])
        for n, (source, target) in enumerate(zip(small_refs, outs))
    ]
    for copy, _, _ in copies:
        copy.start()
    for copy in small:
        copy.start()
    place = iota((2 * margin, 1), 0)
    edges = chosen((2 * margin, columns), 1, jnp.where(place < margin, place, place + columns - 2 * margin))
    for (k, n), (copy, part, size) in zip(pieces, copies):
        copy.wait()
        found = dot(edges, x_out[part].reshape(parts * size, columns), OVER_LANES).astype(BF)
        lanes = slice(parts * n * TILE, parts * (n * TILE + size))
        head_ref[k, :, lanes] = found[:margin]
        tail_ref[k, :, lanes] = found[margin:]
    for copy in small:
        copy.wait()


def load(secondary, *small):
    depth, rows, parts, _ = secondary.shape
    margin = (rows - small[-1].shape[1]) // 2
    operands = (secondary, *small)
    edge = pltpu.VMEM((depth, margin, parts * rows), BF)
    anywhere = pl.BlockSpec(memory_space=pl.ANY)
    outs = pl.pallas_call(
        partial(load_kernel, margin),
        in_specs=[anywhere] * len(operands),
        out_specs=[VMEM] * (len(operands) + 2),
        out_shape=[pltpu.VMEM(a.shape, a.dtype) for a in operands] + [edge, edge],
        scratch_shapes=[pltpu.SemaphoreType.DMA((depth * (rows // TILE) + len(small),))],
        compiler_params=SMALL,
        name="load",
    )(*[pltpu.with_memory_space_constraint(a, pltpu.HBM) for a in operands])
    return outs[:-2], outs[-2], outs[-1]


def range_matrix(margin, kernel_ref, index_row, offset_row, order, column, rg_ref):
    taps = kernel_ref.shape[0]
    both = taps_and_offsets(kernel_ref[...], index_row, offset_row, order)
    base = column + both[taps : taps + 1].astype(jnp.int32) + (margin - 3)
    period = 2 * taps
    place = iota((period, order.shape[1]), 0) - base
    value = tap_pattern(both, place & (taps - 1))
    for block in range(rg_ref.shape[0] // period):
        home = over(place + block * period, taps)
        rg_ref[block * period : (block + 1) * period] = jnp.where(home == 0, value, 0.0).astype(BF)


def tap_pattern(both, which):
    value = jnp.zeros(which.shape, F32)
    for tap in range(both.shape[0] - 8):
        value = jnp.where(which == tap, both[tap : tap + 1], value)
    return value


def resample_kernel(
    margin, x_ref, azk_ref, rgk_ref, rgo_ref, rgi_ref, azi_ref, azo_ref, left_ref, right_ref,
    *refs,
):
    depth, _, _, columns = x_ref.shape
    outs, (spread_ref, band_ref, rg_ref) = refs[:-3], refs[-3:]
    taps = azk_ref.shape[0]
    tile, lanes = spread_ref.shape
    half_rows, half_lanes = tile // 2, lanes // 2
    period = 2 * taps
    lane = iota((1, lanes), 1)
    row, part = lane_row(lane, half_rows)
    spread_ref[...] = chosen((tile, lanes), 0, row + half_rows * over(lane, half_lanes))
    column = look_column(iota((1, columns), 1), columns)
    order = chosen((columns, columns), 0, column)
    for k in range(depth):
        range_matrix(
            margin, rgk_ref, rgi_ref[k : k + 1], rgo_ref[k : k + 1], order, column, rg_ref.at[k]
        )
    for n in range(len(outs) // (depth + 2)):
        *cur_refs, seq_ref, pow_ref = outs[n * (depth + 2) : (n + 1) * (depth + 2)]
        before = None
        for k in range(depth):
            now = []
            for s in range(2):
                start = (2 * n + s) * tile
                rows = slice(start, start + tile)
                both = taps_and_offsets(
                    azk_ref[...], azi_ref[k : k + 1, rows], azo_ref[k : k + 1, rows], spread_ref[...]
                )
                base = row + both[taps : taps + 1].astype(jnp.int32) + (margin - 3)
                sub = iota((period, lanes), 0)
                place = (sub >> 1) - base
                value = tap_pattern(both, jnp.where((sub & 1) == part, place & (taps - 1), taps))
                home = -over(place, taps)
                for half in range(2):
                    mine = slice(half * half_lanes, (half + 1) * half_lanes)
                    band = band_ref.at[k % 2, s, half]
                    for block in range(band.shape[0] // period):
                        band[block * period : (block + 1) * period] = jnp.where(
                            home[:, mine] == block, value[:, mine], 0.0
                        ).astype(BF)
                    first = start + half * half_rows
                    size = half_rows + 2 * margin
                    window = x_ref[k, first : first + size].reshape(2 * size, columns)
                    across = slice(2 * first, 2 * (first + size))
                    wide = jnp.concatenate(
                        [
                            dot(left_ref[k, :, across], band[...]).astype(BF),
                            dot(window, band[...], OVER_ROWS).astype(BF),
                            dot(right_ref[k, :, across], band[...]).astype(BF),
                        ],
                        0,
                    )
                    out = dot(rg_ref[k], wide, OVER_ROWS).astype(BF)
                    cur_refs[k][s, half] = out
                    now.append(out)
            pow_ref[k] = joined([power(halves(a)) for a in now])
            if k:
                seq_ref[k - 1, 0], seq_ref[k - 1, 1] = pairs_of(map(halves, before), map(halves, now))
            before = now


def resample(operands, left, right):
    depth, rows, parts, columns = operands[0].shape
    margin = left.shape[1]
    chunks = (rows - 2 * margin) // TILE // 2
    lanes = parts * TILE
    blocks, width = columns // LOOK_RG, lanes // 4
    shapes = [pltpu.VMEM((2, 2, columns, lanes // 2), BF)] * depth
    shapes += [pltpu.VMEM((max(depth - 1, 1), 2, blocks, width), F32), pltpu.VMEM((depth, blocks, width), F32)]
    arrays = resident(*operands, left, right)
    outs = pl.pallas_call(
        partial(resample_kernel, margin),
        in_specs=[VMEM] * len(arrays),
        out_specs=[VMEM] * len(shapes) * chunks,
        out_shape=shapes * chunks,
        scratch_shapes=[
            pltpu.VMEM((TILE, lanes), BF),
            pltpu.VMEM((2, 2, 2, parts * (TILE // 2 + 2 * margin), lanes // 2), BF),
            pltpu.VMEM((depth, columns + 2 * margin, columns), BF),
        ],
        compiler_params=SMALL,
        name="resample",
    )(*arrays)
    return [outs[n * len(shapes) : (n + 1) * len(shapes)] for n in range(chunks)]


def choose_kernel(first, bit, stored, owner_ref, me_ref, *refs):
    sources, outs, sems = refs[:2], refs[2:-1], refs[-1]
    me = me_ref[0]
    copies = []
    for n, out in enumerate(outs):
        tile = 2 * (first + n) + (me & 1)
        here, there = [ref.at[0, tile] if stored else ref for ref in sources]
        same = ((owner_ref[tile] ^ me) >> bit) & 1 == 0
        copies.append(pltpu.make_async_copy(here, out, sems.at[n]))
        pl.when(same)(copies[n].start)
        pl.when(jnp.logical_not(same))(pltpu.make_async_copy(there, out, sems.at[n]).start)
    for copy in copies:
        copy.wait()


def choose(owner, me, here, there, first, bit, chunks):
    anywhere = pl.BlockSpec(memory_space=pl.ANY)
    return pl.pallas_call(
        partial(choose_kernel, first, bit, here.ndim > 3),
        in_specs=[SMEM, SMEM, anywhere, anywhere],
        out_specs=[VMEM] * chunks,
        out_shape=[pltpu.VMEM(here.shape[-3:], BF)] * chunks,
        scratch_shapes=[pltpu.SemaphoreType.DMA((chunks,))],
        compiler_params=SMALL,
        name="choose",
    )(owner, me, here, there)


def halves(block):
    width = block.shape[1] // 2
    wide = block.astype(F32)
    return wide[:, :width], wide[:, width:]


def looks(value):
    blocks = value.shape[0] // LOOK_RG
    total = value[:blocks]
    for look in range(1, LOOK_RG):
        total = total + value[look * blocks : (look + 1) * blocks]
    shift = value.shape[1] // 2
    while shift >= value.shape[1] // LOOK_AZ:
        total = total + pltpu.roll(total, shift, 1)
        shift //= 2
    return total * (1.0 / (LOOK_AZ * LOOK_RG))


def pair(first, second):
    a_re, a_im = first
    b_re, b_im = second
    return looks(a_re * b_re + a_im * b_im), looks(a_im * b_re - a_re * b_im)


def power(first):
    re, im = first
    return looks(re * re + im * im)


def joined(pieces):
    blocks = pieces[0].shape[1] // LOOK_AZ
    group = over(iota(pieces[0].shape, 1), blocks)
    total = pieces[0]
    for position in range(1, len(pieces)):
        total = jnp.where(group >= position, pieces[position], total)
    return total


def pairs_of(leads, followers):
    found = [pair(a, b) for a, b in zip(leads, followers)]
    return joined([re for re, _ in found]), joined([im for _, im in found])


def unit_refs(ref):
    return [ref.at[s, half] for s in range(ref.shape[0]) for half in range(2)]


def reference_kernel(me_ref, own_ref, mate_ref, *refs):
    depth = len(refs) - 2
    cur_refs, (pair_ref, pow_ref) = refs[:depth], refs[depth:]
    columns, half_rows = own_ref.shape[2], own_ref.shape[0] // 2
    core = me_ref[0] & 1
    size = 2 * half_rows
    row, part = lane_row(iota((1, size), 1), half_rows)
    order = chosen((size, size), 0, 2 * row + part)
    turn = chosen((columns, columns), 1, look_column(iota((columns, 1), 0), columns))
    powers, pairs = [], [[] for _ in range(depth)]
    for ref, place in ((own_ref, core), (mate_ref, 1 - core)):
        for half in range(2):
            rows = ref[half * half_rows : (half + 1) * half_rows].reshape(size, columns)
            lead = dot(turn, dot(rows, order, OVER_ROWS).astype(BF))
            lead = lead[:, :half_rows], lead[:, half_rows:]
            powers.append(power(lead))
            for k in range(depth):
                pairs[k].append(pair(lead, halves(cur_refs[k][place, half])))

    def in_order(pieces):
        return joined([jnp.where(core == 0, pieces[n], pieces[(n + 2) % 4]) for n in range(4)])

    pow_ref[...] = in_order(powers)
    for k in range(depth):
        pair_ref[k, 0] = in_order([re for re, _ in pairs[k]])
        pair_ref[k, 1] = in_order([im for _, im in pairs[k]])


def reference_products(me, own, mate, currents):
    _, _, columns, width = currents[0].shape
    depth = len(currents)
    shapes = [(depth, 2, columns // LOOK_RG, width // 2), (columns // LOOK_RG, width // 2)]
    return pl.pallas_call(
        reference_kernel,
        in_specs=[SMEM] + [VMEM] * (2 + depth),
        out_specs=[VMEM] * len(shapes),
        out_shape=[pltpu.VMEM(shape, F32) for shape in shapes],
        compiler_params=SMALL,
        name="reference_products",
    )(me, *resident(own, mate, *currents))


def leading_kernel(lead_ref, cur_ref, out_ref):
    leads = [halves(r[...]) for r in unit_refs(lead_ref)]
    out_ref[0], out_ref[1] = pairs_of(leads, [halves(r[...]) for r in unit_refs(cur_ref)])
    out_ref[2] = joined([power(a) for a in leads])


def leading_products(lead, current):
    _, _, columns, width = lead.shape
    return pl.pallas_call(
        leading_kernel,
        in_specs=[VMEM] * 2,
        out_specs=VMEM,
        out_shape=pltpu.VMEM((3, columns // LOOK_RG, width // 2), F32),
        compiler_params=SMALL,
        name="leading_products",
    )(*resident(lead, current))


def finish_kernel(me_ref, *refs):
    inputs, (ref_out, seq_out, coh_out) = refs[:-3], refs[-3:]
    at_head = me_ref[0] == 0
    lanes = inputs[1].shape[-1]
    for chunk in range(len(inputs) // 5):
        pairs, pair_pow, lead, seq, powers = inputs[5 * chunk : 5 * chunk + 5]
        rows = slice(chunk * lanes, (chunk + 1) * lanes)
        earlier = jnp.where(at_head, pair_pow[...], lead[2])
        for k in range(ref_out.shape[0]):
            if k:
                re, im = seq[k - 1, 0], seq[k - 1, 1]
            else:
                re = jnp.where(at_head, pairs[0, 0], lead[0])
                im = jnp.where(at_head, pairs[0, 1], lead[1])
            now = powers[k]
            ref_out[k, 0, :, rows] = pairs[k, 0]
            ref_out[k, 1, :, rows] = pairs[k, 1]
            seq_out[k, 0, :, rows] = re
            seq_out[k, 1, :, rows] = im
            coh_out[k, :, rows] = jnp.sqrt(re * re + im * im) / jnp.sqrt(earlier * now + eps_power)
            earlier = now


def finish(me, parts, depth):
    flat = [a for part in parts for a in part]
    blocks, lanes = flat[1].shape
    rows = len(parts) * lanes
    shapes = [(depth, 2, blocks, rows)] * 2 + [(depth, blocks, rows)]
    outs = pl.pallas_call(
        finish_kernel,
        in_specs=[SMEM] + [VMEM] * len(flat),
        out_specs=[VMEM] * 3,
        out_shape=[jax.ShapeDtypeStruct(shape, F32) for shape in shapes],
        compiler_params=SMALL,
        name="finish",
    )(me, *resident(*flat))
    return tuple(jnp.swapaxes(a, -1, -2) for a in outs)


def swapped(block, axis, bit):
    return lax.ppermute(block, axis, [(i, i ^ (1 << bit)) for i in range(lax.axis_size(axis))])


def shifted(block, axis, distance):
    count = lax.axis_size(axis)
    return lax.ppermute(block, axis, [(i, i + distance) for i in range(count) if 0 <= i + distance < count])


def local(
    secondary,
    reference_store,
    tile_owner,
    az_kernel,
    rg_kernel,
    az_offset,
    az_index,
    rg_offset,
    rg_index,
):
    depth = secondary.shape[0]
    chunks = reference_store.shape[1] // 2
    bits = lax.axis_size("scene").bit_length() - 1
    me = lax.axis_index("scene").astype(jnp.int32)[None]

    arrived = swapped(reference_store, "scene", 0)
    operands, head, tail = load(
        secondary, az_kernel.T, rg_kernel.T, rg_offset, rg_index, az_index, az_offset
    )
    stored, owner = (pltpu.with_memory_space_constraint(a, pltpu.HBM) for a in (reference_store, tile_owner))
    held = list(choose(owner, me, stored, arrived, 0, 0, chunks))
    for bit in range(1, bits):
        for n in range(chunks):
            got = swapped(held[n], "scene", bit)
            held[n] = choose(owner, me, held[n], got, n, bit, 1)[0]
    left = shifted(tail, "range", 1)
    right = shifted(head, "range", -1)
    resampled = resample(operands, left, right)
    results = []
    for n, (*currents, seq, powers) in enumerate(resampled):
        backward = n % 2
        handed = shifted(currents[0], "scene", -1) if backward else shifted(currents[-1], "scene", 1)
        if backward:
            lead = leading_products(currents[-1], handed)
            lead = shifted(lead, "scene", 1)
        else:
            lead = leading_products(handed, currents[0])
        mate = swapped(held[n], "scene", 0)
        pairs, pair_pow = reference_products(me, held[n], mate, currents)
        results.append((pairs, pair_pow, lead, seq, powers))
    return finish(me, results, depth)


def solution(mesh):
    in_specs = (
        P(("parts", "scene"), None, None, "range"),
        P(("parts", "scene"), None, None, None, "range"),
        P("parts"),
        P(),
        P(),
        P(("parts", "scene"), None),
        P(("parts", "scene"), None),
        P(("parts", "scene"), "range"),
        P(("parts", "scene"), "range"),
    )
    out_specs = (
        P(("parts", "scene"), None, None, "range"),
        P(("parts", "scene"), None, None, "range"),
        P(("parts", "scene"), None, "range"),
    )
    return jax.shard_map(local, mesh=mesh, in_specs=in_specs, out_specs=out_specs, check_vma=False)
```

profile of v0, /device:TPU:1, one launch (start us, length us, event | category | flops | bytes accessed | tf_op | source)
XLA Modules:
  0.0 53.9 jit_solution(4523494966198095877)
XLA Ops:
  0.6 0.1 collective-permute-start
  0.7 2.7 %load.1 = (bf16[2,1056,2,256]{3,2,1,0:T(2,128)(2,1)S(1)}, f32[8,64]{1,0:T(8,128)S(1)}, f32[8,64]{1,0:T(8,128)S(1)}, s32[2,256]{1,0:T(2,128)S(1)}, s32[2,256]{1,0...) custom-call(bf16[2,1056,2,256]{3,2,1,0:T(2,128)(2,1)} %x_ref.1, ...), custom_call_target="tpu_custom_call" | custom-call | tf_op jit(solution)/shard_map/load/pallas_call | solution.py:105
  3.5 4.7 %collective-permute-start.3 = (bf16[2,16,2112]{2,1,0:T(8,128)(2,1)S(1)}, bf16[2,16,2112]{2,1,0:T(8,128)(2,1)S(1)}, u32[]{:S(2)}, u32[]{:S(2)}) collective-permute-start(bf16[2,16,2112]{2,1,0:T(8,128)(2,1)S(1)} %get-tuple-element.37), channel_id=1, source_target_pairs={{0,1},{1,2},{2,3},{4,5},{5,6},{6,7},{8,9},{9,10},{10,11},{12,13},{... | collective-permute-start | bytes 405512 | tf_op jit(solution)/shard_map/ppermute | solution.py:404
  8.2 1.3 %collective-permute-start.4 = (bf16[2,16,2112]{2,1,0:T(8,128)(2,1)S(1)}, bf16[2,16,2112]{2,1,0:T(8,128)(2,1)S(1)}, u32[]{:S(2)}, u32[]{:S(2)}) collective-permute-start(bf16[2,16,2112]{2,1,0:T(8,128)(2,1)S(1)} %get-tuple-element.38), channel_id=1, source_target_pairs={{1,0},{2,1},{3,2},{5,4},{6,5},{7,6},{9,8},{10,9},{11,10},{13,12},{... | collective-permute-start | bytes 405512 | tf_op jit(solution)/shard_map/ppermute | solution.py:404
  9.5 1.7 %collective-permute-done.3.left_ref = bf16[2,16,2112]{2,1,0:T(8,128)(2,1)S(1)} collective-permute-done((bf16[2,16,2112]{2,1,0:T(8,128)(2,1)S(1)}, bf16[2,16,2112]{2,1,0:T(8,128)(2,1)S(1)}, u32[]{:S(2)}, u32[]{:S(2)}) %collective-permute-start.3) | collective-permute-done | bytes 135200 | tf_op jit(solution)/shard_map/ppermute | solution.py:404
  11.1 3.8 %collective-permute-done.4.right_ref = bf16[2,16,2112]{2,1,0:T(8,128)(2,1)S(1)} collective-permute-done((bf16[2,16,2112]{2,1,0:T(8,128)(2,1)S(1)}, bf16[2,16,2112]{2,1,0:T(8,128)(2,1)S(1)}, u32[]{:S(2)}, u32[]{:S(2)}) %collective-permute-start.4) | collective-permute-done | bytes 135200 | tf_op jit(solution)/shard_map/ppermute | solution.py:404
  15.0 5.8 %resample.1 = (bf16[2,2,256,256]{3,2,1,0:T(8,128)(2,1)S(1)}, bf16[2,2,256,256]{3,2,1,0:T(8,128)(2,1)S(1)}, f32[1,2,16,128]{3,2,1,0:T(8,128)S(1)}, f32[2,16,128]{...) custom-call(bf16[2,1056,2,256]{3,2,1,0:T(2,128)(2,1)S(1)} %get-tuple, ...), custom_call_target="tpu_custom_call" | custom-call | tf_op jit(solution)/shard_map/resample/pallas_call | solution.py:208
  20.8 3.1 %collective-permute-start.8 = (bf16[2,2,256,256]{3,2,1,0:T(8,128)(2,1)S(1)}, bf16[2,2,256,256]{3,2,1,0:T(8,128)(2,1)}, u32[]{:S(2)}, u32[]{:S(2)}) collective-permute-start(bf16[2,2,256,256]{3,2,1,0:T(8,128)(2,1)S(1)} %get-tuple-element.46.refs_0_), channel_id=1, source_target_pairs={{4,0},{8,4},{12,8},{5,1},{9,5},{13,9},{6,2},{10,6},{14,10},{7,3},{... | collective-permute-start | bytes 1572872 | tf_op jit(solution)/shard_map/ppermute | solution.py:404
  23.9 3.0 %collective-permute-start.5 = (bf16[2,2,256,256]{3,2,1,0:T(8,128)(2,1)S(1)}, bf16[2,2,256,256]{3,2,1,0:T(8,128)(2,1)S(1)}, u32[]{:S(2)}, u32[]{:S(2)}) collective-permute-start(bf16[2,2,256,256]{3,2,1,0:T(8,128)(2,1)S(1)} %get-tuple-element.40.refs_1_), channel_id=1, source_target_pairs={{0,4},{4,8},{8,12},{1,5},{5,9},{9,13},{2,6},{6,10},{10,14},{3,7},{... | collective-permute-start | bytes 1572872 | tf_op jit(solution)/shard_map/ppermute | solution.py:404
  26.9 0.0 collective-permute-done.refs_1_
  26.9 1.6 %choose.3 = (bf16[256,2,256]{2,1,0:T(2,128)(2,1)S(1)}, bf16[256,2,256]{2,1,0:T(2,128)(2,1)S(1)}) custom-call(s32[4]{0:T(128)} %owner_ref.5, s32[1]{0:T(128)} %bitcast.me_ref, bf16[1,4,256,2,256]{4,3,2,1,0:T(2,128)(2,1)} %refs_0_.1, bf16[1,4,256,2,256]{4,3,2,1,0:T(2,128)(2,1)S(1)} %collective-permute-done.refs_1_), custom_call_target="tpu_custom_call" | custom-call | tf_op jit(solution)/shard_map/choose/pallas_call | solution.py:241
  28.6 0.3 collective-permute-start.6
  28.9 1.2 %collective-permute-start.1 = (bf16[256,2,256]{2,1,0:T(2,128)(2,1)S(1)}, bf16[256,2,256]{2,1,0:T(2,128)(2,1)S(1)}, u32[]{:S(2)}, u32[]{:S(2)}) collective-permute-start(bf16[256,2,256]{2,1,0:T(2,128)(2,1)S(1)} %get-tuple-element.29.refs_0_), channel_id=1, source_target_pairs={{0,8},{4,12},{8,0},{12,4},{1,9},{5,13},{9,1},{13,5},{2,10},{6,14},... | collective-permute-start | bytes 786440 | tf_op jit(solution)/shard_map/ppermute | solution.py:399
  30.1 10.5 %collective-permute-done.6.refs_1_ = bf16[256,2,256]{2,1,0:T(2,128)(2,1)S(1)} collective-permute-done((bf16[256,2,256]{2,1,0:T(2,128)(2,1)S(1)}, bf16[256,2,256]{2,1,0:T(2,128)(2,1)S(1)}, u32[]{:S(2)}, u32[]{:S(2)}) %collective-permute-start.6) | collective-permute-done | bytes 262176 | tf_op jit(solution)/shard_map/ppermute | solution.py:399
  40.7 0.7 %choose.5.own_ref = bf16[256,2,256]{2,1,0:T(2,128)(2,1)S(1)} custom-call(s32[4]{0:T(128)} %owner_ref.5, s32[1]{0:T(128)} %bitcast.me_ref, bf16[256,2,256]{2,1,0:T(2,128)(2,1)S(1)} %get-tuple-element.45.refs_0_, bf16[256,2,256]{2,1,0:T(2,128)(2,1)S(1)} %collective-permute-done.6.refs_1_), custom_call_target="tpu_custom_call" | custom-call | tf_op jit(solution)/shard_map/choose/pallas_call | solution.py:241
  41.4 0.1 collective-permute-start.7
  41.5 2.8 %collective-permute-done.1.refs_1_ = bf16[256,2,256]{2,1,0:T(2,128)(2,1)S(1)} collective-permute-done((bf16[256,2,256]{2,1,0:T(2,128)(2,1)S(1)}, bf16[256,2,256]{2,1,0:T(2,128)(2,1)S(1)}, u32[]{:S(2)}, u32[]{:S(2)}) %collective-permute-start.1) | collective-permute-done | bytes 262176 | tf_op jit(solution)/shard_map/ppermute | solution.py:399
  44.3 0.7 %choose.4.own_ref = bf16[256,2,256]{2,1,0:T(2,128)(2,1)S(1)} custom-call(s32[4]{0:T(128)} %owner_ref.5, s32[1]{0:T(128)} %bitcast.me_ref, bf16[256,2,256]{2,1,0:T(2,128)(2,1)S(1)} %get-tuple-element.29.refs_0_, bf16[256,2,256]{2,1,0:T(2,128)(2,1)S(1)} %collective-permute-done.1.refs_1_), custom_call_target="tpu_custom_call" | custom-call | tf_op jit(solution)/shard_map/choose/pallas_call | solution.py:241
  45.0 0.1 collective-permute-start.2
  45.1 0.0 collective-permute-done.8.cur_ref
  45.1 1.5 %leading_products.3 = f32[3,16,128]{2,1,0:T(8,128)S(1)} custom-call(bf16[2,2,256,256]{3,2,1,0:T(8,128)(2,1)S(1)} %get-tuple-element.47.refs_1_.lead_ref, bf16[2,2,256,256]{3,2,1,0:T(8,128)(2,1)} %collective-permute-done.8.cur_ref), custom_call_target="tpu_custom_call" | custom-call | tf_op jit(solution)/shard_map/leading_products/pallas_call | solution.py:349
  46.6 4.2 %collective-permute-start.9 = (f32[3,16,128]{2,1,0:T(8,128)S(1)}, f32[3,16,128]{2,1,0:T(8,128)S(1)}, u32[]{:S(2)}, u32[]{:S(2)}) collective-permute-start(f32[3,16,128]{2,1,0:T(8,128)S(1)} %leading_products.3), channel_id=1, source_target_pairs={{0,4},{4,8},{8,12},{1,5},{5,9},{9,13},{2,6},{6,10},{10,14},{3,7},{... | collective-permute-start | bytes 73736 | tf_op jit(solution)/shard_map/ppermute | solution.py:404
  50.8 0.0 collective-permute-done.5.lead_ref
  50.8 0.5 leading_products.2.refs_2_
  51.2 0.0 collective-permute-done.7.mate_ref
  51.2 1.0 %reference_products.3 = (f32[2,2,16,128]{3,2,1,0:T(8,128)S(1)}, f32[16,128]{1,0:T(8,128)S(1)}) custom-call(s32[1]{0:T(128)} %bitcast.me_ref, bf16[256,2,256]{2,1,0:T(2,128)(2,1)S(1)} %choose.5.own_ref, bf16[256,2,256]{2,1,0:T(2,128)(2,1)S(1)} %collective-permute-done.7.mate_ref, bf16[2,2,256,256]{3,2,1,0:T(8,128)(2,1)S(1)} %get-tuple-element.46.refs_0_, ...), custom_call_target="tpu_custom_call" | custom-call | tf_op jit(solution)/shard_map/reference_products/pallas_call | solution.py:331
  52.2 0.0 collective-permute-done.2.mate_ref
  52.2 1.0 %reference_products.2 = (f32[2,2,16,128]{3,2,1,0:T(8,128)S(1)}, f32[16,128]{1,0:T(8,128)S(1)}) custom-call(s32[1]{0:T(128)} %bitcast.me_ref, bf16[256,2,256]{2,1,0:T(2,128)(2,1)S(1)} %choose.4.own_ref, bf16[256,2,256]{2,1,0:T(2,128)(2,1)S(1)} %collective-permute-done.2.mate_ref, bf16[2,2,256,256]{3,2,1,0:T(8,128)(2,1)S(1)} %get-tuple-element.39.refs_0_.cur_ref, ...), custom_call_target="tpu_custom_call" | custom-call | tf_op jit(solution)/shard_map/reference_products/pallas_call | solution.py:331
  53.2 0.0 collective-permute-done.9.refs_7_
  53.2 0.7 %finish.1 = (f32[2,2,16,256]{3,2,1,0:T(8,128)}, f32[2,2,16,256]{3,2,1,0:T(8,128)}, f32[2,16,256]{2,1,0:T(8,128)}) custom-call(s32[1]{0:T(128)} %bitcast.me_ref, f32[2,2,16,128]{3,2,1,0:T(8,128)S(1)} %get-tuple-element.41.refs_0_, f32[16,128]{1,0:T(8,128)S(1)} %get-tuple-element.42.refs_1_, f32[3,16,128]{2,1,0:T(8,128)S(1)} %leading_products.2.refs_2_, ...), custom_call_target="tpu_custom_call" | custom-call | tf_op jit(solution)/shard_map/finish/pallas_call | solution.py:387
Async XLA Ops:
  0.6 26.3 %collective-permute-start = (bf16[1,4,256,2,256]{4,3,2,1,0:T(2,128)(2,1)}, bf16[1,4,256,2,256]{4,3,2,1,0:T(2,128)(2,1)S(1)}, u32[]{:S(2)}, u32[]{:S(2)}) collective-permute-start(bf16[1,4,256,2,256]{4,3,2,1,0:T(2,128)(2,1)} %refs_0_.1), channel_id=1, source_target_pairs={{0,4},{4,0},{8,12},{12,8},{1,5},{5,1},{9,13},{13,9},{2,6},{6,2},{1... | collective-permute-start | bytes 3145736 | tf_op jit(solution)/shard_map/ppermute | solution.py:399
  3.5 7.7 %collective-permute-start.3 = (bf16[2,16,2112]{2,1,0:T(8,128)(2,1)S(1)}, bf16[2,16,2112]{2,1,0:T(8,128)(2,1)S(1)}, u32[]{:S(2)}, u32[]{:S(2)}) collective-permute-start(bf16[2,16,2112]{2,1,0:T(8,128)(2,1)S(1)} %get-tuple-element.37), channel_id=1, source_target_pairs={{0,1},{1,2},{2,3},{4,5},{5,6},{6,7},{8,9},{9,10},{10,11},{12,13},{... | collective-permute-start | bytes 405512 | tf_op jit(solution)/shard_map/ppermute | solution.py:404
  8.2 6.8 %collective-permute-start.4 = (bf16[2,16,2112]{2,1,0:T(8,128)(2,1)S(1)}, bf16[2,16,2112]{2,1,0:T(8,128)(2,1)S(1)}, u32[]{:S(2)}, u32[]{:S(2)}) collective-permute-start(bf16[2,16,2112]{2,1,0:T(8,128)(2,1)S(1)} %get-tuple-element.38), channel_id=1, source_target_pairs={{1,0},{2,1},{3,2},{5,4},{6,5},{7,6},{9,8},{10,9},{11,10},{13,12},{... | collective-permute-start | bytes 405512 | tf_op jit(solution)/shard_map/ppermute | solution.py:404
  20.8 24.3 %collective-permute-start.8 = (bf16[2,2,256,256]{3,2,1,0:T(8,128)(2,1)S(1)}, bf16[2,2,256,256]{3,2,1,0:T(8,128)(2,1)}, u32[]{:S(2)}, u32[]{:S(2)}) collective-permute-start(bf16[2,2,256,256]{3,2,1,0:T(8,128)(2,1)S(1)} %get-tuple-element.46.refs_0_), channel_id=1, source_target_pairs={{4,0},{8,4},{12,8},{5,1},{9,5},{13,9},{6,2},{10,6},{14,10},{7,3},{... | collective-permute-start | bytes 1572872 | tf_op jit(solution)/shard_map/ppermute | solution.py:404
  23.9 26.9 %collective-permute-start.5 = (bf16[2,2,256,256]{3,2,1,0:T(8,128)(2,1)S(1)}, bf16[2,2,256,256]{3,2,1,0:T(8,128)(2,1)S(1)}, u32[]{:S(2)}, u32[]{:S(2)}) collective-permute-start(bf16[2,2,256,256]{3,2,1,0:T(8,128)(2,1)S(1)} %get-tuple-element.40.refs_1_), channel_id=1, source_target_pairs={{0,4},{4,8},{8,12},{1,5},{5,9},{9,13},{2,6},{6,10},{10,14},{3,7},{... | collective-permute-start | bytes 1572872 | tf_op jit(solution)/shard_map/ppermute | solution.py:404
  28.6 12.1 %collective-permute-start.6 = (bf16[256,2,256]{2,1,0:T(2,128)(2,1)S(1)}, bf16[256,2,256]{2,1,0:T(2,128)(2,1)S(1)}, u32[]{:S(2)}, u32[]{:S(2)}) collective-permute-start(bf16[256,2,256]{2,1,0:T(2,128)(2,1)S(1)} %get-tuple-element.45.refs_0_), channel_id=1, source_target_pairs={{0,8},{4,12},{8,0},{12,4},{1,9},{5,13},{9,1},{13,5},{2,10},{6,14},... | collective-permute-start | bytes 786440 | tf_op jit(solution)/shard_map/ppermute | solution.py:399
  28.9 15.4 %collective-permute-start.1 = (bf16[256,2,256]{2,1,0:T(2,128)(2,1)S(1)}, bf16[256,2,256]{2,1,0:T(2,128)(2,1)S(1)}, u32[]{:S(2)}, u32[]{:S(2)}) collective-permute-start(bf16[256,2,256]{2,1,0:T(2,128)(2,1)S(1)} %get-tuple-element.29.refs_0_), channel_id=1, source_target_pairs={{0,8},{4,12},{8,0},{12,4},{1,9},{5,13},{9,1},{13,5},{2,10},{6,14},... | collective-permute-start | bytes 786440 | tf_op jit(solution)/shard_map/ppermute | solution.py:399
  41.4 9.9 %collective-permute-start.7 = (bf16[256,2,256]{2,1,0:T(2,128)(2,1)S(1)}, bf16[256,2,256]{2,1,0:T(2,128)(2,1)S(1)}, u32[]{:S(2)}, u32[]{:S(2)}) collective-permute-start(bf16[256,2,256]{2,1,0:T(2,128)(2,1)S(1)} %choose.5.own_ref), channel_id=1, source_target_pairs={{0,4},{4,0},{8,12},{12,8},{1,5},{5,1},{9,13},{13,9},{2,6},{6,2},{1... | collective-permute-start | bytes 786440 | tf_op jit(solution)/shard_map/ppermute | solution.py:399
  45.0 7.2 %collective-permute-start.2 = (bf16[256,2,256]{2,1,0:T(2,128)(2,1)S(1)}, bf16[256,2,256]{2,1,0:T(2,128)(2,1)S(1)}, u32[]{:S(2)}, u32[]{:S(2)}) collective-permute-start(bf16[256,2,256]{2,1,0:T(2,128)(2,1)S(1)} %choose.4.own_ref), channel_id=1, source_target_pairs={{0,4},{4,0},{8,12},{12,8},{1,5},{5,1},{9,13},{13,9},{2,6},{6,2},{1... | collective-permute-start | bytes 786440 | tf_op jit(solution)/shard_map/ppermute | solution.py:399
  46.6 6.6 %collective-permute-start.9 = (f32[3,16,128]{2,1,0:T(8,128)S(1)}, f32[3,16,128]{2,1,0:T(8,128)S(1)}, u32[]{:S(2)}, u32[]{:S(2)}) collective-permute-start(f32[3,16,128]{2,1,0:T(8,128)S(1)} %leading_products.3), channel_id=1, source_target_pairs={{0,4},{4,8},{8,12},{1,5},{5,9},{9,13},{2,6},{6,10},{10,14},{3,7},{... | collective-permute-start | bytes 73736 | tf_op jit(solution)/shard_map/ppermute | solution.py:404
where the time goes:
time: 54.2 us; the launch traced here: 53.9 us
  waiting for transfers between devices  18.9 us (35%)
  starting transfers between devices  18 us (33%)
  Pallas kernels  16.2 us (30%)
  between operations  0.79 us (1%)
    ppermute x5, starting transfers between devices, shifted(): lax.ppermute(block, axis, [(i, i + distance) for i in range(count) if 0 <...  16.3 us
    ppermute x5, waiting for transfers between devices, swapped(): lax.ppermute(block, axis, [(i, i ^ 1 << bit) for i in range(lax.axis_size...  13.4 us
    pallas_call x1, Pallas kernels, resample(): pl.pallas_call(partial(resample_kernel, margin), in_specs=[VMEM] * len(ar...  5.83 us
    ppermute x5, waiting for transfers between devices, shifted(): lax.ppermute(block, axis, [(i, i + distance) for i in range(count) if 0 <...  5.53 us
    pallas_call x3, Pallas kernels, choose(): pl.pallas_call(partial(choose_kernel, first, bit, here.ndim > 3), in_spec...  3.05 us
    pallas_call x1, Pallas kernels, load(): pl.pallas_call(partial(load_kernel, margin), in_specs=[anywhere] * len(op...  2.75 us
    pallas_call x2, Pallas kernels, leading_products(): pl.pallas_call(leading_kernel, in_specs=[VMEM] * 2, out_specs=VMEM, out_s...  1.95 us
    pallas_call x2, Pallas kernels, reference_products(): pl.pallas_call(reference_kernel, in_specs=[SMEM] + [VMEM] * (2 + depth),...  1.93 us
  transfers between devices with their start and end apart: 10, of which 4 were waited for; matrix products, arithmetic and copies ran while one was open for 0% of the time, Pallas kernels for 29%

commit v1 on v0

v1 whole, which is shorter than its diff:
```python
from functools import partial

import jax
import jax.numpy as jnp
from jax import lax
from jax.experimental import pallas as pl
from jax.experimental.pallas import tpu as pltpu
from jax.sharding import PartitionSpec as P


TILE = 256
PIECE = 64
LOOK_AZ = 4
LOOK_RG = 16

eps_power = 1e-06

BF = jnp.bfloat16
F32 = jnp.float32
ACROSS = (((1,), (0,)), ((), ()))
OVER_ROWS = (((0,), (0,)), ((), ()))
OVER_LANES = (((1,), (1,)), ((), ()))
VMEM = pl.BlockSpec(memory_space=pltpu.VMEM)
SMEM = pl.BlockSpec(memory_space=pltpu.SMEM)
SMALL = pltpu.CompilerParams(vmem_limit_bytes=12 << 20)


def iota(shape, dim):
    return lax.broadcasted_iota(jnp.int32, shape, dim)


def over(value, size):
    return value >> (size.bit_length() - 1)


def dot(a, b, dims=ACROSS):
    return lax.dot_general(a, b, dims, preferred_element_type=F32)


def lane_row(lane, half_rows):
    blocks = half_rows // LOOK_AZ
    inner = lane & (half_rows - 1)
    return LOOK_AZ * (inner & (blocks - 1)) + over(inner, blocks), over(lane, half_rows) & 1


def look_column(place, columns):
    blocks = columns // LOOK_RG
    return LOOK_RG * (place & (blocks - 1)) + over(place, blocks)


def chosen(shape, dim, wanted):
    return (iota(shape, dim) == wanted).astype(F32).astype(BF)


def taps_and_offsets(kernel_t, index_row, offset_row, spread):
    count = kernel_t.shape[1]
    taps = dot(kernel_t.astype(BF), chosen((count, index_row.shape[1]), 0, index_row))
    offsets = jnp.broadcast_to(offset_row.astype(F32), (8, offset_row.shape[1]))
    return dot(jnp.concatenate([taps, offsets], 0).astype(BF), spread)


def resident(*arrays):
    return [pltpu.with_memory_space_constraint(a, pltpu.VMEM) for a in arrays]


def load_kernel(margin, x_ref, *refs):
    count = (len(refs) - 4) // 2
    small_refs, x_out, outs = refs[:count], refs[count], refs[count + 1 : 2 * count + 1]
    first_ref, second_ref, sems = refs[2 * count + 1 :]
    depth, rows, parts, columns = x_ref.shape
    pieces = [(k, n) for k in range(depth) for n in range(rows // TILE)]

    def copy_of(position):
        k, n = pieces[position]
        size = TILE if n + 1 < rows // TILE else rows - n * TILE
        part = (k, pl.ds(n * TILE, size))
        return pltpu.make_async_copy(x_ref.at[part], x_out.at[part], sems.at[position]), part, size

    copies = [copy_of(position) for position in range(len(pieces))]
    small = [
        pltpu.make_async_copy(source, target, sems.at[len(pieces) + n])
        for n, (source, target) in enumerate(zip(small_refs, outs))
    ]
    for copy, _, _ in copies:
        copy.start()
    for copy in small:
        copy.start()
    place = iota((2 * margin, 1), 0)
    right_first = place + jnp.where(place < margin, columns - margin, -margin)
    left_first = place + jnp.where(place < margin, 0, columns - 2 * margin)
    edges = chosen((2 * margin, columns), 1, jnp.where(lax.axis_index("range") & 1 == 0, right_first, left_first))
    for (k, n), (copy, part, size) in zip(pieces, copies):
        copy.wait()
        found = dot(edges, x_out[part].reshape(parts * size, columns), OVER_LANES).astype(BF)
        lanes = slice(parts * n * TILE, parts * (n * TILE + size))
        first_ref[k, :, lanes] = found[:margin]
        second_ref[k, :, lanes] = found[margin:]
    for copy in small:
        copy.wait()


def load(secondary, *small):
    depth, rows, parts, _ = secondary.shape
    margin = (rows - small[-1].shape[1]) // 2
    operands = (secondary, *small)
    edge = pltpu.VMEM((depth, margin, parts * rows), BF)
    anywhere = pl.BlockSpec(memory_space=pl.ANY)
    outs = pl.pallas_call(
        partial(load_kernel, margin),
        in_specs=[anywhere] * len(operands),
        out_specs=[VMEM] * (len(operands) + 2),
        out_shape=[pltpu.VMEM(a.shape, a.dtype) for a in operands] + [edge, edge],
        scratch_shapes=[pltpu.SemaphoreType.DMA((depth * (rows // TILE) + len(small),))],
        compiler_params=SMALL,
        name="load",
    )(*[pltpu.with_memory_space_constraint(a, pltpu.HBM) for a in operands])
    return outs[:-2], outs[-2], outs[-1]


def range_matrix(margin, kernel_ref, index_row, offset_row, order, column, rg_ref):
    taps = kernel_ref.shape[0]
    both = taps_and_offsets(kernel_ref[...], index_row, offset_row, order)
    base = column + both[taps : taps + 1].astype(jnp.int32) + (margin - 3)
    period = 2 * taps
    place = iota((period, order.shape[1]), 0) - base
    value = tap_pattern(both, place & (taps - 1))
    for block in range(rg_ref.shape[0] // period):
        home = over(place + block * period, taps)
        rg_ref[block * period : (block + 1) * period] = jnp.where(home == 0, value, 0.0).astype(BF)


def tap_pattern(both, which):
    value = jnp.zeros(which.shape, F32)
    for tap in range(both.shape[0] - 8):
        value = jnp.where(which == tap, both[tap : tap + 1], value)
    return value


def resample_kernel(
    calls, x_ref, azk_ref, rgk_ref, rgo_ref, rgi_ref, azi_ref, azo_ref, first_ref, second_ref, *refs,
):
    columns = x_ref.shape[3]
    margin = first_ref.shape[1]
    outs, (spread_ref, band_ref, rg_ref) = refs[: len(calls)], refs[len(calls) :]
    odd_column = lax.axis_index("range") & 1 == 1
    taps = azk_ref.shape[0]
    tile, lanes = spread_ref.shape
    half_rows, half_lanes = tile // 2, lanes // 2
    period = 2 * taps
    lane = iota((1, lanes), 1)
    row, part = lane_row(lane, half_rows)
    spread_ref[...] = chosen((tile, lanes), 0, row + half_rows * over(lane, half_lanes))
    column = look_column(iota((1, columns), 1), columns)
    order = chosen((columns, columns), 0, column)
    for k in sorted({k for k, _ in calls}):
        range_matrix(
            margin, rgk_ref, rgi_ref[k : k + 1], rgo_ref[k : k + 1], order, column, rg_ref.at[k]
        )
    for call, (k, chunk) in enumerate(calls):
        for s in range(2):
            start = (2 * chunk + s) * tile
            rows = slice(start, start + tile)
            both = taps_and_offsets(
                azk_ref[...], azi_ref[k : k + 1, rows], azo_ref[k : k + 1, rows], spread_ref[...]
            )
            base = row + both[taps : taps + 1].astype(jnp.int32) + (margin - 3)
            sub = iota((period, lanes), 0)
            place = (sub >> 1) - base
            value = tap_pattern(both, jnp.where((sub & 1) == part, place & (taps - 1), taps))
            home = -over(place, taps)
            for half in range(2):
                mine = slice(half * half_lanes, (half + 1) * half_lanes)
                band = band_ref.at[call % 2, s, half]
                for block in range(band.shape[0] // period):
                    band[block * period : (block + 1) * period] = jnp.where(
                        home[:, mine] == block, value[:, mine], 0.0
                    ).astype(BF)
                begin = start + half * half_rows
                size = half_rows + 2 * margin
                window = x_ref[k, begin : begin + size].reshape(2 * size, columns)
                across = slice(2 * begin, 2 * (begin + size))
                first_side, second_side = first_ref[k, :, across], second_ref[k, :, across]
                wide = jnp.concatenate(
                    [
                        dot(jnp.where(odd_column, first_side, second_side), band[...]).astype(BF),
                        dot(window, band[...], OVER_ROWS).astype(BF),
                        dot(jnp.where(odd_column, second_side, first_side), band[...]).astype(BF),
                    ],
                    0,
                )
                outs[call][s, half] = dot(rg_ref[k], wide, OVER_ROWS).astype(BF)


def resample(operands, first, second, calls):
    depth, _, parts, columns = operands[0].shape
    margin = first.shape[1]
    lanes = parts * TILE
    arrays = resident(*operands, first, second)
    return pl.pallas_call(
        partial(resample_kernel, calls),
        in_specs=[VMEM] * len(arrays),
        out_specs=[VMEM] * len(calls),
        out_shape=[pltpu.VMEM((2, 2, columns, lanes // 2), BF)] * len(calls),
        scratch_shapes=[
            pltpu.VMEM((TILE, lanes), BF),
            pltpu.VMEM((2, 2, 2, parts * (TILE // 2 + 2 * margin), lanes // 2), BF),
            pltpu.VMEM((depth, columns + 2 * margin, columns), BF),
        ],
        compiler_params=SMALL,
        name="resample",
    )(*arrays)


def choose_kernel(first, bit, stored, owner_ref, *refs):
    sources, outs, sems = refs[:2], refs[2:-1], refs[-1]
    me = lax.axis_index("scene")
    copies = []
    for n, out in enumerate(outs):
        tile = 2 * (first + n) + (me & 1)
        here, there = [ref.at[0, tile] if stored else ref for ref in sources]
        same = ((owner_ref[tile] ^ me) >> bit) & 1 == 0
        pieces = [pl.ds(m * PIECE, PIECE) for m in range(out.shape[0] // PIECE)]
        from_here, from_there = [
            [pltpu.make_async_copy(source.at[p], out.at[p], sems.at[n, m]) for m, p in enumerate(pieces)]
            for source in (here, there)
        ]

        @pl.when(same)
        def _():
            for copy in from_here:
                copy.start()

        @pl.when(jnp.logical_not(same))
        def _():
            for copy in from_there:
                copy.start()

        copies += from_here
    for copy in copies:
        copy.wait()


def choose(owner, here, there, first, bit, chunks):
    anywhere = pl.BlockSpec(memory_space=pl.ANY)
    return pl.pallas_call(
        partial(choose_kernel, first, bit, here.ndim > 3),
        in_specs=[SMEM, anywhere, anywhere],
        out_specs=[VMEM] * chunks,
        out_shape=[pltpu.VMEM(here.shape[-3:], BF)] * chunks,
        scratch_shapes=[pltpu.SemaphoreType.DMA((chunks, here.shape[-3] // PIECE))],
        compiler_params=SMALL,
        name="choose",
    )(owner, here, there)


def halves(block):
    width = block.shape[1] // 2
    wide = block.astype(F32)
    return wide[:, :width], wide[:, width:]


def looks(value):
    blocks = value.shape[0] // LOOK_RG
    total = value[:blocks]
    for look in range(1, LOOK_RG):
        total = total + value[look * blocks : (look + 1) * blocks]
    shift = value.shape[1] // 2
    while shift >= value.shape[1] // LOOK_AZ:
        total = total + pltpu.roll(total, shift, 1)
        shift //= 2
    return total * (1.0 / (LOOK_AZ * LOOK_RG))


def pair(first, second):
    a_re, a_im = first
    b_re, b_im = second
    return looks(a_re * b_re + a_im * b_im), looks(a_im * b_re - a_re * b_im)


def power(first):
    re, im = first
    return looks(re * re + im * im)


def joined(pieces):
    blocks = pieces[0].shape[1] // LOOK_AZ
    group = over(iota(pieces[0].shape, 1), blocks)
    total = pieces[0]
    for position in range(1, len(pieces)):
        total = jnp.where(group >= position, pieces[position], total)
    return total


def pairs_of(leads, followers):
    found = [pair(a, b) for a, b in zip(leads, followers)]
    return joined([re for re, _ in found]), joined([im for _, im in found])


def reference_kernel(own_ref, mate_ref, *refs):
    depth = len(refs) - 2
    cur_refs, (pair_ref, pow_ref) = refs[:depth], refs[depth:]
    columns, half_rows = own_ref.shape[2], own_ref.shape[0] // 2
    core = lax.axis_index("scene") & 1
    size = 2 * half_rows
    row, part = lane_row(iota((1, size), 1), half_rows)
    order = chosen((size, size), 0, 2 * row + part)
    turn = chosen((columns, columns), 1, look_column(iota((columns, 1), 0), columns))
    powers, pairs = [], [[] for _ in range(depth)]
    for ref, place in ((own_ref, core), (mate_ref, 1 - core)):
        for half in range(2):
            rows = ref[half * half_rows : (half + 1) * half_rows].reshape(size, columns)
            lead = dot(turn, dot(rows, order, OVER_ROWS).astype(BF))
            lead = lead[:, :half_rows], lead[:, half_rows:]
            powers.append(power(lead))
            for k in range(depth):
                pairs[k].append(pair(lead, halves(cur_refs[k][place, half])))

    def in_order(pieces):
        return joined([jnp.where(core == 0, pieces[n], pieces[(n + 2) % 4]) for n in range(4)])

    pow_ref[...] = in_order(powers)
    for k in range(depth):
        pair_ref[k, 0] = in_order([re for re, _ in pairs[k]])
        pair_ref[k, 1] = in_order([im for _, im in pairs[k]])


def reference_products(own, mate, currents):
    _, _, columns, width = currents[0].shape
    depth = len(currents)
    shapes = [(depth, 2, columns // LOOK_RG, width // 2), (columns // LOOK_RG, width // 2)]
    return pl.pallas_call(
        reference_kernel,
        in_specs=[VMEM] * (2 + depth),
        out_specs=[VMEM] * len(shapes),
        out_shape=[pltpu.VMEM(shape, F32) for shape in shapes],
        compiler_params=SMALL,
        name="reference_products",
    )(*resident(own, mate, *currents))


def write_products(out, leads, followers):
    leads, followers = [[halves(a) for a in units] for units in (leads, followers)]
    out[0], out[1] = pairs_of(leads, followers)
    out[2] = joined([power(a) for a in leads])


def units_of(ref):
    return [ref[n // 2, n % 2] for n in range(4)]


def within_kernel(depth, *refs):
    chunks = len(refs) // (depth + 4)
    for n in range(chunks):
        got_ref, *cur_refs = refs[n * (depth + 1) : (n + 1) * (depth + 1)]
        lead_ref, seq_ref, pow_ref = refs[chunks * (depth + 1) + 3 * n :][:3]
        write_products(lead_ref, units_of(got_ref), units_of(cur_refs[0]))
        before = None
        for k, ref in enumerate(cur_refs):
            now = [halves(a) for a in units_of(ref)]
            pow_ref[k] = joined([power(a) for a in now])
            if k:
                seq_ref[k - 1, 0], seq_ref[k - 1, 1] = pairs_of(before, now)
            before = now


def within_products(got, currents):
    chunks, depth = len(currents), len(currents[0])
    _, _, columns, width = got[0].shape
    size = (columns // LOOK_RG, width // 2)
    arrays = [a for g, chunk in zip(got, currents) for a in (g, *chunk)]
    shapes = [(3, *size), (max(depth - 1, 1), 2, *size), (depth, *size)] * chunks
    outs = pl.pallas_call(
        partial(within_kernel, depth),
        in_specs=[VMEM] * len(arrays),
        out_specs=[VMEM] * len(shapes),
        out_shape=[pltpu.VMEM(shape, F32) for shape in shapes],
        compiler_params=SMALL,
        name="within_products",
    )(*resident(*arrays))
    return [outs[3 * n : 3 * n + 3] for n in range(chunks)]


def across_kernel(got_ref, first_ref, last_ref, out_ref):
    @pl.when(lax.axis_index("scene") & 1 == 1)
    def _():
        write_products(out_ref, units_of(last_ref), units_of(got_ref))

    @pl.when(lax.axis_index("scene") & 1 == 0)
    def _():
        write_products(out_ref, units_of(got_ref), units_of(first_ref))


def across_products(got, first, last):
    _, _, columns, width = got.shape
    return pl.pallas_call(
        across_kernel,
        in_specs=[VMEM] * 3,
        out_specs=VMEM,
        out_shape=pltpu.VMEM((3, columns // LOOK_RG, width // 2), F32),
        compiler_params=SMALL,
        name="across_products",
    )(*resident(got, first, last))


def pick_kernel(odd_ref, even_ref, out_ref):
    out_ref[...] = jnp.where(lax.axis_index("scene") & 1 == 1, odd_ref[...], even_ref[...])


def pick(odd, even):
    return pl.pallas_call(
        pick_kernel,
        in_specs=[VMEM] * 2,
        out_specs=VMEM,
        out_shape=pltpu.VMEM(odd.shape, odd.dtype),
        compiler_params=SMALL,
        name="pick",
    )(*resident(odd, even))


def finish_kernel(*refs):
    inputs, (ref_out, seq_out, coh_out) = refs[:-3], refs[-3:]
    at_head, odd = lax.axis_index("scene") == 0, lax.axis_index("scene") & 1 == 1
    lanes = inputs[1].shape[-1]
    for chunk in range(len(inputs) // 6):
        pairs, pair_pow, across, within, seq, powers = inputs[6 * chunk : 6 * chunk + 6]
        rows = slice(chunk * lanes, (chunk + 1) * lanes)

        def lead(place, own):
            return jnp.where(at_head, own, jnp.where(odd, within[place], across[place]))

        earlier = lead(2, pair_pow[...])
        for k in range(ref_out.shape[0]):
            if k:
                re, im = seq[k - 1, 0], seq[k - 1, 1]
            else:
                re, im = (lead(place, pairs[0, place]) for place in range(2))
            now = powers[k]
            ref_out[k, 0, :, rows] = pairs[k, 0]
            ref_out[k, 1, :, rows] = pairs[k, 1]
            seq_out[k, 0, :, rows] = re
            seq_out[k, 1, :, rows] = im
            coh_out[k, :, rows] = jnp.sqrt(re * re + im * im) / jnp.sqrt(earlier * now + eps_power)
            earlier = now


def finish(results, depth):
    flat = [a for result in results for a in result]
    blocks, lanes = flat[1].shape
    rows = len(results) * lanes
    shapes = [(depth, 2, blocks, rows)] * 2 + [(depth, blocks, rows)]
    outs = pl.pallas_call(
        finish_kernel,
        in_specs=[VMEM] * len(flat),
        out_specs=[VMEM] * 3,
        out_shape=[jax.ShapeDtypeStruct(shape, F32) for shape in shapes],
        compiler_params=SMALL,
        name="finish",
    )(*resident(*flat))
    return tuple(jnp.swapaxes(a, -1, -2) for a in outs)


def swapped(block, axis, bit):
    return lax.ppermute(block, axis, [(i, i ^ (1 << bit)) for i in range(lax.axis_size(axis))])


def neighbours(block, axis, first):
    count = lax.axis_size(axis)
    pairs = [(i, i + 1) for i in range(first, count - 1, 2)]
    return lax.ppermute(block, axis, pairs + [(j, i) for i, j in pairs])


def local(
    secondary,
    reference_store,
    tile_owner,
    az_kernel,
    rg_kernel,
    az_offset,
    az_index,
    rg_offset,
    rg_index,
):
    depth = secondary.shape[0]
    chunks = reference_store.shape[1] // 2
    bits = lax.axis_size("scene").bit_length() - 1

    arrived = swapped(reference_store, "scene", 0)
    operands, first, second = load(
        secondary, az_kernel.T, rg_kernel.T, rg_offset, rg_index, az_index, az_offset
    )
    first = neighbours(first, "range", 0)
    second = neighbours(second, "range", 1)
    stored, owner = (pltpu.with_memory_space_constraint(a, pltpu.HBM) for a in (reference_store, tile_owner))
    held = list(choose(owner, stored, arrived, 0, 0, chunks))
    for bit in range(1, bits):
        for n in range(chunks):
            got = swapped(held[n], "scene", bit)
            held[n] = choose(owner, held[n], got, n, bit, 1)[0]
    last = depth - 1
    early, late = [(last, 0), (0, 1)], [(k, n) for n in range(2) for k in range(depth)]
    late = [call for call in late if call not in early]
    units = dict(zip(early, resample(operands, first, second, early)))
    across = pick(units[last, 0], units[0, 1])
    across = neighbours(across, "scene", 1)
    units.update(zip(late, resample(operands, first, second, late)))
    currents = [[units[k, n] for k in range(depth)] for n in range(2)]
    within = []
    for n in range(2):
        within.append(swapped(currents[n][last], "scene", 0))
    within = within_products(within, currents)
    across = across_products(across, currents[0][0], currents[1][last])
    returned = neighbours(across, "scene", 1)
    results = []
    for n, small in enumerate(within):
        mate = swapped(held[n], "scene", 0)
        pairs, pair_pow = reference_products(held[n], mate, currents[n])
        results.append((pairs, pair_pow, (across, returned)[n], *small))
    return finish(results, depth)


def solution(mesh):
    in_specs = (
        P(("parts", "scene"), None, None, "range"),
        P(("parts", "scene"), None, None, None, "range"),
        P("parts"),
        P(),
        P(),
        P(("parts", "scene"), None),
        P(("parts", "scene"), None),
        P(("parts", "scene"), "range"),
        P(("parts", "scene"), "range"),
    )
    out_specs = (
        P(("parts", "scene"), None, None, "range"),
        P(("parts", "scene"), None, None, "range"),
        P(("parts", "scene"), None, "range"),
    )
    return jax.shard_map(local, mesh=mesh, in_specs=in_specs, out_specs=out_specs, check_vma=False)
```

time: 54.2 us -> 48.2 us (0.89)
  the two profiles are of different devices: /device:TPU:1 before, /device:TPU:17 now
where the time goes in v1:
time: 48.2 us; the launch traced here: 47.9 us
  starting transfers between devices  18.2 us (38%)
  Pallas kernels  18.1 us (38%)
  waiting for transfers between devices  10.8 us (22%)
  between operations  0.78 us (2%)
    ppermute x4, starting transfers between devices, neighbours(): return lax.ppermute(block, axis, pairs + [(j, i) for i, j in pairs])  9.95 us
    ppermute x7, starting transfers between devices, swapped(): lax.ppermute(block, axis, [(i, i ^ 1 << bit) for i in range(lax.axis_size...  8.28 us
    pallas_call x2, Pallas kernels, resample(): pl.pallas_call(partial(resample_kernel, calls), in_specs=[VMEM] * len(arr...  6.14 us
    ppermute x7, waiting for transfers between devices, swapped(): lax.ppermute(block, axis, [(i, i ^ 1 << bit) for i in range(lax.axis_size...  5.94 us
    ppermute x4, waiting for transfers between devices, neighbours(): return lax.ppermute(block, axis, pairs + [(j, i) for i, j in pairs])  4.9 us
    pallas_call x3, Pallas kernels, choose(): pl.pallas_call(partial(choose_kernel, first, bit, here.ndim > 3), in_spec...  3.82 us
    pallas_call x1, Pallas kernels, load(): pl.pallas_call(partial(load_kernel, margin), in_specs=[anywhere] * len(op...  2.75 us
    pallas_call x1, Pallas kernels, within_products(): pl.pallas_call(partial(within_kernel, depth), in_specs=[VMEM] * len(array...  2.24 us
  transfers between devices with their start and end apart: 11, of which 4 were waited for; matrix products, arithmetic and copies ran while one was open for 0% of the time, Pallas kernels for 36%

profile of v1, /device:TPU:17, one launch (start us, length us, event | category | flops | bytes accessed | tf_op | source)
XLA Modules:
  0.0 47.9 jit_solution(18205591129194160832)
XLA Ops:
  0.6 0.7 %collective-permute-start = (bf16[1,4,256,2,256]{4,3,2,1,0:T(2,128)(2,1)}, bf16[1,4,256,2,256]{4,3,2,1,0:T(2,128)(2,1)S(1)}, u32[]{:S(2)}, u32[]{:S(2)}) collective-permute-start(bf16[1,4,256,2,256]{4,3,2,1,0:T(2,128)(2,1)} %refs_0_.1), channel_id=1, source_target_pairs={{0,4},{4,0},{8,12},{12,8},{1,5},{5,1},{9,13},{13,9},{2,6},{6,2},{1... | collective-permute-start | bytes 3145736 | tf_op jit(solution)/shard_map/ppermute | solution.py:463
  1.4 2.7 %load.1 = (bf16[2,1056,2,256]{3,2,1,0:T(2,128)(2,1)S(1)}, f32[8,64]{1,0:T(8,128)S(1)}, f32[8,64]{1,0:T(8,128)S(1)}, s32[2,256]{1,0:T(2,128)S(1)}, s32[2,256]{1,0...) custom-call(bf16[2,1056,2,256]{3,2,1,0:T(2,128)(2,1)} %x_ref.1, ...), custom_call_target="tpu_custom_call" | custom-call | tf_op jit(solution)/shard_map/load/pallas_call | solution.py:108
  4.1 1.4 %collective-permute-start.3 = (bf16[2,16,2112]{2,1,0:T(8,128)(2,1)S(1)}, bf16[2,16,2112]{2,1,0:T(8,128)(2,1)S(1)}, u32[]{:S(2)}, u32[]{:S(2)}) collective-permute-start(bf16[2,16,2112]{2,1,0:T(8,128)(2,1)S(1)} %get-tuple-element.39), channel_id=1, source_target_pairs={{0,1},{2,3},{1,0},{3,2},{4,5},{6,7},{5,4},{7,6},{8,9},{10,11},{9,8... | collective-permute-start | bytes 405512 | tf_op jit(solution)/shard_map/ppermute | solution.py:469
  5.5 1.9 %collective-permute-start.4 = (bf16[2,16,2112]{2,1,0:T(8,128)(2,1)S(1)}, bf16[2,16,2112]{2,1,0:T(8,128)(2,1)S(1)}, u32[]{:S(2)}, u32[]{:S(2)}) collective-permute-start(bf16[2,16,2112]{2,1,0:T(8,128)(2,1)S(1)} %get-tuple-element.40), channel_id=1, source_target_pairs={{1,2},{2,1},{5,6},{6,5},{9,10},{10,9},{13,14},{14,13},{17,18},{18,... | collective-permute-start | bytes 405512 | tf_op jit(solution)/shard_map/ppermute | solution.py:469
  7.4 2.0 %collective-permute-done.3.first_ref = bf16[2,16,2112]{2,1,0:T(8,128)(2,1)S(1)} collective-permute-done((bf16[2,16,2112]{2,1,0:T(8,128)(2,1)S(1)}, bf16[2,16,2112]{2,1,0:T(8,128)(2,1)S(1)}, u32[]{:S(2)}, u32[]{:S(2)}) %collective-permute-start.3) | collective-permute-done | bytes 135200 | tf_op jit(solution)/shard_map/ppermute | solution.py:469
  9.4 2.9 %collective-permute-done.4.second_ref = bf16[2,16,2112]{2,1,0:T(8,128)(2,1)S(1)} collective-permute-done((bf16[2,16,2112]{2,1,0:T(8,128)(2,1)S(1)}, bf16[2,16,2112]{2,1,0:T(8,128)(2,1)S(1)}, u32[]{:S(2)}, u32[]{:S(2)}) %collective-permute-start.4) | collective-permute-done | bytes 135200 | tf_op jit(solution)/shard_map/ppermute | solution.py:469
  12.3 3.1 %resample.3 = (bf16[2,2,256,256]{3,2,1,0:T(8,128)(2,1)S(1)}, bf16[2,2,256,256]{3,2,1,0:T(8,128)(2,1)S(1)}) custom-call(bf16[2,1056,2,256]{3,2,1,0:T(2,128)(2,1)S(1)} %get-tuple-element.32.x_ref, f32[8,64]{1,0:T(8,128)S(1)} %get-tuple-element.33.azk_ref, f32[8,64]{1,0:T(8,128)S(1)} %get-tuple-element.34.rgk_ref, s32[2,256]{1,0:T(2,128)S(1)} %get-tuple-element.35.rgo_ref, ...), custom_call_target="tpu_custom_call" | custom-call | tf_op jit(solution)/shard_map/resample/pallas_call | solution.py:199
  15.4 0.1 pick.1
  15.4 4.2 %collective-permute-start.5 = (bf16[2,2,256,256]{3,2,1,0:T(8,128)(2,1)S(1)}, bf16[2,2,256,256]{3,2,1,0:T(8,128)(2,1)S(1)}, u32[]{:S(2)}, u32[]{:S(2)}) collective-permute-start(bf16[2,2,256,256]{3,2,1,0:T(8,128)(2,1)S(1)} %pick.1), channel_id=1, source_target_pairs={{4,8},{8,4},{5,9},{9,5},{6,10},{10,6},{7,11},{11,7},{20,24},{24,20... | collective-permute-start | bytes 1572872 | tf_op jit(solution)/shard_map/ppermute | solution.py:469
  19.6 0.1 collective-permute-start.6
  19.7 3.1 %resample.2 = (bf16[2,2,256,256]{3,2,1,0:T(8,128)(2,1)S(1)}, bf16[2,2,256,256]{3,2,1,0:T(8,128)(2,1)S(1)}) custom-call(bf16[2,1056,2,256]{3,2,1,0:T(2,128)(2,1)S(1)} %get-tuple-element.32.x_ref, f32[8,64]{1,0:T(8,128)S(1)} %get-tuple-element.33.azk_ref, f32[8,64]{1,0:T(8,128)S(1)} %get-tuple-element.34.rgk_ref, s32[2,256]{1,0:T(2,128)S(1)} %get-tuple-element.35.rgo_ref, ...), custom_call_target="tpu_custom_call" | custom-call | tf_op jit(solution)/shard_map/resample/pallas_call | solution.py:199
  22.8 0.0 collective-permute-done.refs_1_
  22.8 1.7 %choose.3 = (bf16[256,2,256]{2,1,0:T(2,128)(2,1)S(1)}, bf16[256,2,256]{2,1,0:T(2,128)(2,1)S(1)}) custom-call(s32[4]{0:T(128)} %owner_ref.5, bf16[1,4,256,2,256]{4,3,2,1,0:T(2,128)(2,1)} %refs_0_.1, bf16[1,4,256,2,256]{4,3,2,1,0:T(2,128)(2,1)S(1)} %collective-permute-done.refs_1_), custom_call_target="tpu_custom_call" | custom-call | tf_op jit(solution)/shard_map/choose/pallas_call | solution.py:245
  24.5 0.2 collective-permute-start.8
  24.7 0.8 %collective-permute-start.7 = (bf16[2,2,256,256]{3,2,1,0:T(8,128)(2,1)S(1)}, bf16[2,2,256,256]{3,2,1,0:T(8,128)(2,1)S(1)}, u32[]{:S(2)}, u32[]{:S(2)}) collective-permute-start(bf16[2,2,256,256]{3,2,1,0:T(8,128)(2,1)S(1)} %get-tuple-element.46.last_ref.refs_5_.refs_1_), channel_id=1, source_target_pairs={{0,4},{4,0},{8,12},{12,8},{1,5},{5,1},{9,13},{13,9},{2,6},{6,2},{1... | collective-permute-start | bytes 1572872 | tf_op jit(solution)/shard_map/ppermute | solution.py:463
  25.5 1.7 %collective-permute-start.1 = (bf16[256,2,256]{2,1,0:T(2,128)(2,1)S(1)}, bf16[256,2,256]{2,1,0:T(2,128)(2,1)S(1)}, u32[]{:S(2)}, u32[]{:S(2)}) collective-permute-start(bf16[256,2,256]{2,1,0:T(2,128)(2,1)S(1)} %get-tuple-element.31.refs_0_), channel_id=1, source_target_pairs={{0,8},{4,12},{8,0},{12,4},{1,9},{5,13},{9,1},{13,5},{2,10},{6,14},... | collective-permute-start | bytes 786440 | tf_op jit(solution)/shard_map/ppermute | solution.py:463
  27.2 4.4 %collective-permute-done.8.refs_1_ = bf16[256,2,256]{2,1,0:T(2,128)(2,1)S(1)} collective-permute-done((bf16[256,2,256]{2,1,0:T(2,128)(2,1)S(1)}, bf16[256,2,256]{2,1,0:T(2,128)(2,1)S(1)}, u32[]{:S(2)}, u32[]{:S(2)}) %collective-permute-start.8) | collective-permute-done | bytes 262176 | tf_op jit(solution)/shard_map/ppermute | solution.py:463
  31.6 1.1 %choose.5.own_ref = bf16[256,2,256]{2,1,0:T(2,128)(2,1)S(1)} custom-call(s32[4]{0:T(128)} %owner_ref.5, bf16[256,2,256]{2,1,0:T(2,128)(2,1)S(1)} %get-tuple-element.50.refs_0_, bf16[256,2,256]{2,1,0:T(2,128)(2,1)S(1)} %collective-permute-done.8.refs_1_), custom_call_target="tpu_custom_call" | custom-call | tf_op jit(solution)/shard_map/choose/pallas_call | solution.py:245
  32.7 3.1 %collective-permute-start.9 = (bf16[256,2,256]{2,1,0:T(2,128)(2,1)S(1)}, bf16[256,2,256]{2,1,0:T(2,128)(2,1)S(1)}, u32[]{:S(2)}, u32[]{:S(2)}) collective-permute-start(bf16[256,2,256]{2,1,0:T(2,128)(2,1)S(1)} %choose.5.own_ref), channel_id=1, source_target_pairs={{0,4},{4,0},{8,12},{12,8},{1,5},{5,1},{9,13},{13,9},{2,6},{6,2},{1... | collective-permute-start | bytes 786440 | tf_op jit(solution)/shard_map/ppermute | solution.py:463
  35.7 1.5 %collective-permute-done.1.refs_1_ = bf16[256,2,256]{2,1,0:T(2,128)(2,1)S(1)} collective-permute-done((bf16[256,2,256]{2,1,0:T(2,128)(2,1)S(1)}, bf16[256,2,256]{2,1,0:T(2,128)(2,1)S(1)}, u32[]{:S(2)}, u32[]{:S(2)}) %collective-permute-start.1) | collective-permute-done | bytes 262176 | tf_op jit(solution)/shard_map/ppermute | solution.py:463
  37.2 1.1 %choose.4.own_ref = bf16[256,2,256]{2,1,0:T(2,128)(2,1)S(1)} custom-call(s32[4]{0:T(128)} %owner_ref.5, bf16[256,2,256]{2,1,0:T(2,128)(2,1)S(1)} %get-tuple-element.31.refs_0_, bf16[256,2,256]{2,1,0:T(2,128)(2,1)S(1)} %collective-permute-done.1.refs_1_), custom_call_target="tpu_custom_call" | custom-call | tf_op jit(solution)/shard_map/choose/pallas_call | solution.py:245
  38.3 1.8 %collective-permute-start.2 = (bf16[256,2,256]{2,1,0:T(2,128)(2,1)S(1)}, bf16[256,2,256]{2,1,0:T(2,128)(2,1)S(1)}, u32[]{:S(2)}, u32[]{:S(2)}) collective-permute-start(bf16[256,2,256]{2,1,0:T(2,128)(2,1)S(1)} %choose.4.own_ref), channel_id=1, source_target_pairs={{0,4},{4,0},{8,12},{12,8},{1,5},{5,1},{9,13},{13,9},{2,6},{6,2},{1... | collective-permute-start | bytes 786440 | tf_op jit(solution)/shard_map/ppermute | solution.py:463
  40.1 0.0 collective-permute-done.5.got_ref
  40.1 0.5 across_products.1.refs_2_
  40.5 2.5 %collective-permute-start.10 = (f32[3,16,128]{2,1,0:T(8,128)S(1)}, f32[3,16,128]{2,1,0:T(8,128)S(1)}, u32[]{:S(2)}, u32[]{:S(2)}) collective-permute-start(f32[3,16,128]{2,1,0:T(8,128)S(1)} %across_products.1.refs_2_), channel_id=1, source_target_pairs={{4,8},{8,4},{5,9},{9,5},{6,10},{10,6},{7,11},{11,7},{20,24},{24,20... | collective-permute-start | bytes 73736 | tf_op jit(solution)/shard_map/ppermute | solution.py:469
  43.0 0.0 collective-permute-done.6.refs_0_
  43.0 0.0 collective-permute-done.7.refs_3_
  43.0 2.2 %within_products.1 = (f32[3,16,128]{2,1,0:T(8,128)S(1)}, f32[1,2,16,128]{3,2,1,0:T(8,128)S(1)}, f32[2,16,128]{2,1,0:T(8,128)S(1)}, f32[3,16,128]{2,1,0:T(8,128)S...) custom-call(bf16[2,2,256,256]{3,2,1,0:T(8,128)(2,1)S(1)} %collective-permute-done.6.refs_0_, ...), custom_call_target="tpu_custom_call" | custom-call | tf_op jit(solution)/shard_map/within_products/pallas_call | solution.py:372
  45.3 0.0 collective-permute-done.9.mate_ref
  45.3 1.0 %reference_products.3 = (f32[2,2,16,128]{3,2,1,0:T(8,128)S(1)}, f32[16,128]{1,0:T(8,128)S(1)}) custom-call(bf16[256,2,256]{2,1,0:T(2,128)(2,1)S(1)} %choose.5.own_ref, bf16[256,2,256]{2,1,0:T(2,128)(2,1)S(1)} %collective-permute-done.9.mate_ref, bf16[2,2,256,256]{3,2,1,0:T(8,128)(2,1)S(1)} %get-tuple-element.45.even_ref.refs_4_.refs_0_, ...), custom_call_target="tpu_custom_call" | custom-call | tf_op jit(solution)/shard_map/reference_products/pallas_call | solution.py:331
  46.2 0.0 collective-permute-done.2.mate_ref
  46.3 1.0 %reference_products.2 = (f32[2,2,16,128]{3,2,1,0:T(8,128)S(1)}, f32[16,128]{1,0:T(8,128)S(1)}) custom-call(bf16[256,2,256]{2,1,0:T(2,128)(2,1)S(1)} %choose.4.own_ref, bf16[256,2,256]{2,1,0:T(2,128)(2,1)S(1)} %collective-permute-done.2.mate_ref, bf16[2,2,256,256]{3,2,1,0:T(8,128)(2,1)S(1)} %get-tuple-element.41.refs_0_.first_ref.refs_1_, ...), custom_call_target="tpu_custom_call" | custom-call | tf_op jit(solution)/shard_map/reference_products/pallas_call | solution.py:331
  47.2 0.0 collective-permute-done.10.refs_8_
  47.2 0.7 %finish.1 = (f32[2,2,16,256]{3,2,1,0:T(8,128)}, f32[2,2,16,256]{3,2,1,0:T(8,128)}, f32[2,16,256]{2,1,0:T(8,128)}) custom-call(f32[2,2,16,128]{3,2,1,0:T(8,128)S(1)} %get-tuple-element.43.refs_0_, f32[16,128]{1,0:T(8,128)S(1)} %get-tuple-element.44.refs_1_, f32[3,16,128]{2,1,0:T(8,128)S(1)} %across_products.1.refs_2_, ...), custom_call_target="tpu_custom_call" | custom-call | tf_op jit(solution)/shard_map/finish/pallas_call | solution.py:451
Async XLA Ops:
  0.6 22.2 %collective-permute-start = (bf16[1,4,256,2,256]{4,3,2,1,0:T(2,128)(2,1)}, bf16[1,4,256,2,256]{4,3,2,1,0:T(2,128)(2,1)S(1)}, u32[]{:S(2)}, u32[]{:S(2)}) collective-permute-start(bf16[1,4,256,2,256]{4,3,2,1,0:T(2,128)(2,1)} %refs_0_.1), channel_id=1, source_target_pairs={{0,4},{4,0},{8,12},{12,8},{1,5},{5,1},{9,13},{13,9},{2,6},{6,2},{1... | collective-permute-start | bytes 3145736 | tf_op jit(solution)/shard_map/ppermute | solution.py:463
  4.1 5.3 %collective-permute-start.3 = (bf16[2,16,2112]{2,1,0:T(8,128)(2,1)S(1)}, bf16[2,16,2112]{2,1,0:T(8,128)(2,1)S(1)}, u32[]{:S(2)}, u32[]{:S(2)}) collective-permute-start(bf16[2,16,2112]{2,1,0:T(8,128)(2,1)S(1)} %get-tuple-element.39), channel_id=1, source_target_pairs={{0,1},{2,3},{1,0},{3,2},{4,5},{6,7},{5,4},{7,6},{8,9},{10,11},{9,8... | collective-permute-start | bytes 405512 | tf_op jit(solution)/shard_map/ppermute | solution.py:469
  5.5 6.8 %collective-permute-start.4 = (bf16[2,16,2112]{2,1,0:T(8,128)(2,1)S(1)}, bf16[2,16,2112]{2,1,0:T(8,128)(2,1)S(1)}, u32[]{:S(2)}, u32[]{:S(2)}) collective-permute-start(bf16[2,16,2112]{2,1,0:T(8,128)(2,1)S(1)} %get-tuple-element.40), channel_id=1, source_target_pairs={{1,2},{2,1},{5,6},{6,5},{9,10},{10,9},{13,14},{14,13},{17,18},{18,... | collective-permute-start | bytes 405512 | tf_op jit(solution)/shard_map/ppermute | solution.py:469
  15.4 24.6 %collective-permute-start.5 = (bf16[2,2,256,256]{3,2,1,0:T(8,128)(2,1)S(1)}, bf16[2,2,256,256]{3,2,1,0:T(8,128)(2,1)S(1)}, u32[]{:S(2)}, u32[]{:S(2)}) collective-permute-start(bf16[2,2,256,256]{3,2,1,0:T(8,128)(2,1)S(1)} %pick.1), channel_id=1, source_target_pairs={{4,8},{8,4},{5,9},{9,5},{6,10},{10,6},{7,11},{11,7},{20,24},{24,20... | collective-permute-start | bytes 1572872 | tf_op jit(solution)/shard_map/ppermute | solution.py:469
  19.6 23.4 %collective-permute-start.6 = (bf16[2,2,256,256]{3,2,1,0:T(8,128)(2,1)S(1)}, bf16[2,2,256,256]{3,2,1,0:T(8,128)(2,1)S(1)}, u32[]{:S(2)}, u32[]{:S(2)}) collective-permute-start(bf16[2,2,256,256]{3,2,1,0:T(8,128)(2,1)S(1)} %get-tuple-element.42.refs_1_.odd_ref.refs_2_), channel_id=1, source_target_pairs={{0,4},{4,0},{8,12},{12,8},{1,5},{5,1},{9,13},{13,9},{2,6},{6,2},{1... | collective-permute-start | bytes 1572872 | tf_op jit(solution)/shard_map/ppermute | solution.py:463
  24.5 7.1 %collective-permute-start.8 = (bf16[256,2,256]{2,1,0:T(2,128)(2,1)S(1)}, bf16[256,2,256]{2,1,0:T(2,128)(2,1)S(1)}, u32[]{:S(2)}, u32[]{:S(2)}) collective-permute-start(bf16[256,2,256]{2,1,0:T(2,128)(2,1)S(1)} %get-tuple-element.50.refs_0_), channel_id=1, source_target_pairs={{0,8},{4,12},{8,0},{12,4},{1,9},{5,13},{9,1},{13,5},{2,10},{6,14},... | collective-permute-start | bytes 786440 | tf_op jit(solution)/shard_map/ppermute | solution.py:463
  24.7 18.3 %collective-permute-start.7 = (bf16[2,2,256,256]{3,2,1,0:T(8,128)(2,1)S(1)}, bf16[2,2,256,256]{3,2,1,0:T(8,128)(2,1)S(1)}, u32[]{:S(2)}, u32[]{:S(2)}) collective-permute-start(bf16[2,2,256,256]{3,2,1,0:T(8,128)(2,1)S(1)} %get-tuple-element.46.last_ref.refs_5_.refs_1_), channel_id=1, source_target_pairs={{0,4},{4,0},{8,12},{12,8},{1,5},{5,1},{9,13},{13,9},{2,6},{6,2},{1... | collective-permute-start | bytes 1572872 | tf_op jit(solution)/shard_map/ppermute | solution.py:463
  25.5 11.7 %collective-permute-start.1 = (bf16[256,2,256]{2,1,0:T(2,128)(2,1)S(1)}, bf16[256,2,256]{2,1,0:T(2,128)(2,1)S(1)}, u32[]{:S(2)}, u32[]{:S(2)}) collective-permute-start(bf16[256,2,256]{2,1,0:T(2,128)(2,1)S(1)} %get-tuple-element.31.refs_0_), channel_id=1, source_target_pairs={{0,8},{4,12},{8,0},{12,4},{1,9},{5,13},{9,1},{13,5},{2,10},{6,14},... | collective-permute-start | bytes 786440 | tf_op jit(solution)/shard_map/ppermute | solution.py:463
  32.7 12.6 %collective-permute-start.9 = (bf16[256,2,256]{2,1,0:T(2,128)(2,1)S(1)}, bf16[256,2,256]{2,1,0:T(2,128)(2,1)S(1)}, u32[]{:S(2)}, u32[]{:S(2)}) collective-permute-start(bf16[256,2,256]{2,1,0:T(2,128)(2,1)S(1)} %choose.5.own_ref), channel_id=1, source_target_pairs={{0,4},{4,0},{8,12},{12,8},{1,5},{5,1},{9,13},{13,9},{2,6},{6,2},{1... | collective-permute-start | bytes 786440 | tf_op jit(solution)/shard_map/ppermute | solution.py:463
  38.3 8.0 %collective-permute-start.2 = (bf16[256,2,256]{2,1,0:T(2,128)(2,1)S(1)}, bf16[256,2,256]{2,1,0:T(2,128)(2,1)S(1)}, u32[]{:S(2)}, u32[]{:S(2)}) collective-permute-start(bf16[256,2,256]{2,1,0:T(2,128)(2,1)S(1)} %choose.4.own_ref), channel_id=1, source_target_pairs={{0,4},{4,0},{8,12},{12,8},{1,5},{5,1},{9,13},{13,9},{2,6},{6,2},{1... | collective-permute-start | bytes 786440 | tf_op jit(solution)/shard_map/ppermute | solution.py:463
  40.5 6.7 %collective-permute-start.10 = (f32[3,16,128]{2,1,0:T(8,128)S(1)}, f32[3,16,128]{2,1,0:T(8,128)S(1)}, u32[]{:S(2)}, u32[]{:S(2)}) collective-permute-start(f32[3,16,128]{2,1,0:T(8,128)S(1)} %across_products.1.refs_2_), channel_id=1, source_target_pairs={{4,8},{8,4},{5,9},{9,5},{6,10},{10,6},{7,11},{11,7},{20,24},{24,20... | collective-permute-start | bytes 73736 | tf_op jit(solution)/shard_map/ppermute | solution.py:469

commit v2 on v1

--- a/solution.py
+++ b/solution.py
@@ -9,7 +9,6 @@
 
 
 TILE = 256
-PIECE = 64
 LOOK_AZ = 4
 LOOK_RG = 16
 
@@ -117,16 +116,14 @@
     return outs[:-2], outs[-2], outs[-1]
 
 
-def range_matrix(margin, kernel_ref, index_row, offset_row, order, column, rg_ref):
+def range_matrix(margin, rows, kernel_ref, index_row, offset_row, order, column):
     taps = kernel_ref.shape[0]
     both = taps_and_offsets(kernel_ref[...], index_row, offset_row, order)
     base = column + both[taps : taps + 1].astype(jnp.int32) + (margin - 3)
-    period = 2 * taps
-    place = iota((period, order.shape[1]), 0) - base
+    place = iota((taps, order.shape[1]), 0) - base
     value = tap_pattern(both, place & (taps - 1))
-    for block in range(rg_ref.shape[0] // period):
-        home = over(place + block * period, taps)
-        rg_ref[block * period : (block + 1) * period] = jnp.where(home == 0, value, 0.0).astype(BF)
+    blocks = [jnp.where(over(place + start, taps) == 0, value, 0.0) for start in range(0, rows, taps)]
+    return jnp.concatenate(blocks, 0)
 
 
 def tap_pattern(both, which):
@@ -136,13 +133,8 @@
     return value
 
 
-def resample_kernel(
-    calls, x_ref, azk_ref, rgk_ref, rgo_ref, rgi_ref, azi_ref, azo_ref, first_ref, second_ref, *refs,
-):
-    columns = x_ref.shape[3]
-    margin = first_ref.shape[1]
-    outs, (spread_ref, band_ref, rg_ref) = refs[: len(calls)], refs[len(calls) :]
-    odd_column = lax.axis_index("range") & 1 == 1
+def azimuth_kernel(margin, x_ref, azk_ref, rgk_ref, rgo_ref, rgi_ref, azi_ref, azo_ref, z_ref, band_ref, rg_ref, spread_ref):
+    depth, _, _, columns = x_ref.shape
     taps = azk_ref.shape[0]
     tile, lanes = spread_ref.shape
     half_rows, half_lanes = tile // 2, lanes // 2
@@ -152,13 +144,13 @@
     spread_ref[...] = chosen((tile, lanes), 0, row + half_rows * over(lane, half_lanes))
     column = look_column(iota((1, columns), 1), columns)
     order = chosen((columns, columns), 0, column)
-    for k in sorted({k for k, _ in calls}):
-        range_matrix(
-            margin, rgk_ref, rgi_ref[k : k + 1], rgo_ref[k : k + 1], order, column, rg_ref.at[k]
-        )
-    for call, (k, chunk) in enumerate(calls):
-        for s in range(2):
-            start = (2 * chunk + s) * tile
+    for k in range(depth):
+        rg_ref[k] = range_matrix(
+            margin, columns + 2 * margin, rgk_ref, rgi_ref[k : k + 1], rgo_ref[k : k + 1], order, column
+        ).astype(BF)
+    for k in range(depth):
+        for s in range(z_ref.shape[1]):
+            start = s * tile
             rows = slice(start, start + tile)
             both = taps_and_offsets(
                 azk_ref[...], azi_ref[k : k + 1, rows], azo_ref[k : k + 1, rows], spread_ref[...]
@@ -170,7 +162,7 @@
             home = -over(place, taps)
             for half in range(2):
                 mine = slice(half * half_lanes, (half + 1) * half_lanes)
-                band = band_ref.at[call % 2, s, half]
+                band = band_ref.at[k, s, half]
                 for block in range(band.shape[0] // period):
                     band[block * period : (block + 1) * period] = jnp.where(
                         home[:, mine] == block, value[:, mine], 0.0
@@ -178,36 +170,60 @@
                 begin = start + half * half_rows
                 size = half_rows + 2 * margin
                 window = x_ref[k, begin : begin + size].reshape(2 * size, columns)
-                across = slice(2 * begin, 2 * (begin + size))
+                z_ref[k, s, half] = dot(window, band[...], OVER_ROWS).astype(BF)
+
+
+def azimuth(operands, margin):
+    depth, rows, parts, columns = operands[0].shape
+    steps = (rows - 2 * margin) // TILE
+    lanes = parts * TILE // 2
+    shapes = [
+        (depth, steps, 2, columns, lanes),
+        (depth, steps, 2, parts * (TILE // 2 + 2 * margin), lanes),
+        (depth, columns + 2 * margin, columns),
+    ]
+    return pl.pallas_call(
+        partial(azimuth_kernel, margin),
+        in_specs=[VMEM] * len(operands),
+        out_specs=[VMEM] * len(shapes),
+        out_shape=[pltpu.VMEM(shape, BF) for shape in shapes],
+        scratch_shapes=[pltpu.VMEM((TILE, parts * TILE), BF)],
+        compiler_params=SMALL,
+        name="azimuth",
+    )(*resident(*operands))
+
+
+def range_kernel(calls, z_ref, band_ref, rg_ref, first_ref, second_ref, *outs):
+    odd_column = lax.axis_index("range") & 1 == 1
+    half_rows = z_ref.shape[4] // 2
+    for out, (k, chunk) in zip(outs, calls):
+        for s in range(2):
+            for half in range(2):
+                at = (k, 2 * chunk + s, half)
+                begin = 2 * (2 * (2 * chunk + s) + half) * half_rows
+                across = slice(begin, begin + band_ref.shape[3])
                 first_side, second_side = first_ref[k, :, across], second_ref[k, :, across]
                 wide = jnp.concatenate(
                     [
-                        dot(jnp.where(odd_column, first_side, second_side), band[...]).astype(BF),
-                        dot(window, band[...], OVER_ROWS).astype(BF),
-                        dot(jnp.where(odd_column, second_side, first_side), band[...]).astype(BF),
+                        dot(jnp.where(odd_column, first_side, second_side), band_ref[at]).astype(BF),
+                        z_ref[at],
+                        dot(jnp.where(odd_column, second_side, first_side), band_ref[at]).astype(BF),
                     ],
                     0,
                 )
-                outs[call][s, half] = dot(rg_ref[k], wide, OVER_ROWS).astype(BF)
-
-
-def resample(operands, first, second, calls):
-    depth, _, parts, columns = operands[0].shape
-    margin = first.shape[1]
-    lanes = parts * TILE
-    arrays = resident(*operands, first, second)
+                out[s, half] = dot(rg_ref[k], wide, OVER_ROWS).astype(BF)
+
+
+def range_resample(azimuth_outs, first, second, calls):
+    _, _, _, columns, lanes = azimuth_outs[0].shape
+    arrays = resident(*azimuth_outs, first, second)
     return pl.pallas_call(
-        partial(resample_kernel, calls),
+        partial(range_kernel, calls),
         in_specs=[VMEM] * len(arrays),
         out_specs=[VMEM] * len(calls),
-        out_shape=[pltpu.VMEM((2, 2, columns, lanes // 2), BF)] * len(calls),
-        scratch_shapes=[
-            pltpu.VMEM((TILE, lanes), BF),
-            pltpu.VMEM((2, 2, 2, parts * (TILE // 2 + 2 * margin), lanes // 2), BF),
-            pltpu.VMEM((depth, columns + 2 * margin, columns), BF),
-        ],
-        compiler_params=SMALL,
-        name="resample",
+        out_shape=[pltpu.VMEM((2, 2, columns, lanes), BF)] * len(calls),
+        compiler_params=SMALL,
+        name="range_resample",
     )(*arrays)
 
 
@@ -219,67 +235,55 @@
         tile = 2 * (first + n) + (me & 1)
         here, there = [ref.at[0, tile] if stored else ref for ref in sources]
         same = ((owner_ref[tile] ^ me) >> bit) & 1 == 0
-        pieces = [pl.ds(m * PIECE, PIECE) for m in range(out.shape[0] // PIECE)]
-        from_here, from_there = [
-            [pltpu.make_async_copy(source.at[p], out.at[p], sems.at[n, m]) for m, p in enumerate(pieces)]
-            for source in (here, there)
-        ]
-
-        @pl.when(same)
-        def _():
-            for copy in from_here:
-                copy.start()
-
-        @pl.when(jnp.logical_not(same))
-        def _():
-            for copy in from_there:
-                copy.start()
-
-        copies += from_here
+        copies.append(pltpu.make_async_copy(here, out, sems.at[n]))
+        pl.when(same)(copies[n].start)
+        pl.when(jnp.logical_not(same))(pltpu.make_async_copy(there, out, sems.at[n]).start)
     for copy in copies:
         copy.wait()
 
 
 def choose(owner, here, there, first, bit, chunks):
-    anywhere = pl.BlockSpec(memory_space=pl.ANY)
     return pl.pallas_call(
         partial(choose_kernel, first, bit, here.ndim > 3),
-        in_specs=[SMEM, anywhere, anywhere],
+        in_specs=[SMEM, VMEM, VMEM],
         out_specs=[VMEM] * chunks,
         out_shape=[pltpu.VMEM(here.shape[-3:], BF)] * chunks,
-        scratch_shapes=[pltpu.SemaphoreType.DMA((chunks, here.shape[-3] // PIECE))],
+        scratch_shapes=[pltpu.SemaphoreType.DMA((chunks,))],
         compiler_params=SMALL,
         name="choose",
-    )(owner, here, there)
-
-
-def halves(block):
-    width = block.shape[1] // 2
-    wide = block.astype(F32)
+    )(owner, *resident(here, there))
+
+
+def lines(ref, look):
+    blocks, width = ref.shape[0] // LOOK_RG, ref.shape[1] // 2
+    wide = ref[look * blocks : (look + 1) * blocks].astype(F32)
     return wide[:, :width], wide[:, width:]
 
 
-def looks(value):
-    blocks = value.shape[0] // LOOK_RG
-    total = value[:blocks]
-    for look in range(1, LOOK_RG):
-        total = total + value[look * blocks : (look + 1) * blocks]
-    shift = value.shape[1] // 2
-    while shift >= value.shape[1] // LOOK_AZ:
-        total = total + pltpu.roll(total, shift, 1)
-        shift //= 2
-    return total * (1.0 / (LOOK_AZ * LOOK_RG))
+def multilook(terms, *refs):
+    totals = None
+    for look in range(LOOK_RG):
+        found = terms(*[lines(ref, look) for ref in refs])
+        totals = found if totals is None else [a + b for a, b in zip(totals, found)]
+    means = []
+    for total in totals:
+        shift = total.shape[1] // 2
+        while shift >= total.shape[1] // LOOK_AZ:
+            total = total + pltpu.roll(total, shift, 1)
+            shift //= 2
+        means.append(total * (1.0 / (LOOK_AZ * LOOK_RG)))
+    return means
 
 
 def pair(first, second):
     a_re, a_im = first
     b_re, b_im = second
-    return looks(a_re * b_re + a_im * b_im), looks(a_im * b_re - a_re * b_im)
+    return [a_re * b_re + a_im * b_im, a_im * b_re - a_re * b_im]
 
 
 def power(first):
     re, im = first
-    return looks(re * re + im * im)
+    return [re * re + im * im]
 
 
 def joined(pieces):
@@ -291,37 +295,35 @@
     return total
 
 
-def pairs_of(leads, followers):
-    found = [pair(a, b) for a, b in zip(leads, followers)]
-    return joined([re for re, _ in found]), joined([im for _, im in found])
+def gathered(units):
+    return [joined(list(pieces)) for pieces in zip(*units)]
 
 
 def reference_kernel(own_ref, mate_ref, *refs):
-    depth = len(refs) - 2
-    cur_refs, (pair_ref, pow_ref) = refs[:depth], refs[depth:]
+    depth = len(refs) - 3
+    cur_refs, (pair_ref, pow_ref, lead_ref) = refs[:depth], refs[depth:]
     columns, half_rows = own_ref.shape[2], own_ref.shape[0] // 2
     core = lax.axis_index("scene") & 1
     size = 2 * half_rows
     row, part = lane_row(iota((1, size), 1), half_rows)
     order = chosen((size, size), 0, 2 * row + part)
     turn = chosen((columns, columns), 1, look_column(iota((columns, 1), 0), columns))
-    powers, pairs = [], [[] for _ in range(depth)]
-    for ref, place in ((own_ref, core), (mate_ref, 1 - core)):
+
+    def terms(lead, *currents):
+        return power(lead) + [a for current in currents for a in pair(lead, current)]
+
+    units = []
+    for n, (ref, place) in enumerate(((own_ref, core), (mate_ref, 1 - core))):
         for half in range(2):
             rows = ref[half * half_rows : (half + 1) * half_rows].reshape(size, columns)
-            lead = dot(turn, dot(rows, order, OVER_ROWS).astype(BF))
-            lead = lead[:, :half_rows], lead[:, half_rows:]
-            powers.append(power(lead))
-            for k in range(depth):
-                pairs[k].append(pair(lead, halves(cur_refs[k][place, half])))
-
-    def in_order(pieces):
-        return joined([jnp.where(core == 0, pieces[n], pieces[(n + 2) % 4]) for n in range(4)])
-
-    pow_ref[...] = in_order(powers)
-    for k in range(depth):
-        pair_ref[k, 0] = in_order([re for re, _ in pairs[k]])
-        pair_ref[k, 1] = in_order([im for _, im in pairs[k]])
+            lead_ref[2 * n + half] = dot(turn, dot(rows, order, OVER_ROWS).astype(BF)).astype(BF)
+            units.append(
+                multilook(terms, lead_ref.at[2 * n + half], *[ref.at[place, half] for ref in cur_refs])
+            )
+    units = [[jnp.where(core == 0, a, b) for a, b in zip(units[n], units[(n + 2) % 4])] for n in range(4)]
+    pow_ref[...], *pairs = gathered(units)
+    for n, found in enumerate(pairs):
+        pair_ref[n // 2, n % 2] = found
 
 
 def reference_products(own, mate, currents):
@@ -333,34 +335,34 @@
         in_specs=[VMEM] * (2 + depth),
         out_specs=[VMEM] * len(shapes),
         out_shape=[pltpu.VMEM(shape, F32) for shape in shapes],
+        scratch_shapes=[pltpu.VMEM((4, columns, width), BF)],
         compiler_params=SMALL,
         name="reference_products",
     )(*resident(own, mate, *currents))
 
 
-def write_products(out, leads, followers):
-    leads, followers = [[halves(a) for a in units] for units in (leads, followers)]
-    out[0], out[1] = pairs_of(leads, followers)
-    out[2] = joined([power(a) for a in leads])
-
-
 def units_of(ref):
-    return [ref[n // 2, n % 2] for n in range(4)]
+    return [ref.at[n // 2, n % 2] for n in range(4)]
 
 
 def within_kernel(depth, *refs):
     chunks = len(refs) // (depth + 4)
+
+    def terms(*rows):
+        return [a for row in rows for a in power(row)] + [
+            a for k in range(len(rows) - 1) for a in pair(rows[k], rows[k + 1])
+        ]
+
     for n in range(chunks):
-        got_ref, *cur_refs = refs[n * (depth + 1) : (n + 1) * (depth + 1)]
+        sources = refs[n * (depth + 1) : (n + 1) * (depth + 1)]
         lead_ref, seq_ref, pow_ref = refs[chunks * (depth + 1) + 3 * n :][:3]
-        write_products(lead_ref, units_of(got_ref), units_of(cur_refs[0]))
-        before = None
-        for k, ref in enumerate(cur_refs):
-            now = [halves(a) for a in units_of(ref)]
-            pow_ref[k] = joined([power(a) for a in now])
-            if k:
-                seq_ref[k - 1, 0], seq_ref[k - 1, 1] = pairs_of(before, now)
-            before = now
+        units = [multilook(terms, *unit) for unit in zip(*map(units_of, sources))]
+        lead_ref[2], *found = gathered(units)
+        for k in range(depth):
+            pow_ref[k] = found[k]
+        lead_ref[0], lead_ref[1], *pairs = found[depth:]
+        for m, a in enumerate(pairs):
+            seq_ref[m // 2, m % 2] = a
 
 
 def within_products(got, currents):
@@ -381,13 +383,16 @@
 
 
 def across_kernel(got_ref, first_ref, last_ref, out_ref):
-    @pl.when(lax.axis_index("scene") & 1 == 1)
-    def _():
-        write_products(out_ref, units_of(last_ref), units_of(got_ref))
-
-    @pl.when(lax.axis_index("scene") & 1 == 0)
-    def _():
-        write_products(out_ref, units_of(got_ref), units_of(first_ref))
+    def products(leads, followers):
+        units = [
+            multilook(lambda a, b: pair(a, b) + power(a), *unit)
+            for unit in zip(units_of(leads), units_of(followers))
+        ]
+        out_ref[0], out_ref[1], out_ref[2] = gathered(units)
+
+    odd = lax.axis_index("scene") & 1 == 1
+    pl.when(odd)(lambda: products(last_ref, got_ref))
+    pl.when(jnp.logical_not(odd))(lambda: products(got_ref, first_ref))
 
 
 def across_products(got, first, last):
@@ -463,9 +468,9 @@
     return lax.ppermute(block, axis, [(i, i ^ (1 << bit)) for i in range(lax.axis_size(axis))])
 
 
-def neighbours(block, axis, first):
+def neighbours(block, axis, first, around=False):
     count = lax.axis_size(axis)
-    pairs = [(i, i + 1) for i in range(first, count - 1, 2)]
+    pairs = [(i, (i + 1) % count) for i in range(first, count - 1 + around, 2)]
     return lax.ppermute(block, axis, pairs + [(j, i) for i, j in pairs])
 
 
@@ -486,30 +491,33 @@
 
     arrived = swapped(reference_store, "scene", 0)
     operands, first, second = load(
-        secondary, az_kernel.T, rg_kernel.T, rg_offset, rg_index, az_index, az_offset
+        secondary, reference_store, az_kernel.T, rg_kernel.T, rg_offset, rg_index, az_index, az_offset
     )
-    first = neighbours(first, "range", 0)
-    second = neighbours(second, "range", 1)
-    stored, owner = (pltpu.with_memory_space_constraint(a, pltpu.HBM) for a in (reference_store, tile_owner))
+    secondary, stored, *tables = operands
+    operands = (secondary, *tables)
+    owner = pltpu.with_memory_space_constraint(tile_owner, pltpu.HBM)
     held = list(choose(owner, stored, arrived, 0, 0, chunks))
     for bit in range(1, bits):
         for n in range(chunks):
             got = swapped(held[n], "scene", bit)
             held[n] = choose(owner, held[n], got, n, bit, 1)[0]
+    turned = azimuth(operands, first.shape[1])
+    first = neighbours(first, "range", 0)
+    second = neighbours(second, "range", 1)
     last = depth - 1
     early, late = [(last, 0), (0, 1)], [(k, n) for n in range(2) for k in range(depth)]
     late = [call for call in late if call not in early]
-    units = dict(zip(early, resample(operands, first, second, early)))
+    units = dict(zip(early, range_resample(turned, first, second, early)))
     across = pick(units[last, 0], units[0, 1])
     across = neighbours(across, "scene", 1)
-    units.update(zip(late, resample(operands, first, second, late)))
+    units.update(zip(late, range_resample(turned, first, second, late)))
     currents = [[units[k, n] for k in range(depth)] for n in range(2)]
     within = []
     for n in range(2):
         within.append(swapped(currents[n][last], "scene", 0))
     within = within_products(within, currents)
     across = across_products(across, currents[0][0], currents[1][last])
-    returned = neighbours(across, "scene", 1)
+    returned = neighbours(across, "scene", 1, True)
     results = []
     for n, small in enumerate(within):
         mate = swapped(held[n], "scene", 0)

time: 48.2 us -> 44 us (0.913)
  the two profiles are of different devices: /device:TPU:17 before, /device:TPU:9 now
where the time goes in v2:
time: 44 us; the launch traced here: 43.8 us
  Pallas kernels  17.2 us (39%)
  starting transfers between devices  14.8 us (34%)
  waiting for transfers between devices  11 us (25%)
  between operations  0.79 us (2%)
    ppermute x7, waiting for transfers between devices, swapped(): lax.ppermute(block, axis, [(i, i ^ 1 << bit) for i in range(lax.axis_size...  11 us
    ppermute x4, starting transfers between devices, neighbours(): return lax.ppermute(block, axis, pairs + [(j, i) for i, j in pairs])  9.05 us
    ppermute x7, starting transfers between devices, swapped(): lax.ppermute(block, axis, [(i, i ^ 1 << bit) for i in range(lax.axis_size...  5.73 us
    pallas_call x1, Pallas kernels, azimuth(): pl.pallas_call(partial(azimuth_kernel, margin), in_specs=[VMEM] * len(ope...  4.17 us
    pallas_call x2, Pallas kernels, range_resample(): pl.pallas_call(partial(range_kernel, calls), in_specs=[VMEM] * len(arrays...  2.78 us
    pallas_call x1, Pallas kernels, load(): pl.pallas_call(partial(load_kernel, margin), in_specs=[anywhere] * len(op...  2.76 us
    pallas_call x3, Pallas kernels, choose(): pl.pallas_call(partial(choose_kernel, first, bit, here.ndim > 3), in_spec...  2.18 us
    pallas_call x1, Pallas kernels, within_products(): pl.pallas_call(partial(within_kernel, depth), in_specs=[VMEM] * len(array...  2.1 us
  transfers between devices with their start and end apart: 11, of which 2 were waited for; matrix products, arithmetic and copies ran while one was open for 0% of the time, Pallas kernels for 38%

profile of v2, /device:TPU:9, one launch (start us, length us, event | category | flops | bytes accessed | tf_op | source)
XLA Modules:
  0.0 43.8 jit_solution(16573508364919984964)
XLA Ops:
  0.6 0.7 %collective-permute-start = (bf16[1,4,256,2,256]{4,3,2,1,0:T(2,128)(2,1)}, bf16[1,4,256,2,256]{4,3,2,1,0:T(2,128)(2,1)S(1)}, u32[]{:S(2)}, u32[]{:S(2)}) collective-permute-start(bf16[1,4,256,2,256]{4,3,2,1,0:T(2,128)(2,1)} %refs_0_.1), channel_id=1, source_target_pairs={{0,4},{4,0},{8,12},{12,8},{1,5},{5,1},{9,13},{13,9},{2,6},{6,2},{1... | collective-permute-start | bytes 3145736 | tf_op jit(solution)/shard_map/ppermute | solution.py:468
  1.4 2.8 %load.1 = (bf16[2,1056,2,256]{3,2,1,0:T(2,128)(2,1)S(1)}, bf16[1,4,256,2,256]{4,3,2,1,0:T(2,128)(2,1)S(1)}, f32[8,64]{1,0:T(8,128)S(1)}, f32[8,64]{1,0:T(8,128)S...) custom-call(bf16[2,1056,2,256]{3,2,1,0:T(2,128)(2,1)} %x_ref.1, ...), custom_call_target="tpu_custom_call" | custom-call | tf_op jit(solution)/shard_map/load/pallas_call | solution.py:107
  4.1 0.1 collective-permute-start.3
  4.2 4.5 %collective-permute-start.4 = (bf16[2,16,2112]{2,1,0:T(8,128)(2,1)S(1)}, bf16[2,16,2112]{2,1,0:T(8,128)(2,1)S(1)}, u32[]{:S(2)}, u32[]{:S(2)}) collective-permute-start(bf16[2,16,2112]{2,1,0:T(8,128)(2,1)S(1)} %get-tuple-element.48), channel_id=1, source_target_pairs={{1,2},{2,1},{5,6},{6,5},{9,10},{10,9},{13,14},{14,13},{17,18},{18,... | collective-permute-start | bytes 405512 | tf_op jit(solution)/shard_map/ppermute | solution.py:474
  8.7 4.2 %azimuth.1 = (bf16[2,4,2,256,256]{4,3,2,1,0:T(8,128)(2,1)S(1)}, bf16[2,4,2,320,256]{4,3,2,1,0:T(8,128)(2,1)S(1)}, bf16[2,288,256]{2,1,0:T(8,128)(2,1)S(1)}) custom-call(bf16[2,1056,2,256]{3,2,1,0:T(2,128)(2,1)S(1)} %get-tuple-element.37.x_ref, f32[8,64]{1,0:T(8,128)S(1)} %get-tuple-element.38.azk_ref, f32[8,64]{1,0:T(8,128)S(1)} %get-tuple-element.39.rgk_ref, ...), custom_call_target="tpu_custom_call" | custom-call | tf_op jit(solution)/shard_map/azimuth/pallas_call | solution.py:185
  12.9 0.0 collective-permute-done.3.first_ref
  12.9 0.0 collective-permute-done.4.second_ref
  12.9 1.4 %range_resample.3 = (bf16[2,2,256,256]{3,2,1,0:T(8,128)(2,1)S(1)}, bf16[2,2,256,256]{3,2,1,0:T(8,128)(2,1)S(1)}) custom-call(bf16[2,4,2,256,256]{4,3,2,1,0:T(8,128)(2,1)S(1)} %get-tuple-element.44.z_ref, bf16[2,4,2,320,256]{4,3,2,1,0:T(8,128)(2,1)S(1)} %get-tuple-element.45.band_ref, bf16[2,288,256]{2,1,0:T(8,128)(2,1)S(1)} %get-tuple-element.46.rg_ref, ...), custom_call_target="tpu_custom_call" | custom-call | tf_op jit(solution)/shard_map/range_resample/pallas_call | solution.py:220
  14.3 0.1 pick.1
  14.4 3.6 %collective-permute-start.5 = (bf16[2,2,256,256]{3,2,1,0:T(8,128)(2,1)S(1)}, bf16[2,2,256,256]{3,2,1,0:T(8,128)(2,1)S(1)}, u32[]{:S(2)}, u32[]{:S(2)}) collective-permute-start(bf16[2,2,256,256]{3,2,1,0:T(8,128)(2,1)S(1)} %pick.1), channel_id=1, source_target_pairs={{4,8},{8,4},{5,9},{9,5},{6,10},{10,6},{7,11},{11,7},{20,24},{24,20... | collective-permute-start | bytes 1572872 | tf_op jit(solution)/shard_map/ppermute | solution.py:474
  18.0 0.1 collective-permute-start.6
  18.1 1.4 %range_resample.2 = (bf16[2,2,256,256]{3,2,1,0:T(8,128)(2,1)S(1)}, bf16[2,2,256,256]{3,2,1,0:T(8,128)(2,1)S(1)}) custom-call(bf16[2,4,2,256,256]{4,3,2,1,0:T(8,128)(2,1)S(1)} %get-tuple-element.44.z_ref, bf16[2,4,2,320,256]{4,3,2,1,0:T(8,128)(2,1)S(1)} %get-tuple-element.45.band_ref, bf16[2,288,256]{2,1,0:T(8,128)(2,1)S(1)} %get-tuple-element.46.rg_ref, ...), custom_call_target="tpu_custom_call" | custom-call | tf_op jit(solution)/shard_map/range_resample/pallas_call | solution.py:220
  19.5 0.0 collective-permute-done.refs_1_
  19.5 0.8 %choose.3 = (bf16[256,2,256]{2,1,0:T(2,128)(2,1)S(1)}, bf16[256,2,256]{2,1,0:T(2,128)(2,1)S(1)}) custom-call(s32[4]{0:T(128)} %owner_ref.5, bf16[1,4,256,2,256]{4,3,2,1,0:T(2,128)(2,1)S(1)} %get-tuple-element.35.refs_0_, bf16[1,4,256,2,256]{4,3,2,1,0:T(2,128)(2,1)S(1)} %collective-permute-done.refs_1_), custom_call_target="tpu_custom_call" | custom-call | tf_op jit(solution)/shard_map/choose/pallas_call | solution.py:246
  20.2 0.2 collective-permute-start.1
  20.4 0.4 collective-permute-start.7
  20.9 1.7 %collective-permute-start.8 = (bf16[256,2,256]{2,1,0:T(2,128)(2,1)S(1)}, bf16[256,2,256]{2,1,0:T(2,128)(2,1)S(1)}, u32[]{:S(2)}, u32[]{:S(2)}) collective-permute-start(bf16[256,2,256]{2,1,0:T(2,128)(2,1)S(1)} %get-tuple-element.58.refs_0_), channel_id=1, source_target_pairs={{0,8},{4,12},{8,0},{12,4},{1,9},{5,13},{9,1},{13,5},{2,10},{6,14},... | collective-permute-start | bytes 786440 | tf_op jit(solution)/shard_map/ppermute | solution.py:468
  22.5 9.8 %collective-permute-done.1.refs_1_ = bf16[256,2,256]{2,1,0:T(2,128)(2,1)S(1)} collective-permute-done((bf16[256,2,256]{2,1,0:T(2,128)(2,1)S(1)}, bf16[256,2,256]{2,1,0:T(2,128)(2,1)S(1)}, u32[]{:S(2)}, u32[]{:S(2)}) %collective-permute-start.1) | collective-permute-done | bytes 262176 | tf_op jit(solution)/shard_map/ppermute | solution.py:468
  32.3 0.7 %choose.4.own_ref = bf16[256,2,256]{2,1,0:T(2,128)(2,1)S(1)} custom-call(s32[4]{0:T(128)} %owner_ref.5, bf16[256,2,256]{2,1,0:T(2,128)(2,1)S(1)} %get-tuple-element.36.refs_0_, bf16[256,2,256]{2,1,0:T(2,128)(2,1)S(1)} %collective-permute-done.1.refs_1_), custom_call_target="tpu_custom_call" | custom-call | tf_op jit(solution)/shard_map/choose/pallas_call | solution.py:246
  33.0 1.1 %collective-permute-start.2 = (bf16[256,2,256]{2,1,0:T(2,128)(2,1)S(1)}, bf16[256,2,256]{2,1,0:T(2,128)(2,1)S(1)}, u32[]{:S(2)}, u32[]{:S(2)}) collective-permute-start(bf16[256,2,256]{2,1,0:T(2,128)(2,1)S(1)} %choose.4.own_ref), channel_id=1, source_target_pairs={{0,4},{4,0},{8,12},{12,8},{1,5},{5,1},{9,13},{13,9},{2,6},{6,2},{1... | collective-permute-start | bytes 786440 | tf_op jit(solution)/shard_map/ppermute | solution.py:468
  34.1 1.2 %collective-permute-done.8.refs_1_ = bf16[256,2,256]{2,1,0:T(2,128)(2,1)S(1)} collective-permute-done((bf16[256,2,256]{2,1,0:T(2,128)(2,1)S(1)}, bf16[256,2,256]{2,1,0:T(2,128)(2,1)S(1)}, u32[]{:S(2)}, u32[]{:S(2)}) %collective-permute-start.8) | collective-permute-done | bytes 262176 | tf_op jit(solution)/shard_map/ppermute | solution.py:468
  35.3 0.7 %choose.5.own_ref = bf16[256,2,256]{2,1,0:T(2,128)(2,1)S(1)} custom-call(s32[4]{0:T(128)} %owner_ref.5, bf16[256,2,256]{2,1,0:T(2,128)(2,1)S(1)} %get-tuple-element.58.refs_0_, bf16[256,2,256]{2,1,0:T(2,128)(2,1)S(1)} %collective-permute-done.8.refs_1_), custom_call_target="tpu_custom_call" | custom-call | tf_op jit(solution)/shard_map/choose/pallas_call | solution.py:246
  36.0 1.5 %collective-permute-start.9 = (bf16[256,2,256]{2,1,0:T(2,128)(2,1)S(1)}, bf16[256,2,256]{2,1,0:T(2,128)(2,1)S(1)}, u32[]{:S(2)}, u32[]{:S(2)}) collective-permute-start(bf16[256,2,256]{2,1,0:T(2,128)(2,1)S(1)} %choose.5.own_ref), channel_id=1, source_target_pairs={{0,4},{4,0},{8,12},{12,8},{1,5},{5,1},{9,13},{13,9},{2,6},{6,2},{1... | collective-permute-start | bytes 786440 | tf_op jit(solution)/shard_map/ppermute | solution.py:468
  37.6 0.0 collective-permute-done.5.got_ref
  37.6 0.4 %across_products.1.refs_2_ = f32[3,16,128]{2,1,0:T(8,128)S(1)} custom-call(bf16[2,2,256,256]{3,2,1,0:T(8,128)(2,1)S(1)} %collective-permute-done.5.got_ref, bf16[2,2,256,256]{3,2,1,0:T(8,128)(2,1)S(1)} %get-tuple-element.49.refs_0_.first_ref.refs_1_, bf16[2,2,256,256]{3,2,1,0:T(8,128)(2,1)S(1)} %get-tuple-element.54.last_ref.refs_5_.refs_1_), custom_call_target="tpu_custom_call" | custom-call | tf_op jit(solution)/shard_map/across_products/pallas_call | solution.py:400
  38.0 0.9 %collective-permute-start.10 = (f32[3,16,128]{2,1,0:T(8,128)S(1)}, f32[3,16,128]{2,1,0:T(8,128)S(1)}, u32[]{:S(2)}, u32[]{:S(2)}) collective-permute-start(f32[3,16,128]{2,1,0:T(8,128)S(1)} %across_products.1.refs_2_), channel_id=1, source_target_pairs={{4,8},{12,0},{8,4},{0,12},{5,9},{13,1},{9,5},{1,13},{6,10},{14,2},... | collective-permute-start | bytes 73736 | tf_op jit(solution)/shard_map/ppermute | solution.py:474
  38.9 0.0 collective-permute-done.6.refs_0_
  38.9 0.0 collective-permute-done.7.refs_3_
  38.9 2.1 %within_products.1 = (f32[3,16,128]{2,1,0:T(8,128)S(1)}, f32[1,2,16,128]{3,2,1,0:T(8,128)S(1)}, f32[2,16,128]{2,1,0:T(8,128)S(1)}, f32[3,16,128]{2,1,0:T(8,128)S...) custom-call(bf16[2,2,256,256]{3,2,1,0:T(8,128)(2,1)S(1)} %collective-permute-done.6.refs_0_, ...), custom_call_target="tpu_custom_call" | custom-call | tf_op jit(solution)/shard_map/within_products/pallas_call | solution.py:374
  41.0 0.0 collective-permute-done.2.mate_ref
  41.0 1.0 %reference_products.2 = (f32[2,2,16,128]{3,2,1,0:T(8,128)S(1)}, f32[16,128]{1,0:T(8,128)S(1)}) custom-call(bf16[256,2,256]{2,1,0:T(2,128)(2,1)S(1)} %choose.4.own_ref, bf16[256,2,256]{2,1,0:T(2,128)(2,1)S(1)} %collective-permute-done.2.mate_ref, bf16[2,2,256,256]{3,2,1,0:T(8,128)(2,1)S(1)} %get-tuple-element.49.refs_0_.first_ref.refs_1_, ...), custom_call_target="tpu_custom_call" | custom-call | tf_op jit(solution)/shard_map/reference_products/pallas_call | solution.py:333
  42.1 0.0 collective-permute-done.9.mate_ref
  42.1 1.0 %reference_products.3 = (f32[2,2,16,128]{3,2,1,0:T(8,128)S(1)}, f32[16,128]{1,0:T(8,128)S(1)}) custom-call(bf16[256,2,256]{2,1,0:T(2,128)(2,1)S(1)} %choose.5.own_ref, bf16[256,2,256]{2,1,0:T(2,128)(2,1)S(1)} %collective-permute-done.9.mate_ref, bf16[2,2,256,256]{3,2,1,0:T(8,128)(2,1)S(1)} %get-tuple-element.53.even_ref.refs_4_.refs_0_, ...), custom_call_target="tpu_custom_call" | custom-call | tf_op jit(solution)/shard_map/reference_products/pallas_call | solution.py:333
  43.1 0.0 collective-permute-done.10.refs_8_
  43.1 0.7 %finish.1 = (f32[2,2,16,256]{3,2,1,0:T(8,128)}, f32[2,2,16,256]{3,2,1,0:T(8,128)}, f32[2,16,256]{2,1,0:T(8,128)}) custom-call(f32[2,2,16,128]{3,2,1,0:T(8,128)S(1)} %get-tuple-element.51.refs_0_, f32[16,128]{1,0:T(8,128)S(1)} %get-tuple-element.52.refs_1_, f32[3,16,128]{2,1,0:T(8,128)S(1)} %across_products.1.refs_2_, ...), custom_call_target="tpu_custom_call" | custom-call | tf_op jit(solution)/shard_map/finish/pallas_call | solution.py:456
Async XLA Ops:
  0.6 18.8 %collective-permute-start = (bf16[1,4,256,2,256]{4,3,2,1,0:T(2,128)(2,1)}, bf16[1,4,256,2,256]{4,3,2,1,0:T(2,128)(2,1)S(1)}, u32[]{:S(2)}, u32[]{:S(2)}) collective-permute-start(bf16[1,4,256,2,256]{4,3,2,1,0:T(2,128)(2,1)} %refs_0_.1), channel_id=1, source_target_pairs={{0,4},{4,0},{8,12},{12,8},{1,5},{5,1},{9,13},{13,9},{2,6},{6,2},{1... | collective-permute-start | bytes 3145736 | tf_op jit(solution)/shard_map/ppermute | solution.py:468
  4.1 8.7 %collective-permute-start.3 = (bf16[2,16,2112]{2,1,0:T(8,128)(2,1)S(1)}, bf16[2,16,2112]{2,1,0:T(8,128)(2,1)S(1)}, u32[]{:S(2)}, u32[]{:S(2)}) collective-permute-start(bf16[2,16,2112]{2,1,0:T(8,128)(2,1)S(1)} %get-tuple-element.47), channel_id=1, source_target_pairs={{0,1},{2,3},{1,0},{3,2},{4,5},{6,7},{5,4},{7,6},{8,9},{10,11},{9,8... | collective-permute-start | bytes 405512 | tf_op jit(solution)/shard_map/ppermute | solution.py:474
  4.2 8.7 %collective-permute-start.4 = (bf16[2,16,2112]{2,1,0:T(8,128)(2,1)S(1)}, bf16[2,16,2112]{2,1,0:T(8,128)(2,1)S(1)}, u32[]{:S(2)}, u32[]{:S(2)}) collective-permute-start(bf16[2,16,2112]{2,1,0:T(8,128)(2,1)S(1)} %get-tuple-element.48), channel_id=1, source_target_pairs={{1,2},{2,1},{5,6},{6,5},{9,10},{10,9},{13,14},{14,13},{17,18},{18,... | collective-permute-start | bytes 405512 | tf_op jit(solution)/shard_map/ppermute | solution.py:474
  14.4 23.2 %collective-permute-start.5 = (bf16[2,2,256,256]{3,2,1,0:T(8,128)(2,1)S(1)}, bf16[2,2,256,256]{3,2,1,0:T(8,128)(2,1)S(1)}, u32[]{:S(2)}, u32[]{:S(2)}) collective-permute-start(bf16[2,2,256,256]{3,2,1,0:T(8,128)(2,1)S(1)} %pick.1), channel_id=1, source_target_pairs={{4,8},{8,4},{5,9},{9,5},{6,10},{10,6},{7,11},{11,7},{20,24},{24,20... | collective-permute-start | bytes 1572872 | tf_op jit(solution)/shard_map/ppermute | solution.py:474
  18.0 20.9 %collective-permute-start.6 = (bf16[2,2,256,256]{3,2,1,0:T(8,128)(2,1)S(1)}, bf16[2,2,256,256]{3,2,1,0:T(8,128)(2,1)S(1)}, u32[]{:S(2)}, u32[]{:S(2)}) collective-permute-start(bf16[2,2,256,256]{3,2,1,0:T(8,128)(2,1)S(1)} %get-tuple-element.50.refs_1_.odd_ref.refs_2_), channel_id=1, source_target_pairs={{0,4},{4,0},{8,12},{12,8},{1,5},{5,1},{9,13},{13,9},{2,6},{6,2},{1... | collective-permute-start | bytes 1572872 | tf_op jit(solution)/shard_map/ppermute | solution.py:468
  20.2 12.1 %collective-permute-start.1 = (bf16[256,2,256]{2,1,0:T(2,128)(2,1)S(1)}, bf16[256,2,256]{2,1,0:T(2,128)(2,1)S(1)}, u32[]{:S(2)}, u32[]{:S(2)}) collective-permute-start(bf16[256,2,256]{2,1,0:T(2,128)(2,1)S(1)} %get-tuple-element.36.refs_0_), channel_id=1, source_target_pairs={{0,8},{4,12},{8,0},{12,4},{1,9},{5,13},{9,1},{13,5},{2,10},{6,14},... | collective-permute-start | bytes 786440 | tf_op jit(solution)/shard_map/ppermute | solution.py:468
  20.4 18.5 %collective-permute-start.7 = (bf16[2,2,256,256]{3,2,1,0:T(8,128)(2,1)S(1)}, bf16[2,2,256,256]{3,2,1,0:T(8,128)(2,1)S(1)}, u32[]{:S(2)}, u32[]{:S(2)}) collective-permute-start(bf16[2,2,256,256]{3,2,1,0:T(8,128)(2,1)S(1)} %get-tuple-element.54.last_ref.refs_5_.refs_1_), channel_id=1, source_target_pairs={{0,4},{4,0},{8,12},{12,8},{1,5},{5,1},{9,13},{13,9},{2,6},{6,2},{1... | collective-permute-start | bytes 1572872 | tf_op jit(solution)/shard_map/ppermute | solution.py:468
  20.9 14.4 %collective-permute-start.8 = (bf16[256,2,256]{2,1,0:T(2,128)(2,1)S(1)}, bf16[256,2,256]{2,1,0:T(2,128)(2,1)S(1)}, u32[]{:S(2)}, u32[]{:S(2)}) collective-permute-start(bf16[256,2,256]{2,1,0:T(2,128)(2,1)S(1)} %get-tuple-element.58.refs_0_), channel_id=1, source_target_pairs={{0,8},{4,12},{8,0},{12,4},{1,9},{5,13},{9,1},{13,5},{2,10},{6,14},... | collective-permute-start | bytes 786440 | tf_op jit(solution)/shard_map/ppermute | solution.py:468
  33.0 8.0 %collective-permute-start.2 = (bf16[256,2,256]{2,1,0:T(2,128)(2,1)S(1)}, bf16[256,2,256]{2,1,0:T(2,128)(2,1)S(1)}, u32[]{:S(2)}, u32[]{:S(2)}) collective-permute-start(bf16[256,2,256]{2,1,0:T(2,128)(2,1)S(1)} %choose.4.own_ref), channel_id=1, source_target_pairs={{0,4},{4,0},{8,12},{12,8},{1,5},{5,1},{9,13},{13,9},{2,6},{6,2},{1... | collective-permute-start | bytes 786440 | tf_op jit(solution)/shard_map/ppermute | solution.py:468
  36.0 6.0 %collective-permute-start.9 = (bf16[256,2,256]{2,1,0:T(2,128)(2,1)S(1)}, bf16[256,2,256]{2,1,0:T(2,128)(2,1)S(1)}, u32[]{:S(2)}, u32[]{:S(2)}) collective-permute-start(bf16[256,2,256]{2,1,0:T(2,128)(2,1)S(1)} %choose.5.own_ref), channel_id=1, source_target_pairs={{0,4},{4,0},{8,12},{12,8},{1,5},{5,1},{9,13},{13,9},{2,6},{6,2},{1... | collective-permute-start | bytes 786440 | tf_op jit(solution)/shard_map/ppermute | solution.py:468
  38.0 5.1 %collective-permute-start.10 = (f32[3,16,128]{2,1,0:T(8,128)S(1)}, f32[3,16,128]{2,1,0:T(8,128)S(1)}, u32[]{:S(2)}, u32[]{:S(2)}) collective-permute-start(f32[3,16,128]{2,1,0:T(8,128)S(1)} %across_products.1.refs_2_), channel_id=1, source_target_pairs={{4,8},{12,0},{8,4},{0,12},{5,9},{13,1},{9,5},{1,13},{6,10},{14,2},... | collective-permute-start | bytes 73736 | tf_op jit(solution)/shard_map/ppermute | solution.py:474

commit v3 on v2

--- a/solution.py
+++ b/solution.py
@@ -227,27 +227,26 @@
     )(*arrays)
 
 
-def choose_kernel(first, bit, stored, owner_ref, *refs):
-    sources, outs, sems = refs[:2], refs[2:-1], refs[-1]
+def choose_kernel(bit, owner_ref, here_ref, there_ref, out_ref, sems):
     me = lax.axis_index("scene")
     copies = []
-    for n, out in enumerate(outs):
-        tile = 2 * (first + n) + (me & 1)
-        here, there = [ref.at[0, tile] if stored else ref for ref in sources]
+    for n in range(out_ref.shape[0]):
+        tile = 2 * n + (me & 1)
+        here, there = [ref.at[0, tile] if len(ref.shape) > 4 else ref.at[n] for ref in (here_ref, there_ref)]
         same = ((owner_ref[tile] ^ me) >> bit) & 1 == 0
-        copies.append(pltpu.make_async_copy(here, out, sems.at[n]))
+        copies.append(pltpu.make_async_copy(here, out_ref.at[n], sems.at[n]))
         pl.when(same)(copies[n].start)
-        pl.when(jnp.logical_not(same))(pltpu.make_async_copy(there, out, sems.at[n]).start)
+        pl.when(jnp.logical_not(same))(pltpu.make_async_copy(there, out_ref.at[n], sems.at[n]).start)
     for copy in copies:
         copy.wait()
 
 
-def choose(owner, here, there, first, bit, chunks):
+def choose(owner, here, there, bit, chunks):
     return pl.pallas_call(
-        partial(choose_kernel, first, bit, here.ndim > 3),
+        partial(choose_kernel, bit),
         in_specs=[SMEM, VMEM, VMEM],
-        out_specs=[VMEM] * chunks,
-        out_shape=[pltpu.VMEM(here.shape[-3:], BF)] * chunks,
+        out_specs=VMEM,
+        out_shape=pltpu.VMEM((chunks, *here.shape[-3:]), BF),
         scratch_shapes=[pltpu.SemaphoreType.DMA((chunks,))],
         compiler_params=SMALL,
         name="choose",
@@ -299,10 +298,10 @@
     return [joined(list(pieces)) for pieces in zip(*units)]
 
 
-def reference_kernel(own_ref, mate_ref, *refs):
+def reference_kernel(chunk, own_ref, mate_ref, *refs):
     depth = len(refs) - 3
     cur_refs, (pair_ref, pow_ref, lead_ref) = refs[:depth], refs[depth:]
-    columns, half_rows = own_ref.shape[2], own_ref.shape[0] // 2
+    columns, half_rows = own_ref.shape[3], own_ref.shape[1] // 2
     core = lax.axis_index("scene") & 1
     size = 2 * half_rows
     row, part = lane_row(iota((1, size), 1), half_rows)
@@ -315,7 +314,7 @@
     units = []
     for n, (ref, place) in enumerate(((own_ref, core), (mate_ref, 1 - core))):
         for half in range(2):
-            rows = ref[half * half_rows : (half + 1) * half_rows].reshape(size, columns)
+            rows = ref[chunk, half * half_rows : (half + 1) * half_rows].reshape(size, columns)
             lead_ref[2 * n + half] = dot(turn, dot(rows, order, OVER_ROWS).astype(BF)).astype(BF)
             units.append(
                 multilook(terms, lead_ref.at[2 * n + half], *[ref.at[place, half] for ref in cur_refs])
@@ -326,12 +325,12 @@
         pair_ref[n // 2, n % 2] = found
 
 
-def reference_products(own, mate, currents):
+def reference_products(own, mate, currents, chunk):
     _, _, columns, width = currents[0].shape
     depth = len(currents)
     shapes = [(depth, 2, columns // LOOK_RG, width // 2), (columns // LOOK_RG, width // 2)]
     return pl.pallas_call(
-        reference_kernel,
+        partial(reference_kernel, chunk),
         in_specs=[VMEM] * (2 + depth),
         out_specs=[VMEM] * len(shapes),
         out_shape=[pltpu.VMEM(shape, F32) for shape in shapes],
@@ -496,11 +495,11 @@
     secondary, stored, *tables = operands
     operands = (secondary, *tables)
     owner = pltpu.with_memory_space_constraint(tile_owner, pltpu.HBM)
-    held = list(choose(owner, stored, arrived, 0, 0, chunks))
+    held = choose(owner, stored, arrived, 0, chunks)
     for bit in range(1, bits):
-        for n in range(chunks):
-            got = swapped(held[n], "scene", bit)
-            held[n] = choose(owner, held[n], got, n, bit, 1)[0]
+        got = swapped(held, "scene", bit)
+        held = choose(owner, held, got, bit, chunks)
+    mate = swapped(held, "scene", 0)
     turned = azimuth(operands, first.shape[1])
     first = neighbours(first, "range", 0)
     second = neighbours(second, "range", 1)
@@ -520,8 +519,7 @@
     returned = neighbours(across, "scene", 1, True)
     results = []
     for n, small in enumerate(within):
-        mate = swapped(held[n], "scene", 0)
-        pairs, pair_pow = reference_products(held[n], mate, currents[n])
+        pairs, pair_pow = reference_products(held, mate, currents[n], n)
         results.append((pairs, pair_pow, (across, returned)[n], *small))
     return finish(results, depth)
 

time: 44 us -> 33.7 us (0.77)
  waiting for transfers between devices: 11 us -> 4.93 us
  starting transfers between devices: 14.8 us -> 11.3 us
  Pallas kernels: 17.2 us -> 16.5 us
    ppermute x7 -> x5, waiting for transfers between devices: 11 us -> 0.01 us  [swapped(): lax.ppermute(block, axis, [(i, i ^ 1 << bit) for i in range(lax.axis_size...]
    ppermute x4, waiting for transfers between devices: 0.01 us -> 4.92 us  [neighbours(): return lax.ppermute(block, axis, pairs + [(j, i) for i, j in pairs])]
    ppermute x7 -> x5, starting transfers between devices: 5.73 us -> 2.76 us  [swapped(): lax.ppermute(block, axis, [(i, i ^ 1 << bit) for i in range(lax.axis_size...]
    pallas_call x5 -> x4, Pallas kernels: 4.23 us -> 3.56 us  [the longest x2 2.05 us: reference_products(): pl.pallas_call(partial(reference_kernel, chunk), in_specs=[VMEM] * (2 + d...]
    ppermute x4, starting transfers between devices: 9.05 us -> 8.55 us  [neighbours(): return lax.ppermute(block, axis, pairs + [(j, i) for i, j in pairs])]
  transfers between devices with their start and end apart: 11 -> 9, of which waited for: 2 -> 1; matrix products, arithmetic and copies ran while one was open for 0% -> 0% of each run, Pallas kernels for 38% -> 45%
where the time goes in v3:
time: 33.7 us; the launch traced here: 33.5 us
  Pallas kernels  16.5 us (49%)
  starting transfers between devices  11.3 us (34%)
  waiting for transfers between devices  4.93 us (15%)
  between operations  0.76 us (2%)
    ppermute x4, starting transfers between devices, neighbours(): return lax.ppermute(block, axis, pairs + [(j, i) for i, j in pairs])  8.55 us
    ppermute x4, waiting for transfers between devices, neighbours(): return lax.ppermute(block, axis, pairs + [(j, i) for i, j in pairs])  4.92 us
    pallas_call x1, Pallas kernels, azimuth(): pl.pallas_call(partial(azimuth_kernel, margin), in_specs=[VMEM] * len(ope...  4.17 us
    pallas_call x2, Pallas kernels, range_resample(): pl.pallas_call(partial(range_kernel, calls), in_specs=[VMEM] * len(arrays...  2.78 us
    ppermute x5, starting transfers between devices, swapped(): lax.ppermute(block, axis, [(i, i ^ 1 << bit) for i in range(lax.axis_size...  2.76 us
    pallas_call x1, Pallas kernels, load(): pl.pallas_call(partial(load_kernel, margin), in_specs=[anywhere] * len(op...  2.76 us
    pallas_call x1, Pallas kernels, within_products(): pl.pallas_call(partial(within_kernel, depth), in_specs=[VMEM] * len(array...  2.1 us
    pallas_call x2, Pallas kernels, reference_products(): pl.pallas_call(partial(reference_kernel, chunk), in_specs=[VMEM] * (2 + d...  2.05 us
  transfers between devices with their start and end apart: 9, of which 1 were waited for; matrix products, arithmetic and copies ran while one was open for 0% of the time, Pallas kernels for 45%

profile of v3, /device:TPU:9, one launch (start us, length us, event | category | flops | bytes accessed | tf_op | source)
XLA Modules:
  0.0 33.5 jit_solution(8644041881820868720)
XLA Ops:
  0.6 0.7 %collective-permute-start = (bf16[1,4,256,2,256]{4,3,2,1,0:T(2,128)(2,1)}, bf16[1,4,256,2,256]{4,3,2,1,0:T(2,128)(2,1)S(1)}, u32[]{:S(2)}, u32[]{:S(2)}) collective-permute-start(bf16[1,4,256,2,256]{4,3,2,1,0:T(2,128)(2,1)} %refs_0_.1), channel_id=1, source_target_pairs={{0,4},{4,0},{8,12},{12,8},{1,5},{5,1},{9,13},{13,9},{2,6},{6,2},{1... | collective-permute-start | bytes 3145736 | tf_op jit(solution)/shard_map/ppermute | solution.py:467
  1.4 2.8 %load.1 = (bf16[2,1056,2,256]{3,2,1,0:T(2,128)(2,1)S(1)}, bf16[1,4,256,2,256]{4,3,2,1,0:T(2,128)(2,1)S(1)}, f32[8,64]{1,0:T(8,128)S(1)}, f32[8,64]{1,0:T(8,128)S...) custom-call(bf16[2,1056,2,256]{3,2,1,0:T(2,128)(2,1)} %x_ref.1, ...), custom_call_target="tpu_custom_call" | custom-call | tf_op jit(solution)/shard_map/load/pallas_call | solution.py:107
  4.1 0.0 collective-permute-done.there_ref
  4.2 0.8 %choose.2.here_ref = bf16[2,256,2,256]{3,2,1,0:T(2,128)(2,1)S(1)} custom-call(s32[4]{0:T(128)} %owner_ref.3, bf16[1,4,256,2,256]{4,3,2,1,0:T(2,128)(2,1)S(1)} %get-tuple-element.33.here_ref, bf16[1,4,256,2,256]{4,3,2,1,0:T(2,128)(2,1)S(1)} %collective-permute-done.there_ref), custom_call_target="tpu_custom_call" | custom-call | tf_op jit(solution)/shard_map/choose/pallas_call | solution.py:245
  4.9 1.3 %collective-permute-start.1 = (bf16[2,256,2,256]{3,2,1,0:T(2,128)(2,1)S(1)}, bf16[2,256,2,256]{3,2,1,0:T(2,128)(2,1)S(1)}, u32[]{:S(2)}, u32[]{:S(2)}) collective-permute-start(bf16[2,256,2,256]{3,2,1,0:T(2,128)(2,1)S(1)} %choose.2.here_ref), channel_id=1, source_target_pairs={{0,8},{4,12},{8,0},{12,4},{1,9},{5,13},{9,1},{13,5},{2,10},{6,14},... | collective-permute-start | bytes 1572872 | tf_op jit(solution)/shard_map/ppermute | solution.py:467
  6.2 0.2 collective-permute-start.3
  6.4 4.3 %collective-permute-start.4 = (bf16[2,16,2112]{2,1,0:T(8,128)(2,1)S(1)}, bf16[2,16,2112]{2,1,0:T(8,128)(2,1)S(1)}, u32[]{:S(2)}, u32[]{:S(2)}) collective-permute-start(bf16[2,16,2112]{2,1,0:T(8,128)(2,1)S(1)} %get-tuple-element.45), channel_id=1, source_target_pairs={{1,2},{2,1},{5,6},{6,5},{9,10},{10,9},{13,14},{14,13},{17,18},{18,... | collective-permute-start | bytes 405512 | tf_op jit(solution)/shard_map/ppermute | solution.py:473
  10.7 4.2 %azimuth.1 = (bf16[2,4,2,256,256]{4,3,2,1,0:T(8,128)(2,1)S(1)}, bf16[2,4,2,320,256]{4,3,2,1,0:T(8,128)(2,1)S(1)}, bf16[2,288,256]{2,1,0:T(8,128)(2,1)S(1)}) custom-call(bf16[2,1056,2,256]{3,2,1,0:T(2,128)(2,1)S(1)} %get-tuple-element.34.x_ref, f32[8,64]{1,0:T(8,128)S(1)} %get-tuple-element.35.azk_ref, f32[8,64]{1,0:T(8,128)S(1)} %get-tuple-element.36.rgk_ref, ...), custom_call_target="tpu_custom_call" | custom-call | tf_op jit(solution)/shard_map/azimuth/pallas_call | solution.py:185
  14.9 0.0 collective-permute-done.3.first_ref
  14.9 0.0 collective-permute-done.4.second_ref
  14.9 1.4 %range_resample.3 = (bf16[2,2,256,256]{3,2,1,0:T(8,128)(2,1)S(1)}, bf16[2,2,256,256]{3,2,1,0:T(8,128)(2,1)S(1)}) custom-call(bf16[2,4,2,256,256]{4,3,2,1,0:T(8,128)(2,1)S(1)} %get-tuple-element.41.z_ref, bf16[2,4,2,320,256]{4,3,2,1,0:T(8,128)(2,1)S(1)} %get-tuple-element.42.band_ref, bf16[2,288,256]{2,1,0:T(8,128)(2,1)S(1)} %get-tuple-element.43.rg_ref, ...), custom_call_target="tpu_custom_call" | custom-call | tf_op jit(solution)/shard_map/range_resample/pallas_call | solution.py:220
  16.3 0.1 pick.1
  16.4 3.0 %collective-permute-start.5 = (bf16[2,2,256,256]{3,2,1,0:T(8,128)(2,1)S(1)}, bf16[2,2,256,256]{3,2,1,0:T(8,128)(2,1)S(1)}, u32[]{:S(2)}, u32[]{:S(2)}) collective-permute-start(bf16[2,2,256,256]{3,2,1,0:T(8,128)(2,1)S(1)} %pick.1), channel_id=1, source_target_pairs={{4,8},{8,4},{5,9},{9,5},{6,10},{10,6},{7,11},{11,7},{20,24},{24,20... | collective-permute-start | bytes 1572872 | tf_op jit(solution)/shard_map/ppermute | solution.py:473
  19.3 0.1 collective-permute-start.6
  19.4 1.4 %range_resample.2 = (bf16[2,2,256,256]{3,2,1,0:T(8,128)(2,1)S(1)}, bf16[2,2,256,256]{3,2,1,0:T(8,128)(2,1)S(1)}) custom-call(bf16[2,4,2,256,256]{4,3,2,1,0:T(8,128)(2,1)S(1)} %get-tuple-element.41.z_ref, bf16[2,4,2,320,256]{4,3,2,1,0:T(8,128)(2,1)S(1)} %get-tuple-element.42.band_ref, bf16[2,288,256]{2,1,0:T(8,128)(2,1)S(1)} %get-tuple-element.43.rg_ref, ...), custom_call_target="tpu_custom_call" | custom-call | tf_op jit(solution)/shard_map/range_resample/pallas_call | solution.py:220
  20.8 0.6 %collective-permute-start.7 = (bf16[2,2,256,256]{3,2,1,0:T(8,128)(2,1)S(1)}, bf16[2,2,256,256]{3,2,1,0:T(8,128)(2,1)S(1)}, u32[]{:S(2)}, u32[]{:S(2)}) collective-permute-start(bf16[2,2,256,256]{3,2,1,0:T(8,128)(2,1)S(1)} %get-tuple-element.51.last_ref.refs_5_.refs_1_), channel_id=1, source_target_pairs={{0,4},{4,0},{8,12},{12,8},{1,5},{5,1},{9,13},{13,9},{2,6},{6,2},{1... | collective-permute-start | bytes 1572872 | tf_op jit(solution)/shard_map/ppermute | solution.py:467
  21.4 0.0 collective-permute-done.1.there_ref
  21.4 0.8 %choose.3.own_ref = bf16[2,256,2,256]{3,2,1,0:T(2,128)(2,1)S(1)} custom-call(s32[4]{0:T(128)} %owner_ref.3, bf16[2,256,2,256]{3,2,1,0:T(2,128)(2,1)S(1)} %choose.2.here_ref, bf16[2,256,2,256]{3,2,1,0:T(2,128)(2,1)S(1)} %collective-permute-done.1.there_ref), custom_call_target="tpu_custom_call" | custom-call | tf_op jit(solution)/shard_map/choose/pallas_call | solution.py:245
  22.1 0.1 collective-permute-start.2
  22.2 4.9 %collective-permute-done.5.got_ref = bf16[2,2,256,256]{3,2,1,0:T(8,128)(2,1)S(1)} collective-permute-done((bf16[2,2,256,256]{3,2,1,0:T(8,128)(2,1)S(1)}, bf16[2,2,256,256]{3,2,1,0:T(8,128)(2,1)S(1)}, u32[]{:S(2)}, u32[]{:S(2)}) %collective-permute-start.5) | collective-permute-done | bytes 524320 | tf_op jit(solution)/shard_map/ppermute | solution.py:473
  27.1 0.4 %across_products.1.refs_2_ = f32[3,16,128]{2,1,0:T(8,128)S(1)} custom-call(bf16[2,2,256,256]{3,2,1,0:T(8,128)(2,1)S(1)} %collective-permute-done.5.got_ref, bf16[2,2,256,256]{3,2,1,0:T(8,128)(2,1)S(1)} %get-tuple-element.46.refs_0_.first_ref.refs_1_, bf16[2,2,256,256]{3,2,1,0:T(8,128)(2,1)S(1)} %get-tuple-element.51.last_ref.refs_5_.refs_1_), custom_call_target="tpu_custom_call" | custom-call | tf_op jit(solution)/shard_map/across_products/pallas_call | solution.py:399
  27.6 1.1 %collective-permute-start.8 = (f32[3,16,128]{2,1,0:T(8,128)S(1)}, f32[3,16,128]{2,1,0:T(8,128)S(1)}, u32[]{:S(2)}, u32[]{:S(2)}) collective-permute-start(f32[3,16,128]{2,1,0:T(8,128)S(1)} %across_products.1.refs_2_), channel_id=1, source_target_pairs={{4,8},{12,0},{8,4},{0,12},{5,9},{13,1},{9,5},{1,13},{6,10},{14,2},... | collective-permute-start | bytes 73736 | tf_op jit(solution)/shard_map/ppermute | solution.py:473
  28.7 0.0 collective-permute-done.6.refs_0_
  28.7 0.0 collective-permute-done.7.refs_3_
  28.7 2.1 %within_products.1 = (f32[3,16,128]{2,1,0:T(8,128)S(1)}, f32[1,2,16,128]{3,2,1,0:T(8,128)S(1)}, f32[2,16,128]{2,1,0:T(8,128)S(1)}, f32[3,16,128]{2,1,0:T(8,128)S...) custom-call(bf16[2,2,256,256]{3,2,1,0:T(8,128)(2,1)S(1)} %collective-permute-done.6.refs_0_, ...), custom_call_target="tpu_custom_call" | custom-call | tf_op jit(solution)/shard_map/within_products/pallas_call | solution.py:373
  30.8 0.0 collective-permute-done.2.mate_ref
  30.8 1.0 %reference_products.3 = (f32[2,2,16,128]{3,2,1,0:T(8,128)S(1)}, f32[16,128]{1,0:T(8,128)S(1)}) custom-call(bf16[2,256,2,256]{3,2,1,0:T(2,128)(2,1)S(1)} %choose.3.own_ref, bf16[2,256,2,256]{3,2,1,0:T(2,128)(2,1)S(1)} %collective-permute-done.2.mate_ref, bf16[2,2,256,256]{3,2,1,0:T(8,128)(2,1)S(1)} %get-tuple-element.50.even_ref.refs_4_.refs_0_, ...), custom_call_target="tpu_custom_call" | custom-call | tf_op jit(solution)/shard_map/reference_products/pallas_call | solution.py:332
  31.8 1.0 %reference_products.2 = (f32[2,2,16,128]{3,2,1,0:T(8,128)S(1)}, f32[16,128]{1,0:T(8,128)S(1)}) custom-call(bf16[2,256,2,256]{3,2,1,0:T(2,128)(2,1)S(1)} %choose.3.own_ref, bf16[2,256,2,256]{3,2,1,0:T(2,128)(2,1)S(1)} %collective-permute-done.2.mate_ref, bf16[2,2,256,256]{3,2,1,0:T(8,128)(2,1)S(1)} %get-tuple-element.46.refs_0_.first_ref.refs_1_, ...), custom_call_target="tpu_custom_call" | custom-call | tf_op jit(solution)/shard_map/reference_products/pallas_call | solution.py:332
  32.9 0.0 collective-permute-done.8.refs_8_
  32.9 0.7 %finish.1 = (f32[2,2,16,256]{3,2,1,0:T(8,128)}, f32[2,2,16,256]{3,2,1,0:T(8,128)}, f32[2,16,256]{2,1,0:T(8,128)}) custom-call(f32[2,2,16,128]{3,2,1,0:T(8,128)S(1)} %get-tuple-element.48.refs_0_, f32[16,128]{1,0:T(8,128)S(1)} %get-tuple-element.49.refs_1_, f32[3,16,128]{2,1,0:T(8,128)S(1)} %across_products.1.refs_2_, ...), custom_call_target="tpu_custom_call" | custom-call | tf_op jit(solution)/shard_map/finish/pallas_call | solution.py:455
Async XLA Ops:
  0.6 3.5 %collective-permute-start = (bf16[1,4,256,2,256]{4,3,2,1,0:T(2,128)(2,1)}, bf16[1,4,256,2,256]{4,3,2,1,0:T(2,128)(2,1)S(1)}, u32[]{:S(2)}, u32[]{:S(2)}) collective-permute-start(bf16[1,4,256,2,256]{4,3,2,1,0:T(2,128)(2,1)} %refs_0_.1), channel_id=1, source_target_pairs={{0,4},{4,0},{8,12},{12,8},{1,5},{5,1},{9,13},{13,9},{2,6},{6,2},{1... | collective-permute-start | bytes 3145736 | tf_op jit(solution)/shard_map/ppermute | solution.py:467
  4.9 16.5 %collective-permute-start.1 = (bf16[2,256,2,256]{3,2,1,0:T(2,128)(2,1)S(1)}, bf16[2,256,2,256]{3,2,1,0:T(2,128)(2,1)S(1)}, u32[]{:S(2)}, u32[]{:S(2)}) collective-permute-start(bf16[2,256,2,256]{3,2,1,0:T(2,128)(2,1)S(1)} %choose.2.here_ref), channel_id=1, source_target_pairs={{0,8},{4,12},{8,0},{12,4},{1,9},{5,13},{9,1},{13,5},{2,10},{6,14},... | collective-permute-start | bytes 1572872 | tf_op jit(solution)/shard_map/ppermute | solution.py:467
  6.2 8.7 %collective-permute-start.3 = (bf16[2,16,2112]{2,1,0:T(8,128)(2,1)S(1)}, bf16[2,16,2112]{2,1,0:T(8,128)(2,1)S(1)}, u32[]{:S(2)}, u32[]{:S(2)}) collective-permute-start(bf16[2,16,2112]{2,1,0:T(8,128)(2,1)S(1)} %get-tuple-element.44), channel_id=1, source_target_pairs={{0,1},{2,3},{1,0},{3,2},{4,5},{6,7},{5,4},{7,6},{8,9},{10,11},{9,8... | collective-permute-start | bytes 405512 | tf_op jit(solution)/shard_map/ppermute | solution.py:473
  6.4 8.5 %collective-permute-start.4 = (bf16[2,16,2112]{2,1,0:T(8,128)(2,1)S(1)}, bf16[2,16,2112]{2,1,0:T(8,128)(2,1)S(1)}, u32[]{:S(2)}, u32[]{:S(2)}) collective-permute-start(bf16[2,16,2112]{2,1,0:T(8,128)(2,1)S(1)} %get-tuple-element.45), channel_id=1, source_target_pairs={{1,2},{2,1},{5,6},{6,5},{9,10},{10,9},{13,14},{14,13},{17,18},{18,... | collective-permute-start | bytes 405512 | tf_op jit(solution)/shard_map/ppermute | solution.py:473
  16.4 10.8 %collective-permute-start.5 = (bf16[2,2,256,256]{3,2,1,0:T(8,128)(2,1)S(1)}, bf16[2,2,256,256]{3,2,1,0:T(8,128)(2,1)S(1)}, u32[]{:S(2)}, u32[]{:S(2)}) collective-permute-start(bf16[2,2,256,256]{3,2,1,0:T(8,128)(2,1)S(1)} %pick.1), channel_id=1, source_target_pairs={{4,8},{8,4},{5,9},{9,5},{6,10},{10,6},{7,11},{11,7},{20,24},{24,20... | collective-permute-start | bytes 1572872 | tf_op jit(solution)/shard_map/ppermute | solution.py:473
  19.3 9.4 %collective-permute-start.6 = (bf16[2,2,256,256]{3,2,1,0:T(8,128)(2,1)S(1)}, bf16[2,2,256,256]{3,2,1,0:T(8,128)(2,1)S(1)}, u32[]{:S(2)}, u32[]{:S(2)}) collective-permute-start(bf16[2,2,256,256]{3,2,1,0:T(8,128)(2,1)S(1)} %get-tuple-element.47.refs_1_.odd_ref.refs_2_), channel_id=1, source_target_pairs={{0,4},{4,0},{8,12},{12,8},{1,5},{5,1},{9,13},{13,9},{2,6},{6,2},{1... | collective-permute-start | bytes 1572872 | tf_op jit(solution)/shard_map/ppermute | solution.py:467
  20.8 7.9 %collective-permute-start.7 = (bf16[2,2,256,256]{3,2,1,0:T(8,128)(2,1)S(1)}, bf16[2,2,256,256]{3,2,1,0:T(8,128)(2,1)S(1)}, u32[]{:S(2)}, u32[]{:S(2)}) collective-permute-start(bf16[2,2,256,256]{3,2,1,0:T(8,128)(2,1)S(1)} %get-tuple-element.51.last_ref.refs_5_.refs_1_), channel_id=1, source_target_pairs={{0,4},{4,0},{8,12},{12,8},{1,5},{5,1},{9,13},{13,9},{2,6},{6,2},{1... | collective-permute-start | bytes 1572872 | tf_op jit(solution)/shard_map/ppermute | solution.py:467
  22.1 8.7 %collective-permute-start.2 = (bf16[2,256,2,256]{3,2,1,0:T(2,128)(2,1)S(1)}, bf16[2,256,2,256]{3,2,1,0:T(2,128)(2,1)S(1)}, u32[]{:S(2)}, u32[]{:S(2)}) collective-permute-start(bf16[2,256,2,256]{3,2,1,0:T(2,128)(2,1)S(1)} %choose.3.own_ref), channel_id=1, source_target_pairs={{0,4},{4,0},{8,12},{12,8},{1,5},{5,1},{9,13},{13,9},{2,6},{6,2},{1... | collective-permute-start | bytes 1572872 | tf_op jit(solution)/shard_map/ppermute | solution.py:467
  27.6 5.3 %collective-permute-start.8 = (f32[3,16,128]{2,1,0:T(8,128)S(1)}, f32[3,16,128]{2,1,0:T(8,128)S(1)}, u32[]{:S(2)}, u32[]{:S(2)}) collective-permute-start(f32[3,16,128]{2,1,0:T(8,128)S(1)} %across_products.1.refs_2_), channel_id=1, source_target_pairs={{4,8},{12,0},{8,4},{0,12},{5,9},{13,1},{9,5},{1,13},{6,10},{14,2},... | collective-permute-start | bytes 73736 | tf_op jit(solution)/shard_map/ppermute | solution.py:473

commit v4 on v3

--- a/solution.py
+++ b/solution.py
@@ -107,8 +107,8 @@
     outs = pl.pallas_call(
         partial(load_kernel, margin),
         in_specs=[anywhere] * len(operands),
-        out_specs=[VMEM] * (len(operands) + 2),
-        out_shape=[pltpu.VMEM(a.shape, a.dtype) for a in operands] + [edge, edge],
+        out_specs=[SMEM if a.ndim == 1 else VMEM for a in operands] + [VMEM] * 2,
+        out_shape=[(pltpu.SMEM if a.ndim == 1 else pltpu.VMEM)(a.shape, a.dtype) for a in operands] + [edge, edge],
         scratch_shapes=[pltpu.SemaphoreType.DMA((depth * (rows // TILE) + len(small),))],
         compiler_params=SMALL,
         name="load",
@@ -490,11 +490,11 @@
 
     arrived = swapped(reference_store, "scene", 0)
     operands, first, second = load(
-        secondary, reference_store, az_kernel.T, rg_kernel.T, rg_offset, rg_index, az_index, az_offset
+        secondary, tile_owner, reference_store, az_kernel.T, rg_kernel.T, rg_offset, rg_index, az_index, az_offset
     )
-    secondary, stored, *tables = operands
+    secondary, owner, stored, *tables = operands
     operands = (secondary, *tables)
-    owner = pltpu.with_memory_space_constraint(tile_owner, pltpu.HBM)
+    owner = pltpu.with_memory_space_constraint(owner, pltpu.SMEM)
     held = choose(owner, stored, arrived, 0, chunks)
     for bit in range(1, bits):
         got = swapped(held, "scene", bit)

time: 33.7 us -> 33 us (0.979)
  the two profiles are of different devices: /device:TPU:9 before, /device:TPU:11 now
where the time goes in v4:
time: 33 us; the launch traced here: 32.9 us
  Pallas kernels  15.2 us (46%)
  starting transfers between devices  11.2 us (34%)
  waiting for transfers between devices  5.64 us (17%)
  between operations  0.77 us (2%)
    ppermute x4, starting transfers between devices, neighbours(): return lax.ppermute(block, axis, pairs + [(j, i) for i, j in pairs])  8.46 us
    ppermute x4, waiting for transfers between devices, neighbours(): return lax.ppermute(block, axis, pairs + [(j, i) for i, j in pairs])  5.63 us
    pallas_call x1, Pallas kernels, azimuth(): pl.pallas_call(partial(azimuth_kernel, margin), in_specs=[VMEM] * len(ope...  4.17 us
    ppermute x5, starting transfers between devices, swapped(): lax.ppermute(block, axis, [(i, i ^ 1 << bit) for i in range(lax.axis_size...  2.78 us
    pallas_call x2, Pallas kernels, range_resample(): pl.pallas_call(partial(range_kernel, calls), in_specs=[VMEM] * len(arrays...  2.78 us
    pallas_call x1, Pallas kernels, load(): pl.pallas_call(partial(load_kernel, margin), in_specs=[anywhere] * len(op...  2.78 us
    pallas_call x1, Pallas kernels, within_products(): pl.pallas_call(partial(within_kernel, depth), in_specs=[VMEM] * len(array...  2.1 us
    pallas_call x2, Pallas kernels, reference_products(): pl.pallas_call(partial(reference_kernel, chunk), in_specs=[VMEM] * (2 + d...  2.05 us
  transfers between devices with their start and end apart: 9, of which 1 were waited for; matrix products, arithmetic and copies ran while one was open for 0% of the time, Pallas kernels for 44%

profile of v4, /device:TPU:11, one launch (start us, length us, event | category | flops | bytes accessed | tf_op | source)
XLA Modules:
  0.0 32.9 jit_solution(4244258953565650347)
XLA Ops:
  0.6 0.7 %collective-permute-start = (bf16[1,4,256,2,256]{4,3,2,1,0:T(2,128)(2,1)}, bf16[1,4,256,2,256]{4,3,2,1,0:T(2,128)(2,1)S(1)}, u32[]{:S(2)}, u32[]{:S(2)}) collective-permute-start(bf16[1,4,256,2,256]{4,3,2,1,0:T(2,128)(2,1)} %refs_1_.1), channel_id=1, source_target_pairs={{0,4},{4,0},{8,12},{12,8},{1,5},{5,1},{9,13},{13,9},{2,6},{6,2},{1... | collective-permute-start | bytes 3145736 | tf_op jit(solution)/shard_map/ppermute | solution.py:467
  1.4 2.8 %load.1 = (bf16[2,1056,2,256]{3,2,1,0:T(2,128)(2,1)S(1)}, s32[4]{0:T(128)S(4)}, bf16[1,4,256,2,256]{4,3,2,1,0:T(2,128)(2,1)S(1)}, f32[8,64]{1,0:T(8,128)S(1)}, f...) custom-call(bf16[2,1056,2,256]{3,2,1,0:T(2,128)(2,1)} %x_ref.1, ...), custom_call_target="tpu_custom_call" | custom-call | tf_op jit(solution)/shard_map/load/pallas_call | solution.py:107
  4.2 0.0 collective-permute-done.there_ref
  4.2 0.1 choose.2.here_ref
  4.3 1.3 %collective-permute-start.1 = (bf16[2,256,2,256]{3,2,1,0:T(2,128)(2,1)S(1)}, bf16[2,256,2,256]{3,2,1,0:T(2,128)(2,1)S(1)}, u32[]{:S(2)}, u32[]{:S(2)}) collective-permute-start(bf16[2,256,2,256]{3,2,1,0:T(2,128)(2,1)S(1)} %choose.2.here_ref), channel_id=1, source_target_pairs={{0,8},{4,12},{8,0},{12,4},{1,9},{5,13},{9,1},{13,5},{2,10},{6,14},... | collective-permute-start | bytes 1572872 | tf_op jit(solution)/shard_map/ppermute | solution.py:467
  5.6 0.2 collective-permute-start.3
  5.7 4.3 %collective-permute-start.4 = (bf16[2,16,2112]{2,1,0:T(8,128)(2,1)S(1)}, bf16[2,16,2112]{2,1,0:T(8,128)(2,1)S(1)}, u32[]{:S(2)}, u32[]{:S(2)}) collective-permute-start(bf16[2,16,2112]{2,1,0:T(8,128)(2,1)S(1)} %get-tuple-element.47), channel_id=1, source_target_pairs={{1,2},{2,1},{5,6},{6,5},{9,10},{10,9},{13,14},{14,13},{17,18},{18,... | collective-permute-start | bytes 405512 | tf_op jit(solution)/shard_map/ppermute | solution.py:473
  10.1 4.2 %azimuth.1 = (bf16[2,4,2,256,256]{4,3,2,1,0:T(8,128)(2,1)S(1)}, bf16[2,4,2,320,256]{4,3,2,1,0:T(8,128)(2,1)S(1)}, bf16[2,288,256]{2,1,0:T(8,128)(2,1)S(1)}) custom-call(bf16[2,1056,2,256]{3,2,1,0:T(2,128)(2,1)S(1)} %get-tuple-element.36.x_ref, f32[8,64]{1,0:T(8,128)S(1)} %get-tuple-element.37.azk_ref, f32[8,64]{1,0:T(8,128)S(1)} %get-tuple-element.38.rgk_ref, ...), custom_call_target="tpu_custom_call" | custom-call | tf_op jit(solution)/shard_map/azimuth/pallas_call | solution.py:185
  14.2 0.0 collective-permute-done.3.first_ref
  14.3 0.0 collective-permute-done.4.second_ref
  14.3 1.4 %range_resample.3 = (bf16[2,2,256,256]{3,2,1,0:T(8,128)(2,1)S(1)}, bf16[2,2,256,256]{3,2,1,0:T(8,128)(2,1)S(1)}) custom-call(bf16[2,4,2,256,256]{4,3,2,1,0:T(8,128)(2,1)S(1)} %get-tuple-element.43.z_ref, bf16[2,4,2,320,256]{4,3,2,1,0:T(8,128)(2,1)S(1)} %get-tuple-element.44.band_ref, bf16[2,288,256]{2,1,0:T(8,128)(2,1)S(1)} %get-tuple-element.45.rg_ref, ...), custom_call_target="tpu_custom_call" | custom-call | tf_op jit(solution)/shard_map/range_resample/pallas_call | solution.py:220
  15.7 0.1 pick.1
  15.7 2.9 %collective-permute-start.5 = (bf16[2,2,256,256]{3,2,1,0:T(8,128)(2,1)S(1)}, bf16[2,2,256,256]{3,2,1,0:T(8,128)(2,1)S(1)}, u32[]{:S(2)}, u32[]{:S(2)}) collective-permute-start(bf16[2,2,256,256]{3,2,1,0:T(8,128)(2,1)S(1)} %pick.1), channel_id=1, source_target_pairs={{4,8},{8,4},{5,9},{9,5},{6,10},{10,6},{7,11},{11,7},{20,24},{24,20... | collective-permute-start | bytes 1572872 | tf_op jit(solution)/shard_map/ppermute | solution.py:473
  18.7 0.1 collective-permute-start.6
  18.7 1.4 %range_resample.2 = (bf16[2,2,256,256]{3,2,1,0:T(8,128)(2,1)S(1)}, bf16[2,2,256,256]{3,2,1,0:T(8,128)(2,1)S(1)}) custom-call(bf16[2,4,2,256,256]{4,3,2,1,0:T(8,128)(2,1)S(1)} %get-tuple-element.43.z_ref, bf16[2,4,2,320,256]{4,3,2,1,0:T(8,128)(2,1)S(1)} %get-tuple-element.44.band_ref, bf16[2,288,256]{2,1,0:T(8,128)(2,1)S(1)} %get-tuple-element.45.rg_ref, ...), custom_call_target="tpu_custom_call" | custom-call | tf_op jit(solution)/shard_map/range_resample/pallas_call | solution.py:220
  20.1 0.6 %collective-permute-start.7 = (bf16[2,2,256,256]{3,2,1,0:T(8,128)(2,1)S(1)}, bf16[2,2,256,256]{3,2,1,0:T(8,128)(2,1)S(1)}, u32[]{:S(2)}, u32[]{:S(2)}) collective-permute-start(bf16[2,2,256,256]{3,2,1,0:T(8,128)(2,1)S(1)} %get-tuple-element.53.last_ref.refs_5_.refs_1_), channel_id=1, source_target_pairs={{0,4},{4,0},{8,12},{12,8},{1,5},{5,1},{9,13},{13,9},{2,6},{6,2},{1... | collective-permute-start | bytes 1572872 | tf_op jit(solution)/shard_map/ppermute | solution.py:467
  20.7 0.0 collective-permute-done.1.there_ref
  20.7 0.1 choose.3.own_ref
  20.8 0.1 collective-permute-start.2
  20.9 5.6 %collective-permute-done.5.got_ref = bf16[2,2,256,256]{3,2,1,0:T(8,128)(2,1)S(1)} collective-permute-done((bf16[2,2,256,256]{3,2,1,0:T(8,128)(2,1)S(1)}, bf16[2,2,256,256]{3,2,1,0:T(8,128)(2,1)S(1)}, u32[]{:S(2)}, u32[]{:S(2)}) %collective-permute-start.5) | collective-permute-done | bytes 524320 | tf_op jit(solution)/shard_map/ppermute | solution.py:473
  26.5 0.4 %across_products.1.refs_2_ = f32[3,16,128]{2,1,0:T(8,128)S(1)} custom-call(bf16[2,2,256,256]{3,2,1,0:T(8,128)(2,1)S(1)} %collective-permute-done.5.got_ref, bf16[2,2,256,256]{3,2,1,0:T(8,128)(2,1)S(1)} %get-tuple-element.48.refs_0_.first_ref.refs_1_, bf16[2,2,256,256]{3,2,1,0:T(8,128)(2,1)S(1)} %get-tuple-element.53.last_ref.refs_5_.refs_1_), custom_call_target="tpu_custom_call" | custom-call | tf_op jit(solution)/shard_map/across_products/pallas_call | solution.py:399
  26.9 1.1 %collective-permute-start.8 = (f32[3,16,128]{2,1,0:T(8,128)S(1)}, f32[3,16,128]{2,1,0:T(8,128)S(1)}, u32[]{:S(2)}, u32[]{:S(2)}) collective-permute-start(f32[3,16,128]{2,1,0:T(8,128)S(1)} %across_products.1.refs_2_), channel_id=1, source_target_pairs={{4,8},{12,0},{8,4},{0,12},{5,9},{13,1},{9,5},{1,13},{6,10},{14,2},... | collective-permute-start | bytes 73736 | tf_op jit(solution)/shard_map/ppermute | solution.py:473
  28.0 0.0 collective-permute-done.6.refs_0_
  28.0 0.0 collective-permute-done.7.refs_3_
  28.0 2.1 %within_products.1 = (f32[3,16,128]{2,1,0:T(8,128)S(1)}, f32[1,2,16,128]{3,2,1,0:T(8,128)S(1)}, f32[2,16,128]{2,1,0:T(8,128)S(1)}, f32[3,16,128]{2,1,0:T(8,128)S...) custom-call(bf16[2,2,256,256]{3,2,1,0:T(8,128)(2,1)S(1)} %collective-permute-done.6.refs_0_, ...), custom_call_target="tpu_custom_call" | custom-call | tf_op jit(solution)/shard_map/within_products/pallas_call | solution.py:373
  30.1 0.0 collective-permute-done.2.mate_ref
  30.1 1.0 %reference_products.3 = (f32[2,2,16,128]{3,2,1,0:T(8,128)S(1)}, f32[16,128]{1,0:T(8,128)S(1)}) custom-call(bf16[2,256,2,256]{3,2,1,0:T(2,128)(2,1)S(1)} %choose.3.own_ref, bf16[2,256,2,256]{3,2,1,0:T(2,128)(2,1)S(1)} %collective-permute-done.2.mate_ref, bf16[2,2,256,256]{3,2,1,0:T(8,128)(2,1)S(1)} %get-tuple-element.52.even_ref.refs_4_.refs_0_, ...), custom_call_target="tpu_custom_call" | custom-call | tf_op jit(solution)/shard_map/reference_products/pallas_call | solution.py:332
  31.1 1.0 %reference_products.2 = (f32[2,2,16,128]{3,2,1,0:T(8,128)S(1)}, f32[16,128]{1,0:T(8,128)S(1)}) custom-call(bf16[2,256,2,256]{3,2,1,0:T(2,128)(2,1)S(1)} %choose.3.own_ref, bf16[2,256,2,256]{3,2,1,0:T(2,128)(2,1)S(1)} %collective-permute-done.2.mate_ref, bf16[2,2,256,256]{3,2,1,0:T(8,128)(2,1)S(1)} %get-tuple-element.48.refs_0_.first_ref.refs_1_, ...), custom_call_target="tpu_custom_call" | custom-call | tf_op jit(solution)/shard_map/reference_products/pallas_call | solution.py:332
  32.2 0.0 collective-permute-done.8.refs_8_
  32.2 0.7 %finish.1 = (f32[2,2,16,256]{3,2,1,0:T(8,128)}, f32[2,2,16,256]{3,2,1,0:T(8,128)}, f32[2,16,256]{2,1,0:T(8,128)}) custom-call(f32[2,2,16,128]{3,2,1,0:T(8,128)S(1)} %get-tuple-element.50.refs_0_, f32[16,128]{1,0:T(8,128)S(1)} %get-tuple-element.51.refs_1_, f32[3,16,128]{2,1,0:T(8,128)S(1)} %across_products.1.refs_2_, ...), custom_call_target="tpu_custom_call" | custom-call | tf_op jit(solution)/shard_map/finish/pallas_call | solution.py:455
Async XLA Ops:
  0.6 3.5 %collective-permute-start = (bf16[1,4,256,2,256]{4,3,2,1,0:T(2,128)(2,1)}, bf16[1,4,256,2,256]{4,3,2,1,0:T(2,128)(2,1)S(1)}, u32[]{:S(2)}, u32[]{:S(2)}) collective-permute-start(bf16[1,4,256,2,256]{4,3,2,1,0:T(2,128)(2,1)} %refs_1_.1), channel_id=1, source_target_pairs={{0,4},{4,0},{8,12},{12,8},{1,5},{5,1},{9,13},{13,9},{2,6},{6,2},{1... | collective-permute-start | bytes 3145736 | tf_op jit(solution)/shard_map/ppermute | solution.py:467
  4.3 16.4 %collective-permute-start.1 = (bf16[2,256,2,256]{3,2,1,0:T(2,128)(2,1)S(1)}, bf16[2,256,2,256]{3,2,1,0:T(2,128)(2,1)S(1)}, u32[]{:S(2)}, u32[]{:S(2)}) collective-permute-start(bf16[2,256,2,256]{3,2,1,0:T(2,128)(2,1)S(1)} %choose.2.here_ref), channel_id=1, source_target_pairs={{0,8},{4,12},{8,0},{12,4},{1,9},{5,13},{9,1},{13,5},{2,10},{6,14},... | collective-permute-start | bytes 1572872 | tf_op jit(solution)/shard_map/ppermute | solution.py:467
  5.6 8.7 %collective-permute-start.3 = (bf16[2,16,2112]{2,1,0:T(8,128)(2,1)S(1)}, bf16[2,16,2112]{2,1,0:T(8,128)(2,1)S(1)}, u32[]{:S(2)}, u32[]{:S(2)}) collective-permute-start(bf16[2,16,2112]{2,1,0:T(8,128)(2,1)S(1)} %get-tuple-element.46), channel_id=1, source_target_pairs={{0,1},{2,3},{1,0},{3,2},{4,5},{6,7},{5,4},{7,6},{8,9},{10,11},{9,8... | collective-permute-start | bytes 405512 | tf_op jit(solution)/shard_map/ppermute | solution.py:473
  5.7 8.5 %collective-permute-start.4 = (bf16[2,16,2112]{2,1,0:T(8,128)(2,1)S(1)}, bf16[2,16,2112]{2,1,0:T(8,128)(2,1)S(1)}, u32[]{:S(2)}, u32[]{:S(2)}) collective-permute-start(bf16[2,16,2112]{2,1,0:T(8,128)(2,1)S(1)} %get-tuple-element.47), channel_id=1, source_target_pairs={{1,2},{2,1},{5,6},{6,5},{9,10},{10,9},{13,14},{14,13},{17,18},{18,... | collective-permute-start | bytes 405512 | tf_op jit(solution)/shard_map/ppermute | solution.py:473
  15.7 10.8 %collective-permute-start.5 = (bf16[2,2,256,256]{3,2,1,0:T(8,128)(2,1)S(1)}, bf16[2,2,256,256]{3,2,1,0:T(8,128)(2,1)S(1)}, u32[]{:S(2)}, u32[]{:S(2)}) collective-permute-start(bf16[2,2,256,256]{3,2,1,0:T(8,128)(2,1)S(1)} %pick.1), channel_id=1, source_target_pairs={{4,8},{8,4},{5,9},{9,5},{6,10},{10,6},{7,11},{11,7},{20,24},{24,20... | collective-permute-start | bytes 1572872 | tf_op jit(solution)/shard_map/ppermute | solution.py:473
  18.7 9.4 %collective-permute-start.6 = (bf16[2,2,256,256]{3,2,1,0:T(8,128)(2,1)S(1)}, bf16[2,2,256,256]{3,2,1,0:T(8,128)(2,1)S(1)}, u32[]{:S(2)}, u32[]{:S(2)}) collective-permute-start(bf16[2,2,256,256]{3,2,1,0:T(8,128)(2,1)S(1)} %get-tuple-element.49.refs_1_.odd_ref.refs_2_), channel_id=1, source_target_pairs={{0,4},{4,0},{8,12},{12,8},{1,5},{5,1},{9,13},{13,9},{2,6},{6,2},{1... | collective-permute-start | bytes 1572872 | tf_op jit(solution)/shard_map/ppermute | solution.py:467
  20.1 7.9 %collective-permute-start.7 = (bf16[2,2,256,256]{3,2,1,0:T(8,128)(2,1)S(1)}, bf16[2,2,256,256]{3,2,1,0:T(8,128)(2,1)S(1)}, u32[]{:S(2)}, u32[]{:S(2)}) collective-permute-start(bf16[2,2,256,256]{3,2,1,0:T(8,128)(2,1)S(1)} %get-tuple-element.53.last_ref.refs_5_.refs_1_), channel_id=1, source_target_pairs={{0,4},{4,0},{8,12},{12,8},{1,5},{5,1},{9,13},{13,9},{2,6},{6,2},{1... | collective-permute-start | bytes 1572872 | tf_op jit(solution)/shard_map/ppermute | solution.py:467
  20.8 9.3 %collective-permute-start.2 = (bf16[2,256,2,256]{3,2,1,0:T(2,128)(2,1)S(1)}, bf16[2,256,2,256]{3,2,1,0:T(2,128)(2,1)S(1)}, u32[]{:S(2)}, u32[]{:S(2)}) collective-permute-start(bf16[2,256,2,256]{3,2,1,0:T(2,128)(2,1)S(1)} %choose.3.own_ref), channel_id=1, source_target_pairs={{0,4},{4,0},{8,12},{12,8},{1,5},{5,1},{9,13},{13,9},{2,6},{6,2},{1... | collective-permute-start | bytes 1572872 | tf_op jit(solution)/shard_map/ppermute | solution.py:467
  26.9 5.2 %collective-permute-start.8 = (f32[3,16,128]{2,1,0:T(8,128)S(1)}, f32[3,16,128]{2,1,0:T(8,128)S(1)}, u32[]{:S(2)}, u32[]{:S(2)}) collective-permute-start(f32[3,16,128]{2,1,0:T(8,128)S(1)} %across_products.1.refs_2_), channel_id=1, source_target_pairs={{4,8},{12,0},{8,4},{0,12},{5,9},{13,1},{9,5},{1,13},{6,10},{14,2},... | collective-permute-start | bytes 73736 | tf_op jit(solution)/shard_map/ppermute | solution.py:473

commit v5 on v4

--- a/solution.py
+++ b/solution.py
@@ -133,7 +133,10 @@
     return value
 
 
-def azimuth_kernel(margin, x_ref, azk_ref, rgk_ref, rgo_ref, rgi_ref, azi_ref, azo_ref, z_ref, band_ref, rg_ref, spread_ref):
+def azimuth_kernel(
+    margin, calls, x_ref, azk_ref, rgk_ref, rgo_ref, rgi_ref, azi_ref, azo_ref, z_ref, band_ref, *refs
+):
+    *rg_refs, spread_ref = refs
     depth, _, _, columns = x_ref.shape
     taps = azk_ref.shape[0]
     tile, lanes = spread_ref.shape
@@ -144,13 +147,14 @@
     spread_ref[...] = chosen((tile, lanes), 0, row + half_rows * over(lane, half_lanes))
     column = look_column(iota((1, columns), 1), columns)
     order = chosen((columns, columns), 0, column)
-    for k in range(depth):
-        rg_ref[k] = range_matrix(
-            margin, columns + 2 * margin, rgk_ref, rgi_ref[k : k + 1], rgo_ref[k : k + 1], order, column
-        ).astype(BF)
-    for k in range(depth):
-        for s in range(z_ref.shape[1]):
-            start = s * tile
+    for rg_ref in rg_refs:
+        for k in range(depth):
+            rg_ref[k] = range_matrix(
+                margin, columns + 2 * margin, rgk_ref, rgi_ref[k : k + 1], rgo_ref[k : k + 1], order, column
+            ).astype(BF)
+    for call, (k, chunk) in enumerate(calls):
+        for s in range(2):
+            start = (2 * chunk + s) * tile
             rows = slice(start, start + tile)
             both = taps_and_offsets(
                 azk_ref[...], azi_ref[k : k + 1, rows], azo_ref[k : k + 1, rows], spread_ref[...]
@@ -162,7 +166,7 @@
             home = -over(place, taps)
             for half in range(2):
                 mine = slice(half * half_lanes, (half + 1) * half_lanes)
-                band = band_ref.at[k, s, half]
+                band = band_ref.at[call, s, half]
                 for block in range(band.shape[0] // period):
                     band[block * period : (block + 1) * period] = jnp.where(
                         home[:, mine] == block, value[:, mine], 0.0
@@ -170,20 +174,20 @@
                 begin = start + half * half_rows
                 size = half_rows + 2 * margin
                 window = x_ref[k, begin : begin + size].reshape(2 * size, columns)
-                z_ref[k, s, half] = dot(window, band[...], OVER_ROWS).astype(BF)
-
-
-def azimuth(operands, margin):
-    depth, rows, parts, columns = operands[0].shape
-    steps = (rows - 2 * margin) // TILE
+                z_ref[call, s, half] = dot(window, band[...], OVER_ROWS).astype(BF)
+
+
+def azimuth(operands, margin, calls, matrices):
+    depth, _, parts, columns = operands[0].shape
     lanes = parts * TILE // 2
     shapes = [
-        (depth, steps, 2, columns, lanes),
-        (depth, steps, 2, parts * (TILE // 2 + 2 * margin), lanes),
-        (depth, columns + 2 * margin, columns),
+        (len(calls), 2, 2, columns, lanes),
+        (len(calls), 2, 2, parts * (TILE // 2 + 2 * margin), lanes),
     ]
+    if matrices:
+        shapes.append((depth, columns + 2 * margin, columns))
     return pl.pallas_call(
-        partial(azimuth_kernel, margin),
+        partial(azimuth_kernel, margin, calls),
         in_specs=[VMEM] * len(operands),
         out_specs=[VMEM] * len(shapes),
         out_shape=[pltpu.VMEM(shape, BF) for shape in shapes],
@@ -196,10 +200,10 @@
 def range_kernel(calls, z_ref, band_ref, rg_ref, first_ref, second_ref, *outs):
     odd_column = lax.axis_index("range") & 1 == 1
     half_rows = z_ref.shape[4] // 2
-    for out, (k, chunk) in zip(outs, calls):
+    for call, (out, (k, chunk)) in enumerate(zip(outs, calls)):
         for s in range(2):
             for half in range(2):
-                at = (k, 2 * chunk + s, half)
+                at = (call, s, half)
                 begin = 2 * (2 * (2 * chunk + s) + half) * half_rows
                 across = slice(begin, begin + band_ref.shape[3])
                 first_side, second_side = first_ref[k, :, across], second_ref[k, :, across]
@@ -500,21 +504,23 @@
         got = swapped(held, "scene", bit)
         held = choose(owner, held, got, bit, chunks)
     mate = swapped(held, "scene", 0)
-    turned = azimuth(operands, first.shape[1])
     first = neighbours(first, "range", 0)
     second = neighbours(second, "range", 1)
     last = depth - 1
     early, late = [(last, 0), (0, 1)], [(k, n) for n in range(2) for k in range(depth)]
     late = [call for call in late if call not in early]
-    units = dict(zip(early, range_resample(turned, first, second, early)))
+    *turned, matrices = azimuth(operands, first.shape[1], early, True)
+    units = dict(zip(early, range_resample((*turned, matrices), first, second, early)))
     across = pick(units[last, 0], units[0, 1])
     across = neighbours(across, "scene", 1)
-    units.update(zip(late, range_resample(turned, first, second, late)))
+    turned = azimuth(operands, first.shape[1], late, False)
+    units.update(zip(late, range_resample((*turned, matrices), first, second, late)))
     currents = [[units[k, n] for k in range(depth)] for n in range(2)]
     within = []
     for n in range(2):
         within.append(swapped(currents[n][last], "scene", 0))
-    within = within_products(within, currents)
+    for n in range(2):
+        within[n] = within_products([within[n]], [currents[n]])[0]
     across = across_products(across, currents[0][0], currents[1][last])
     returned = neighbours(across, "scene", 1, True)
     results = []

time: 33 us -> 31.9 us (0.967)
  the two profiles are of different devices: /device:TPU:11 before, /device:TPU:1 now
where the time goes in v5:
time: 31.9 us; the launch traced here: 31.3 us
  Pallas kernels  14.7 us (46%)
  starting transfers between devices  10.6 us (33%)
  waiting for transfers between devices  5.14 us (16%)
  between operations  0.77 us (2%)
    ppermute x4, starting transfers between devices, neighbours(): return lax.ppermute(block, axis, pairs + [(j, i) for i, j in pairs])  7.1 us
    ppermute x4, waiting for transfers between devices, neighbours(): return lax.ppermute(block, axis, pairs + [(j, i) for i, j in pairs])  5.06 us
    pallas_call x2, Pallas kernels, azimuth(): pl.pallas_call(partial(azimuth_kernel, margin, calls), in_specs=[VMEM] *...  4.31 us
    ppermute x5, starting transfers between devices, swapped(): lax.ppermute(block, axis, [(i, i ^ 1 << bit) for i in range(lax.axis_size...  3.54 us
    pallas_call x1, Pallas kernels, load(): pl.pallas_call(partial(load_kernel, margin), in_specs=[anywhere] * len(op...  2.78 us
    pallas_call x2, Pallas kernels, range_resample(): pl.pallas_call(partial(range_kernel, calls), in_specs=[VMEM] * len(arrays...  2.78 us
    pallas_call x2, Pallas kernels, reference_products(): pl.pallas_call(partial(reference_kernel, chunk), in_specs=[VMEM] * (2 + d...  2.04 us
    pallas_call x2, Pallas kernels, within_products(): pl.pallas_call(partial(within_kernel, depth), in_specs=[VMEM] * len(array...  1.48 us
  transfers between devices with their start and end apart: 9, of which 3 were waited for; matrix products, arithmetic and copies ran while one was open for 0% of the time, Pallas kernels for 45%

profile of v5, /device:TPU:1, one launch (start us, length us, event | category | flops | bytes accessed | tf_op | source)
XLA Modules:
  0.0 31.3 jit_solution(14027549206089337439)
XLA Ops:
  0.6 0.1 collective-permute-start
  0.7 2.8 %load.1 = (bf16[2,1056,2,256]{3,2,1,0:T(2,128)(2,1)S(1)}, s32[4]{0:T(128)S(4)}, bf16[1,4,256,2,256]{4,3,2,1,0:T(2,128)(2,1)S(1)}, f32[8,64]{1,0:T(8,128)S(1)}, f...) custom-call(bf16[2,1056,2,256]{3,2,1,0:T(2,128)(2,1)} %x_ref.1, ...), custom_call_target="tpu_custom_call" | custom-call | tf_op jit(solution)/shard_map/load/pallas_call | solution.py:107
  3.5 0.1 collective-permute-done.there_ref
  3.6 0.1 choose.2.here_ref
  3.6 2.7 %collective-permute-start.1 = (bf16[2,256,2,256]{3,2,1,0:T(2,128)(2,1)S(1)}, bf16[2,256,2,256]{3,2,1,0:T(2,128)(2,1)S(1)}, u32[]{:S(2)}, u32[]{:S(2)}) collective-permute-start(bf16[2,256,2,256]{3,2,1,0:T(2,128)(2,1)S(1)} %choose.2.here_ref), channel_id=1, source_target_pairs={{0,8},{4,12},{8,0},{12,4},{1,9},{5,13},{9,1},{13,5},{2,10},{6,14},... | collective-permute-start | bytes 1572872 | tf_op jit(solution)/shard_map/ppermute | solution.py:471
  6.4 1.3 %collective-permute-start.3 = (bf16[2,16,2112]{2,1,0:T(8,128)(2,1)S(1)}, bf16[2,16,2112]{2,1,0:T(8,128)(2,1)S(1)}, u32[]{:S(2)}, u32[]{:S(2)}) collective-permute-start(bf16[2,16,2112]{2,1,0:T(8,128)(2,1)S(1)} %get-tuple-element.48), channel_id=1, source_target_pairs={{0,1},{2,3},{1,0},{3,2},{4,5},{6,7},{5,4},{7,6},{8,9},{10,11},{9,8... | collective-permute-start | bytes 405512 | tf_op jit(solution)/shard_map/ppermute | solution.py:477
  7.7 0.7 %collective-permute-start.4 = (bf16[2,16,2112]{2,1,0:T(8,128)(2,1)S(1)}, bf16[2,16,2112]{2,1,0:T(8,128)(2,1)S(1)}, u32[]{:S(2)}, u32[]{:S(2)}) collective-permute-start(bf16[2,16,2112]{2,1,0:T(8,128)(2,1)S(1)} %get-tuple-element.49), channel_id=1, source_target_pairs={{1,2},{2,1},{5,6},{6,5},{9,10},{10,9},{13,14},{14,13},{17,18},{18,... | collective-permute-start | bytes 405512 | tf_op jit(solution)/shard_map/ppermute | solution.py:477
  8.4 2.2 %azimuth.3 = (bf16[2,2,2,256,256]{4,3,2,1,0:T(8,128)(2,1)S(1)}, bf16[2,2,2,320,256]{4,3,2,1,0:T(8,128)(2,1)S(1)}, bf16[2,288,256]{2,1,0:T(8,128)(2,1)S(1)}) custom-call(bf16[2,1056,2,256]{3,2,1,0:T(2,128)(2,1)S(1)} %get-tuple-element.38.x_ref, f32[8,64]{1,0:T(8,128)S(1)} %get-tuple-element.39.azk_ref, f32[8,64]{1,0:T(8,128)S(1)} %get-tuple-element.40.rgk_ref, ...), custom_call_target="tpu_custom_call" | custom-call | tf_op jit(solution)/shard_map/azimuth/pallas_call | solution.py:189
  10.6 0.7 %collective-permute-done.3.first_ref = bf16[2,16,2112]{2,1,0:T(8,128)(2,1)S(1)} collective-permute-done((bf16[2,16,2112]{2,1,0:T(8,128)(2,1)S(1)}, bf16[2,16,2112]{2,1,0:T(8,128)(2,1)S(1)}, u32[]{:S(2)}, u32[]{:S(2)}) %collective-permute-start.3) | collective-permute-done | bytes 135200 | tf_op jit(solution)/shard_map/ppermute | solution.py:477
  11.3 0.0 collective-permute-done.4.second_ref
  11.3 1.4 %range_resample.3 = (bf16[2,2,256,256]{3,2,1,0:T(8,128)(2,1)S(1)}, bf16[2,2,256,256]{3,2,1,0:T(8,128)(2,1)S(1)}) custom-call(bf16[2,2,2,256,256]{4,3,2,1,0:T(8,128)(2,1)S(1)} %get-tuple-element.51.z_ref, bf16[2,2,2,320,256]{4,3,2,1,0:T(8,128)(2,1)S(1)} %get-tuple-element.52.band_ref, bf16[2,288,256]{2,1,0:T(8,128)(2,1)S(1)} %get-tuple-element.47.rg_ref, ...), custom_call_target="tpu_custom_call" | custom-call | tf_op jit(solution)/shard_map/range_resample/pallas_call | solution.py:224
  12.7 0.1 pick.1
  12.8 3.1 %collective-permute-start.5 = (bf16[2,2,256,256]{3,2,1,0:T(8,128)(2,1)S(1)}, bf16[2,2,256,256]{3,2,1,0:T(8,128)(2,1)S(1)}, u32[]{:S(2)}, u32[]{:S(2)}) collective-permute-start(bf16[2,2,256,256]{3,2,1,0:T(8,128)(2,1)S(1)} %pick.1), channel_id=1, source_target_pairs={{4,8},{8,4},{5,9},{9,5},{6,10},{10,6},{7,11},{11,7},{20,24},{24,20... | collective-permute-start | bytes 1572872 | tf_op jit(solution)/shard_map/ppermute | solution.py:477
  15.8 2.1 %azimuth.2 = (bf16[2,2,2,256,256]{4,3,2,1,0:T(8,128)(2,1)S(1)}, bf16[2,2,2,320,256]{4,3,2,1,0:T(8,128)(2,1)S(1)}) custom-call(bf16[2,1056,2,256]{3,2,1,0:T(2,128)(2,1)S(1)} %get-tuple-element.38.x_ref, f32[8,64]{1,0:T(8,128)S(1)} %get-tuple-element.39.azk_ref, f32[8,64]{1,0:T(8,128)S(1)} %get-tuple-element.40.rgk_ref, ...), custom_call_target="tpu_custom_call" | custom-call | tf_op jit(solution)/shard_map/azimuth/pallas_call | solution.py:189
  17.9 1.4 %range_resample.2 = (bf16[2,2,256,256]{3,2,1,0:T(8,128)(2,1)S(1)}, bf16[2,2,256,256]{3,2,1,0:T(8,128)(2,1)S(1)}) custom-call(bf16[2,2,2,256,256]{4,3,2,1,0:T(8,128)(2,1)S(1)} %get-tuple-element.45.z_ref, bf16[2,2,2,320,256]{4,3,2,1,0:T(8,128)(2,1)S(1)} %get-tuple-element.46.band_ref, bf16[2,288,256]{2,1,0:T(8,128)(2,1)S(1)} %get-tuple-element.47.rg_ref, ...), custom_call_target="tpu_custom_call" | custom-call | tf_op jit(solution)/shard_map/range_resample/pallas_call | solution.py:224
  19.3 0.1 collective-permute-start.8
  19.4 0.5 %collective-permute-start.6 = (bf16[2,2,256,256]{3,2,1,0:T(8,128)(2,1)S(1)}, bf16[2,2,256,256]{3,2,1,0:T(8,128)(2,1)S(1)}, u32[]{:S(2)}, u32[]{:S(2)}) collective-permute-start(bf16[2,2,256,256]{3,2,1,0:T(8,128)(2,1)S(1)} %get-tuple-element.53.refs_1_.odd_ref.refs_2_), channel_id=1, source_target_pairs={{0,4},{4,0},{8,12},{12,8},{1,5},{5,1},{9,13},{13,9},{2,6},{6,2},{1... | collective-permute-start | bytes 1572872 | tf_op jit(solution)/shard_map/ppermute | solution.py:471
  19.9 0.0 collective-permute-done.1.there_ref
  19.9 0.1 choose.3.own_ref
  20.0 0.1 collective-permute-start.2
  20.1 4.4 %collective-permute-done.5.got_ref = bf16[2,2,256,256]{3,2,1,0:T(8,128)(2,1)S(1)} collective-permute-done((bf16[2,2,256,256]{3,2,1,0:T(8,128)(2,1)S(1)}, bf16[2,2,256,256]{3,2,1,0:T(8,128)(2,1)S(1)}, u32[]{:S(2)}, u32[]{:S(2)}) %collective-permute-start.5) | collective-permute-done | bytes 524320 | tf_op jit(solution)/shard_map/ppermute | solution.py:477
  24.5 0.5 %across_products.1.refs_2_ = f32[3,16,128]{2,1,0:T(8,128)S(1)} custom-call(bf16[2,2,256,256]{3,2,1,0:T(8,128)(2,1)S(1)} %collective-permute-done.5.got_ref, bf16[2,2,256,256]{3,2,1,0:T(8,128)(2,1)S(1)} %get-tuple-element.50.refs_0_.first_ref.refs_1_, bf16[2,2,256,256]{3,2,1,0:T(8,128)(2,1)S(1)} %get-tuple-element.57.last_ref.refs_1_.refs_2_), custom_call_target="tpu_custom_call" | custom-call | tf_op jit(solution)/shard_map/across_products/pallas_call | solution.py:403
  24.9 2.1 %collective-permute-start.7 = (f32[3,16,128]{2,1,0:T(8,128)S(1)}, f32[3,16,128]{2,1,0:T(8,128)S(1)}, u32[]{:S(2)}, u32[]{:S(2)}) collective-permute-start(f32[3,16,128]{2,1,0:T(8,128)S(1)} %across_products.1.refs_2_), channel_id=1, source_target_pairs={{4,8},{12,0},{8,4},{0,12},{5,9},{13,1},{9,5},{1,13},{6,10},{14,2},... | collective-permute-start | bytes 73736 | tf_op jit(solution)/shard_map/ppermute | solution.py:477
  27.0 0.0 collective-permute-done.8.refs_0_
  27.0 0.7 %within_products.3 = (f32[3,16,128]{2,1,0:T(8,128)S(1)}, f32[1,2,16,128]{3,2,1,0:T(8,128)S(1)}, f32[2,16,128]{2,1,0:T(8,128)S(1)}) custom-call(bf16[2,2,256,256]{3,2,1,0:T(8,128)(2,1)S(1)} %collective-permute-done.8.refs_0_, bf16[2,2,256,256]{3,2,1,0:T(8,128)(2,1)S(1)} %get-tuple-element.56.even_ref.refs_0_.refs_1_, ...), custom_call_target="tpu_custom_call" | custom-call | tf_op jit(solution)/shard_map/within_products/pallas_call | solution.py:377
  27.8 0.0 collective-permute-done.6.refs_0_
  27.8 0.7 %within_products.2 = (f32[3,16,128]{2,1,0:T(8,128)S(1)}, f32[1,2,16,128]{3,2,1,0:T(8,128)S(1)}, f32[2,16,128]{2,1,0:T(8,128)S(1)}) custom-call(bf16[2,2,256,256]{3,2,1,0:T(8,128)(2,1)S(1)} %collective-permute-done.6.refs_0_, bf16[2,2,256,256]{3,2,1,0:T(8,128)(2,1)S(1)} %get-tuple-element.50.refs_0_.first_ref.refs_1_, ...), custom_call_target="tpu_custom_call" | custom-call | tf_op jit(solution)/shard_map/within_products/pallas_call | solution.py:377
  28.5 0.0 collective-permute-done.2.mate_ref
  28.5 1.0 %reference_products.3 = (f32[2,2,16,128]{3,2,1,0:T(8,128)S(1)}, f32[16,128]{1,0:T(8,128)S(1)}) custom-call(bf16[2,256,2,256]{3,2,1,0:T(2,128)(2,1)S(1)} %choose.3.own_ref, bf16[2,256,2,256]{3,2,1,0:T(2,128)(2,1)S(1)} %collective-permute-done.2.mate_ref, bf16[2,2,256,256]{3,2,1,0:T(8,128)(2,1)S(1)} %get-tuple-element.56.even_ref.refs_0_.refs_1_, ...), custom_call_target="tpu_custom_call" | custom-call | tf_op jit(solution)/shard_map/reference_products/pallas_call | solution.py:336
  29.6 1.0 %reference_products.2 = (f32[2,2,16,128]{3,2,1,0:T(8,128)S(1)}, f32[16,128]{1,0:T(8,128)S(1)}) custom-call(bf16[2,256,2,256]{3,2,1,0:T(2,128)(2,1)S(1)} %choose.3.own_ref, bf16[2,256,2,256]{3,2,1,0:T(2,128)(2,1)S(1)} %collective-permute-done.2.mate_ref, bf16[2,2,256,256]{3,2,1,0:T(8,128)(2,1)S(1)} %get-tuple-element.50.refs_0_.first_ref.refs_1_, ...), custom_call_target="tpu_custom_call" | custom-call | tf_op jit(solution)/shard_map/reference_products/pallas_call | solution.py:336
  30.6 0.0 collective-permute-done.7.refs_8_
  30.6 0.7 %finish.1 = (f32[2,2,16,256]{3,2,1,0:T(8,128)}, f32[2,2,16,256]{3,2,1,0:T(8,128)}, f32[2,16,256]{2,1,0:T(8,128)}) custom-call(f32[2,2,16,128]{3,2,1,0:T(8,128)S(1)} %get-tuple-element.54.refs_0_, f32[16,128]{1,0:T(8,128)S(1)} %get-tuple-element.55.refs_1_, f32[3,16,128]{2,1,0:T(8,128)S(1)} %across_products.1.refs_2_, ...), custom_call_target="tpu_custom_call" | custom-call | tf_op jit(solution)/shard_map/finish/pallas_call | solution.py:459
Async XLA Ops:
  0.6 2.9 %collective-permute-start = (bf16[1,4,256,2,256]{4,3,2,1,0:T(2,128)(2,1)}, bf16[1,4,256,2,256]{4,3,2,1,0:T(2,128)(2,1)S(1)}, u32[]{:S(2)}, u32[]{:S(2)}) collective-permute-start(bf16[1,4,256,2,256]{4,3,2,1,0:T(2,128)(2,1)} %refs_1_.1), channel_id=1, source_target_pairs={{0,4},{4,0},{8,12},{12,8},{1,5},{5,1},{9,13},{13,9},{2,6},{6,2},{1... | collective-permute-start | bytes 3145736 | tf_op jit(solution)/shard_map/ppermute | solution.py:471
  3.6 16.2 %collective-permute-start.1 = (bf16[2,256,2,256]{3,2,1,0:T(2,128)(2,1)S(1)}, bf16[2,256,2,256]{3,2,1,0:T(2,128)(2,1)S(1)}, u32[]{:S(2)}, u32[]{:S(2)}) collective-permute-start(bf16[2,256,2,256]{3,2,1,0:T(2,128)(2,1)S(1)} %choose.2.here_ref), channel_id=1, source_target_pairs={{0,8},{4,12},{8,0},{12,4},{1,9},{5,13},{9,1},{13,5},{2,10},{6,14},... | collective-permute-start | bytes 1572872 | tf_op jit(solution)/shard_map/ppermute | solution.py:471
  6.4 4.9 %collective-permute-start.3 = (bf16[2,16,2112]{2,1,0:T(8,128)(2,1)S(1)}, bf16[2,16,2112]{2,1,0:T(8,128)(2,1)S(1)}, u32[]{:S(2)}, u32[]{:S(2)}) collective-permute-start(bf16[2,16,2112]{2,1,0:T(8,128)(2,1)S(1)} %get-tuple-element.48), channel_id=1, source_target_pairs={{0,1},{2,3},{1,0},{3,2},{4,5},{6,7},{5,4},{7,6},{8,9},{10,11},{9,8... | collective-permute-start | bytes 405512 | tf_op jit(solution)/shard_map/ppermute | solution.py:477
  7.7 3.6 %collective-permute-start.4 = (bf16[2,16,2112]{2,1,0:T(8,128)(2,1)S(1)}, bf16[2,16,2112]{2,1,0:T(8,128)(2,1)S(1)}, u32[]{:S(2)}, u32[]{:S(2)}) collective-permute-start(bf16[2,16,2112]{2,1,0:T(8,128)(2,1)S(1)} %get-tuple-element.49), channel_id=1, source_target_pairs={{1,2},{2,1},{5,6},{6,5},{9,10},{10,9},{13,14},{14,13},{17,18},{18,... | collective-permute-start | bytes 405512 | tf_op jit(solution)/shard_map/ppermute | solution.py:477
  12.8 11.7 %collective-permute-start.5 = (bf16[2,2,256,256]{3,2,1,0:T(8,128)(2,1)S(1)}, bf16[2,2,256,256]{3,2,1,0:T(8,128)(2,1)S(1)}, u32[]{:S(2)}, u32[]{:S(2)}) collective-permute-start(bf16[2,2,256,256]{3,2,1,0:T(8,128)(2,1)S(1)} %pick.1), channel_id=1, source_target_pairs={{4,8},{8,4},{5,9},{9,5},{6,10},{10,6},{7,11},{11,7},{20,24},{24,20... | collective-permute-start | bytes 1572872 | tf_op jit(solution)/shard_map/ppermute | solution.py:477
  19.3 7.7 %collective-permute-start.8 = (bf16[2,2,256,256]{3,2,1,0:T(8,128)(2,1)S(1)}, bf16[2,2,256,256]{3,2,1,0:T(8,128)(2,1)S(1)}, u32[]{:S(2)}, u32[]{:S(2)}) collective-permute-start(bf16[2,2,256,256]{3,2,1,0:T(8,128)(2,1)S(1)} %get-tuple-element.57.last_ref.refs_1_.refs_2_), channel_id=1, source_target_pairs={{0,4},{4,0},{8,12},{12,8},{1,5},{5,1},{9,13},{13,9},{2,6},{6,2},{1... | collective-permute-start | bytes 1572872 | tf_op jit(solution)/shard_map/ppermute | solution.py:471
  19.4 8.4 %collective-permute-start.6 = (bf16[2,2,256,256]{3,2,1,0:T(8,128)(2,1)S(1)}, bf16[2,2,256,256]{3,2,1,0:T(8,128)(2,1)S(1)}, u32[]{:S(2)}, u32[]{:S(2)}) collective-permute-start(bf16[2,2,256,256]{3,2,1,0:T(8,128)(2,1)S(1)} %get-tuple-element.53.refs_1_.odd_ref.refs_2_), channel_id=1, source_target_pairs={{0,4},{4,0},{8,12},{12,8},{1,5},{5,1},{9,13},{13,9},{2,6},{6,2},{1... | collective-permute-start | bytes 1572872 | tf_op jit(solution)/shard_map/ppermute | solution.py:471
  20.0 8.6 %collective-permute-start.2 = (bf16[2,256,2,256]{3,2,1,0:T(2,128)(2,1)S(1)}, bf16[2,256,2,256]{3,2,1,0:T(2,128)(2,1)S(1)}, u32[]{:S(2)}, u32[]{:S(2)}) collective-permute-start(bf16[2,256,2,256]{3,2,1,0:T(2,128)(2,1)S(1)} %choose.3.own_ref), channel_id=1, source_target_pairs={{0,4},{4,0},{8,12},{12,8},{1,5},{5,1},{9,13},{13,9},{2,6},{6,2},{1... | collective-permute-start | bytes 1572872 | tf_op jit(solution)/shard_map/ppermute | solution.py:471
  24.9 5.7 %collective-permute-start.7 = (f32[3,16,128]{2,1,0:T(8,128)S(1)}, f32[3,16,128]{2,1,0:T(8,128)S(1)}, u32[]{:S(2)}, u32[]{:S(2)}) collective-permute-start(f32[3,16,128]{2,1,0:T(8,128)S(1)} %across_products.1.refs_2_), channel_id=1, source_target_pairs={{4,8},{12,0},{8,4},{0,12},{5,9},{13,1},{9,5},{1,13},{6,10},{14,2},... | collective-permute-start | bytes 73736 | tf_op jit(solution)/shard_map/ppermute | solution.py:477

commit v6 on v5

--- a/solution.py
+++ b/solution.py
@@ -67,12 +67,13 @@
     small_refs, x_out, outs = refs[:count], refs[count], refs[count + 1 : 2 * count + 1]
     first_ref, second_ref, sems = refs[2 * count + 1 :]
     depth, rows, parts, columns = x_ref.shape
-    pieces = [(k, n) for k in range(depth) for n in range(rows // TILE)]
+    step = 2 * TILE
+    pieces = [(k, n) for k in range(depth) for n in range(rows // step)]
 
     def copy_of(position):
         k, n = pieces[position]
-        size = TILE if n + 1 < rows // TILE else rows - n * TILE
-        part = (k, pl.ds(n * TILE, size))
+        size = step if n + 1 < rows // step else rows - n * step
+        part = (k, pl.ds(n * step, size))
         return pltpu.make_async_copy(x_ref.at[part], x_out.at[part], sems.at[position]), part, size
 
     copies = [copy_of(position) for position in range(len(pieces))]
@@ -91,7 +92,7 @@
     for (k, n), (copy, part, size) in zip(pieces, copies):
         copy.wait()
         found = dot(edges, x_out[part].reshape(parts * size, columns), OVER_LANES).astype(BF)
-        lanes = slice(parts * n * TILE, parts * (n * TILE + size))
+        lanes = slice(parts * n * step, parts * (n * step + size))
         first_ref[k, :, lanes] = found[:margin]
         second_ref[k, :, lanes] = found[margin:]
     for copy in small:

time: 31.9 us -> 31.7 us (level)
  the two profiles are of different devices: /device:TPU:1 before, /device:TPU:19 now
where the time goes in v6:
time: 31.7 us; the launch traced here: 31.5 us
  Pallas kernels  14.3 us (45%)
  starting transfers between devices  11.7 us (37%)
  waiting for transfers between devices  4.72 us (15%)
  between operations  0.77 us (2%)
    ppermute x4, starting transfers between devices, neighbours(): return lax.ppermute(block, axis, pairs + [(j, i) for i, j in pairs])  8.98 us
    ppermute x4, waiting for transfers between devices, neighbours(): return lax.ppermute(block, axis, pairs + [(j, i) for i, j in pairs])  4.59 us
    pallas_call x2, Pallas kernels, azimuth(): pl.pallas_call(partial(azimuth_kernel, margin, calls), in_specs=[VMEM] *...  4.31 us
    pallas_call x2, Pallas kernels, range_resample(): pl.pallas_call(partial(range_kernel, calls), in_specs=[VMEM] * len(arrays...  2.77 us
    ppermute x5, starting transfers between devices, swapped(): lax.ppermute(block, axis, [(i, i ^ 1 << bit) for i in range(lax.axis_size...  2.75 us
    pallas_call x1, Pallas kernels, load(): pl.pallas_call(partial(load_kernel, margin), in_specs=[anywhere] * len(op...  2.37 us
    pallas_call x2, Pallas kernels, reference_products(): pl.pallas_call(partial(reference_kernel, chunk), in_specs=[VMEM] * (2 + d...  2.04 us
    pallas_call x2, Pallas kernels, within_products(): pl.pallas_call(partial(within_kernel, depth), in_specs=[VMEM] * len(array...  1.48 us
  transfers between devices with their start and end apart: 9, of which 3 were waited for; matrix products, arithmetic and copies ran while one was open for 0% of the time, Pallas kernels for 43%

profile of v6, /device:TPU:19, one launch (start us, length us, event | category | flops | bytes accessed | tf_op | source)
XLA Modules:
  0.0 31.5 jit_solution(17160818604790675679)
XLA Ops:
  0.6 0.7 %collective-permute-start = (bf16[1,4,256,2,256]{4,3,2,1,0:T(2,128)(2,1)}, bf16[1,4,256,2,256]{4,3,2,1,0:T(2,128)(2,1)S(1)}, u32[]{:S(2)}, u32[]{:S(2)}) collective-permute-start(bf16[1,4,256,2,256]{4,3,2,1,0:T(2,128)(2,1)} %refs_1_.1), channel_id=1, source_target_pairs={{0,4},{4,0},{8,12},{12,8},{1,5},{5,1},{9,13},{13,9},{2,6},{6,2},{1... | collective-permute-start | bytes 3145736 | tf_op jit(solution)/shard_map/ppermute | solution.py:472
  1.4 2.4 %load.1 = (bf16[2,1056,2,256]{3,2,1,0:T(2,128)(2,1)S(1)}, s32[4]{0:T(128)S(4)}, bf16[1,4,256,2,256]{4,3,2,1,0:T(2,128)(2,1)S(1)}, f32[8,64]{1,0:T(8,128)S(1)}, f...) custom-call(bf16[2,1056,2,256]{3,2,1,0:T(2,128)(2,1)} %x_ref.1, ...), custom_call_target="tpu_custom_call" | custom-call | tf_op jit(solution)/shard_map/load/pallas_call | solution.py:108
  3.8 0.1 collective-permute-done.there_ref
  3.9 0.1 choose.2.here_ref
  3.9 1.3 %collective-permute-start.1 = (bf16[2,256,2,256]{3,2,1,0:T(2,128)(2,1)S(1)}, bf16[2,256,2,256]{3,2,1,0:T(2,128)(2,1)S(1)}, u32[]{:S(2)}, u32[]{:S(2)}) collective-permute-start(bf16[2,256,2,256]{3,2,1,0:T(2,128)(2,1)S(1)} %choose.2.here_ref), channel_id=1, source_target_pairs={{0,8},{4,12},{8,0},{12,4},{1,9},{5,13},{9,1},{13,5},{2,10},{6,14},... | collective-permute-start | bytes 1572872 | tf_op jit(solution)/shard_map/ppermute | solution.py:472
  5.3 1.3 %collective-permute-start.3 = (bf16[2,16,2112]{2,1,0:T(8,128)(2,1)S(1)}, bf16[2,16,2112]{2,1,0:T(8,128)(2,1)S(1)}, u32[]{:S(2)}, u32[]{:S(2)}) collective-permute-start(bf16[2,16,2112]{2,1,0:T(8,128)(2,1)S(1)} %get-tuple-element.48), channel_id=1, source_target_pairs={{0,1},{2,3},{1,0},{3,2},{4,5},{6,7},{5,4},{7,6},{8,9},{10,11},{9,8... | collective-permute-start | bytes 405512 | tf_op jit(solution)/shard_map/ppermute | solution.py:478
  6.6 1.9 %collective-permute-start.4 = (bf16[2,16,2112]{2,1,0:T(8,128)(2,1)S(1)}, bf16[2,16,2112]{2,1,0:T(8,128)(2,1)S(1)}, u32[]{:S(2)}, u32[]{:S(2)}) collective-permute-start(bf16[2,16,2112]{2,1,0:T(8,128)(2,1)S(1)} %get-tuple-element.49), channel_id=1, source_target_pairs={{1,2},{2,1},{5,6},{6,5},{9,10},{10,9},{13,14},{14,13},{17,18},{18,... | collective-permute-start | bytes 405512 | tf_op jit(solution)/shard_map/ppermute | solution.py:478
  8.5 2.2 %azimuth.3 = (bf16[2,2,2,256,256]{4,3,2,1,0:T(8,128)(2,1)S(1)}, bf16[2,2,2,320,256]{4,3,2,1,0:T(8,128)(2,1)S(1)}, bf16[2,288,256]{2,1,0:T(8,128)(2,1)S(1)}) custom-call(bf16[2,1056,2,256]{3,2,1,0:T(2,128)(2,1)S(1)} %get-tuple-element.38.x_ref, f32[8,64]{1,0:T(8,128)S(1)} %get-tuple-element.39.azk_ref, f32[8,64]{1,0:T(8,128)S(1)} %get-tuple-element.40.rgk_ref, ...), custom_call_target="tpu_custom_call" | custom-call | tf_op jit(solution)/shard_map/azimuth/pallas_call | solution.py:190
  10.7 0.0 collective-permute-done.3.first_ref
  10.7 2.0 %collective-permute-done.4.second_ref = bf16[2,16,2112]{2,1,0:T(8,128)(2,1)S(1)} collective-permute-done((bf16[2,16,2112]{2,1,0:T(8,128)(2,1)S(1)}, bf16[2,16,2112]{2,1,0:T(8,128)(2,1)S(1)}, u32[]{:S(2)}, u32[]{:S(2)}) %collective-permute-start.4) | collective-permute-done | bytes 135200 | tf_op jit(solution)/shard_map/ppermute | solution.py:478
  12.7 1.4 %range_resample.3 = (bf16[2,2,256,256]{3,2,1,0:T(8,128)(2,1)S(1)}, bf16[2,2,256,256]{3,2,1,0:T(8,128)(2,1)S(1)}) custom-call(bf16[2,2,2,256,256]{4,3,2,1,0:T(8,128)(2,1)S(1)} %get-tuple-element.51.z_ref, bf16[2,2,2,320,256]{4,3,2,1,0:T(8,128)(2,1)S(1)} %get-tuple-element.52.band_ref, bf16[2,288,256]{2,1,0:T(8,128)(2,1)S(1)} %get-tuple-element.47.rg_ref, ...), custom_call_target="tpu_custom_call" | custom-call | tf_op jit(solution)/shard_map/range_resample/pallas_call | solution.py:225
  14.1 0.1 pick.1
  14.2 3.8 %collective-permute-start.5 = (bf16[2,2,256,256]{3,2,1,0:T(8,128)(2,1)S(1)}, bf16[2,2,256,256]{3,2,1,0:T(8,128)(2,1)S(1)}, u32[]{:S(2)}, u32[]{:S(2)}) collective-permute-start(bf16[2,2,256,256]{3,2,1,0:T(8,128)(2,1)S(1)} %pick.1), channel_id=1, source_target_pairs={{4,8},{8,4},{5,9},{9,5},{6,10},{10,6},{7,11},{11,7},{20,24},{24,20... | collective-permute-start | bytes 1572872 | tf_op jit(solution)/shard_map/ppermute | solution.py:478
  18.0 2.1 %azimuth.2 = (bf16[2,2,2,256,256]{4,3,2,1,0:T(8,128)(2,1)S(1)}, bf16[2,2,2,320,256]{4,3,2,1,0:T(8,128)(2,1)S(1)}) custom-call(bf16[2,1056,2,256]{3,2,1,0:T(2,128)(2,1)S(1)} %get-tuple-element.38.x_ref, f32[8,64]{1,0:T(8,128)S(1)} %get-tuple-element.39.azk_ref, f32[8,64]{1,0:T(8,128)S(1)} %get-tuple-element.40.rgk_ref, ...), custom_call_target="tpu_custom_call" | custom-call | tf_op jit(solution)/shard_map/azimuth/pallas_call | solution.py:190
  20.1 1.4 %range_resample.2 = (bf16[2,2,256,256]{3,2,1,0:T(8,128)(2,1)S(1)}, bf16[2,2,256,256]{3,2,1,0:T(8,128)(2,1)S(1)}) custom-call(bf16[2,2,2,256,256]{4,3,2,1,0:T(8,128)(2,1)S(1)} %get-tuple-element.45.z_ref, bf16[2,2,2,320,256]{4,3,2,1,0:T(8,128)(2,1)S(1)} %get-tuple-element.46.band_ref, bf16[2,288,256]{2,1,0:T(8,128)(2,1)S(1)} %get-tuple-element.47.rg_ref, ...), custom_call_target="tpu_custom_call" | custom-call | tf_op jit(solution)/shard_map/range_resample/pallas_call | solution.py:225
  21.5 0.1 collective-permute-start.8
  21.6 0.5 %collective-permute-start.6 = (bf16[2,2,256,256]{3,2,1,0:T(8,128)(2,1)S(1)}, bf16[2,2,256,256]{3,2,1,0:T(8,128)(2,1)S(1)}, u32[]{:S(2)}, u32[]{:S(2)}) collective-permute-start(bf16[2,2,256,256]{3,2,1,0:T(8,128)(2,1)S(1)} %get-tuple-element.53.refs_1_.odd_ref.refs_2_), channel_id=1, source_target_pairs={{0,4},{4,0},{8,12},{12,8},{1,5},{5,1},{9,13},{13,9},{2,6},{6,2},{1... | collective-permute-start | bytes 1572872 | tf_op jit(solution)/shard_map/ppermute | solution.py:472
  22.1 0.0 collective-permute-done.1.there_ref
  22.1 0.1 choose.3.own_ref
  22.1 0.1 collective-permute-start.2
  22.3 2.6 %collective-permute-done.5.got_ref = bf16[2,2,256,256]{3,2,1,0:T(8,128)(2,1)S(1)} collective-permute-done((bf16[2,2,256,256]{3,2,1,0:T(8,128)(2,1)S(1)}, bf16[2,2,256,256]{3,2,1,0:T(8,128)(2,1)S(1)}, u32[]{:S(2)}, u32[]{:S(2)}) %collective-permute-start.5) | collective-permute-done | bytes 524320 | tf_op jit(solution)/shard_map/ppermute | solution.py:478
  24.9 0.5 %across_products.1.refs_2_ = f32[3,16,128]{2,1,0:T(8,128)S(1)} custom-call(bf16[2,2,256,256]{3,2,1,0:T(8,128)(2,1)S(1)} %collective-permute-done.5.got_ref, bf16[2,2,256,256]{3,2,1,0:T(8,128)(2,1)S(1)} %get-tuple-element.50.refs_0_.first_ref.refs_1_, bf16[2,2,256,256]{3,2,1,0:T(8,128)(2,1)S(1)} %get-tuple-element.57.last_ref.refs_1_.refs_2_), custom_call_target="tpu_custom_call" | custom-call | tf_op jit(solution)/shard_map/across_products/pallas_call | solution.py:404
  25.3 2.0 %collective-permute-start.7 = (f32[3,16,128]{2,1,0:T(8,128)S(1)}, f32[3,16,128]{2,1,0:T(8,128)S(1)}, u32[]{:S(2)}, u32[]{:S(2)}) collective-permute-start(f32[3,16,128]{2,1,0:T(8,128)S(1)} %across_products.1.refs_2_), channel_id=1, source_target_pairs={{4,8},{12,0},{8,4},{0,12},{5,9},{13,1},{9,5},{1,13},{6,10},{14,2},... | collective-permute-start | bytes 73736 | tf_op jit(solution)/shard_map/ppermute | solution.py:478
  27.3 0.0 collective-permute-done.8.refs_0_
  27.3 0.7 %within_products.3 = (f32[3,16,128]{2,1,0:T(8,128)S(1)}, f32[1,2,16,128]{3,2,1,0:T(8,128)S(1)}, f32[2,16,128]{2,1,0:T(8,128)S(1)}) custom-call(bf16[2,2,256,256]{3,2,1,0:T(8,128)(2,1)S(1)} %collective-permute-done.8.refs_0_, bf16[2,2,256,256]{3,2,1,0:T(8,128)(2,1)S(1)} %get-tuple-element.56.even_ref.refs_0_.refs_1_, ...), custom_call_target="tpu_custom_call" | custom-call | tf_op jit(solution)/shard_map/within_products/pallas_call | solution.py:378
  28.0 0.0 collective-permute-done.6.refs_0_
  28.0 0.7 %within_products.2 = (f32[3,16,128]{2,1,0:T(8,128)S(1)}, f32[1,2,16,128]{3,2,1,0:T(8,128)S(1)}, f32[2,16,128]{2,1,0:T(8,128)S(1)}) custom-call(bf16[2,2,256,256]{3,2,1,0:T(8,128)(2,1)S(1)} %collective-permute-done.6.refs_0_, bf16[2,2,256,256]{3,2,1,0:T(8,128)(2,1)S(1)} %get-tuple-element.50.refs_0_.first_ref.refs_1_, ...), custom_call_target="tpu_custom_call" | custom-call | tf_op jit(solution)/shard_map/within_products/pallas_call | solution.py:378
  28.8 0.0 collective-permute-done.2.mate_ref
  28.8 1.0 %reference_products.3 = (f32[2,2,16,128]{3,2,1,0:T(8,128)S(1)}, f32[16,128]{1,0:T(8,128)S(1)}) custom-call(bf16[2,256,2,256]{3,2,1,0:T(2,128)(2,1)S(1)} %choose.3.own_ref, bf16[2,256,2,256]{3,2,1,0:T(2,128)(2,1)S(1)} %collective-permute-done.2.mate_ref, bf16[2,2,256,256]{3,2,1,0:T(8,128)(2,1)S(1)} %get-tuple-element.56.even_ref.refs_0_.refs_1_, ...), custom_call_target="tpu_custom_call" | custom-call | tf_op jit(solution)/shard_map/reference_products/pallas_call | solution.py:337
  29.8 1.0 %reference_products.2 = (f32[2,2,16,128]{3,2,1,0:T(8,128)S(1)}, f32[16,128]{1,0:T(8,128)S(1)}) custom-call(bf16[2,256,2,256]{3,2,1,0:T(2,128)(2,1)S(1)} %choose.3.own_ref, bf16[2,256,2,256]{3,2,1,0:T(2,128)(2,1)S(1)} %collective-permute-done.2.mate_ref, bf16[2,2,256,256]{3,2,1,0:T(8,128)(2,1)S(1)} %get-tuple-element.50.refs_0_.first_ref.refs_1_, ...), custom_call_target="tpu_custom_call" | custom-call | tf_op jit(solution)/shard_map/reference_products/pallas_call | solution.py:337
  30.8 0.0 collective-permute-done.7.refs_8_
  30.9 0.7 %finish.1 = (f32[2,2,16,256]{3,2,1,0:T(8,128)}, f32[2,2,16,256]{3,2,1,0:T(8,128)}, f32[2,16,256]{2,1,0:T(8,128)}) custom-call(f32[2,2,16,128]{3,2,1,0:T(8,128)S(1)} %get-tuple-element.54.refs_0_, f32[16,128]{1,0:T(8,128)S(1)} %get-tuple-element.55.refs_1_, f32[3,16,128]{2,1,0:T(8,128)S(1)} %across_products.1.refs_2_, ...), custom_call_target="tpu_custom_call" | custom-call | tf_op jit(solution)/shard_map/finish/pallas_call | solution.py:460
Async XLA Ops:
  0.6 3.2 %collective-permute-start = (bf16[1,4,256,2,256]{4,3,2,1,0:T(2,128)(2,1)}, bf16[1,4,256,2,256]{4,3,2,1,0:T(2,128)(2,1)S(1)}, u32[]{:S(2)}, u32[]{:S(2)}) collective-permute-start(bf16[1,4,256,2,256]{4,3,2,1,0:T(2,128)(2,1)} %refs_1_.1), channel_id=1, source_target_pairs={{0,4},{4,0},{8,12},{12,8},{1,5},{5,1},{9,13},{13,9},{2,6},{6,2},{1... | collective-permute-start | bytes 3145736 | tf_op jit(solution)/shard_map/ppermute | solution.py:472
  3.9 18.1 %collective-permute-start.1 = (bf16[2,256,2,256]{3,2,1,0:T(2,128)(2,1)S(1)}, bf16[2,256,2,256]{3,2,1,0:T(2,128)(2,1)S(1)}, u32[]{:S(2)}, u32[]{:S(2)}) collective-permute-start(bf16[2,256,2,256]{3,2,1,0:T(2,128)(2,1)S(1)} %choose.2.here_ref), channel_id=1, source_target_pairs={{0,8},{4,12},{8,0},{12,4},{1,9},{5,13},{9,1},{13,5},{2,10},{6,14},... | collective-permute-start | bytes 1572872 | tf_op jit(solution)/shard_map/ppermute | solution.py:472
  5.3 5.5 %collective-permute-start.3 = (bf16[2,16,2112]{2,1,0:T(8,128)(2,1)S(1)}, bf16[2,16,2112]{2,1,0:T(8,128)(2,1)S(1)}, u32[]{:S(2)}, u32[]{:S(2)}) collective-permute-start(bf16[2,16,2112]{2,1,0:T(8,128)(2,1)S(1)} %get-tuple-element.48), channel_id=1, source_target_pairs={{0,1},{2,3},{1,0},{3,2},{4,5},{6,7},{5,4},{7,6},{8,9},{10,11},{9,8... | collective-permute-start | bytes 405512 | tf_op jit(solution)/shard_map/ppermute | solution.py:478
  6.6 6.2 %collective-permute-start.4 = (bf16[2,16,2112]{2,1,0:T(8,128)(2,1)S(1)}, bf16[2,16,2112]{2,1,0:T(8,128)(2,1)S(1)}, u32[]{:S(2)}, u32[]{:S(2)}) collective-permute-start(bf16[2,16,2112]{2,1,0:T(8,128)(2,1)S(1)} %get-tuple-element.49), channel_id=1, source_target_pairs={{1,2},{2,1},{5,6},{6,5},{9,10},{10,9},{13,14},{14,13},{17,18},{18,... | collective-permute-start | bytes 405512 | tf_op jit(solution)/shard_map/ppermute | solution.py:478
  14.2 10.7 %collective-permute-start.5 = (bf16[2,2,256,256]{3,2,1,0:T(8,128)(2,1)S(1)}, bf16[2,2,256,256]{3,2,1,0:T(8,128)(2,1)S(1)}, u32[]{:S(2)}, u32[]{:S(2)}) collective-permute-start(bf16[2,2,256,256]{3,2,1,0:T(8,128)(2,1)S(1)} %pick.1), channel_id=1, source_target_pairs={{4,8},{8,4},{5,9},{9,5},{6,10},{10,6},{7,11},{11,7},{20,24},{24,20... | collective-permute-start | bytes 1572872 | tf_op jit(solution)/shard_map/ppermute | solution.py:478
  21.5 5.8 %collective-permute-start.8 = (bf16[2,2,256,256]{3,2,1,0:T(8,128)(2,1)S(1)}, bf16[2,2,256,256]{3,2,1,0:T(8,128)(2,1)S(1)}, u32[]{:S(2)}, u32[]{:S(2)}) collective-permute-start(bf16[2,2,256,256]{3,2,1,0:T(8,128)(2,1)S(1)} %get-tuple-element.57.last_ref.refs_1_.refs_2_), channel_id=1, source_target_pairs={{0,4},{4,0},{8,12},{12,8},{1,5},{5,1},{9,13},{13,9},{2,6},{6,2},{1... | collective-permute-start | bytes 1572872 | tf_op jit(solution)/shard_map/ppermute | solution.py:472
  21.6 6.5 %collective-permute-start.6 = (bf16[2,2,256,256]{3,2,1,0:T(8,128)(2,1)S(1)}, bf16[2,2,256,256]{3,2,1,0:T(8,128)(2,1)S(1)}, u32[]{:S(2)}, u32[]{:S(2)}) collective-permute-start(bf16[2,2,256,256]{3,2,1,0:T(8,128)(2,1)S(1)} %get-tuple-element.53.refs_1_.odd_ref.refs_2_), channel_id=1, source_target_pairs={{0,4},{4,0},{8,12},{12,8},{1,5},{5,1},{9,13},{13,9},{2,6},{6,2},{1... | collective-permute-start | bytes 1572872 | tf_op jit(solution)/shard_map/ppermute | solution.py:472
  22.1 6.6 %collective-permute-start.2 = (bf16[2,256,2,256]{3,2,1,0:T(2,128)(2,1)S(1)}, bf16[2,256,2,256]{3,2,1,0:T(2,128)(2,1)S(1)}, u32[]{:S(2)}, u32[]{:S(2)}) collective-permute-start(bf16[2,256,2,256]{3,2,1,0:T(2,128)(2,1)S(1)} %choose.3.own_ref), channel_id=1, source_target_pairs={{0,4},{4,0},{8,12},{12,8},{1,5},{5,1},{9,13},{13,9},{2,6},{6,2},{1... | collective-permute-start | bytes 1572872 | tf_op jit(solution)/shard_map/ppermute | solution.py:472
  25.3 5.5 %collective-permute-start.7 = (f32[3,16,128]{2,1,0:T(8,128)S(1)}, f32[3,16,128]{2,1,0:T(8,128)S(1)}, u32[]{:S(2)}, u32[]{:S(2)}) collective-permute-start(f32[3,16,128]{2,1,0:T(8,128)S(1)} %across_products.1.refs_2_), channel_id=1, source_target_pairs={{4,8},{12,0},{8,4},{0,12},{5,9},{13,1},{9,5},{1,13},{6,10},{14,2},... | collective-permute-start | bytes 73736 | tf_op jit(solution)/shard_map/ppermute | solution.py:478
